TPU v7x, 512 devices: a whole 4x8x8 slice. The times are simulated.
512 devices in a mesh: ha: 8 (over y_lo, core), az: 64 (over x, z, y_hi).
Axes of the slice: x: 4, y: 8 (y_hi: 2, y_lo: 4; y = y_hi * 4 + y_lo), z: 8, core: 2. Of those that a mesh axis runs over, the one named last changes fastest.
Arguments:
- field: float32 [2, 4096, 8192], P(None, 'ha', 'az'), may hold values from -6 to 6
- terrain: int32 [8192], P('az'), may hold values from 0 to 63
- profile_pick: int32 [8192], P('az'), may hold values from 0 to 15
- profile_table: float32 [16, 4096], replicated, may hold values from -3.140625 to 3.140625
- clutter_mask: int32 [128, 8192], P(None, 'az'), may hold values 0 or 1
- pulse: float32 [63], replicated, may hold values from -0.6 to 0.6
- beam: float32 [31], replicated, may hold values from -0.9 to 0.9
- measured: float32 [2, 128, 8192], P(None, None, 'az'), may hold values from -6 to 6
Outputs:
- field_out: float32 [2, 4096, 8192], P(None, 'ha', 'az')
- sources: float32 [2, 2, 128, 8192], P(None, None, 'ha', 'az')
All inputs are finite; a program needn't handle non-finite values. No bound on the sum of `clutter_mask` on one device may be relied on, other than what follows from the above.
Results may differ from a plain program's by a relative error of at most 0.00022.
Values sent between devices are 32-bit elements; how exact they have to be, the bound alone decides.
No kernel may reach another device: no remote copies, remote signals or barrier semaphores. Data moves between devices by JAX's collectives and lax.ppermute only.
A program may use at most 64 MiB of HBM per device.

v0:
```python
import math

import jax
import jax.numpy as jnp
from jax import lax
from jax.sharding import PartitionSpec as P

height_chirp = 1
azimuth_chirp = 3


def broadcast(block, axis, owner):
    block = jnp.where(lax.axis_index(axis) == owner, block, jnp.zeros_like(block))
    return lax.psum(block, axis)


def with_halo(cells, sides, width):
    for axis, dim in sides:
        count = lax.axis_size(axis)
        head = lax.slice_in_dim(cells, 0, width, axis=dim)
        tail = lax.slice_in_dim(cells, cells.shape[dim] - width, cells.shape[dim], axis=dim)
        cells = jnp.concatenate(
            [
                lax.ppermute(tail, axis, [(i, (i + 1) % count) for i in range(count)]),
                cells,
                lax.ppermute(head, axis, [((i + 1) % count, i) for i in range(count)]),
            ],
            axis=dim,
        )
    return cells


def factors(count):
    first = 1
    probe = 1
    while probe * probe <= count:
        if count % probe == 0:
            first = probe
        probe += 1
    return (first, count // first)


def unit_roots(rows, cols, modulus):
    left = lax.broadcasted_iota(jnp.int32, (rows, cols), 0)
    right = lax.broadcasted_iota(jnp.int32, (rows, cols), 1)
    turn = (left * right % modulus).astype(jnp.float32) * (2.0 * math.pi / modulus)
    return (jnp.cos(turn), -jnp.sin(turn))


def chirp_table(first, second, spread, count):
    low = lax.broadcasted_iota(jnp.int32, (first, second), 0)
    high = lax.broadcasted_iota(jnp.int32, (first, second), 1)
    index = low + first * high
    angle = (spread * index * index % (2 * count)).astype(jnp.float32) * (-math.pi / count)
    return (jnp.cos(angle), jnp.sin(angle))


def complex_table(table_re, table_im):
    return jnp.stack([jnp.stack([table_re, -table_im]), jnp.stack([table_im, table_re])])


def cmul(left_re, left_im, right_re, right_im):
    return (left_re * right_re - left_im * right_im, left_re * right_im + left_im * right_re)


def stacked_mul(vals, table_re, table_im):
    new_re, new_im = cmul(vals[0], vals[1], table_re, table_im)
    return jnp.stack([new_re, new_im])


def propagate(part_re, part_im, spread):
    highest = lax.Precision.HIGHEST
    count = part_re.shape[1]
    first, second = factors(count)
    split = (part_re.shape[0], first, second)
    table_shape = (1, first, second)
    outer_re, outer_im = unit_roots(first, first, first)
    inner_re, inner_im = unit_roots(second, second, second)
    twist_re, twist_im = unit_roots(first, second, count)
    twist_re = twist_re.reshape(table_shape)
    twist_im = twist_im.reshape(table_shape)
    phase_re, phase_im = chirp_table(first, second, spread, count)
    phase_re = phase_re.reshape(table_shape)
    phase_im = phase_im.reshape(table_shape)
    outer_fwd = complex_table(outer_re, outer_im)
    inner_fwd = complex_table(inner_re, inner_im)
    inner_inv = complex_table(inner_re.T, -inner_im.T)
    outer_inv = complex_table(outer_re.T, -outer_im.T)
    vals = jnp.stack([part_re.reshape(split), part_im.reshape(split)])
    vals = jnp.einsum("ocka,clab->olkb", outer_fwd, vals, precision=highest)
    vals = stacked_mul(vals, twist_re, twist_im)
    vals = jnp.einsum("clkb,ocbq->olkq", vals, inner_fwd, precision=highest)
    vals = stacked_mul(vals, phase_re, phase_im)
    vals = jnp.einsum("clkq,ocqb->olkb", vals, inner_inv, precision=highest)
    vals = stacked_mul(vals, twist_re, -twist_im)
    vals = jnp.einsum("ocak,clkb->olab", outer_inv, vals, precision=highest)
    scale = 1.0 / count
    return ((vals[0] * scale).reshape(part_re.shape), (vals[1] * scale).reshape(part_im.shape))


def screen_coef(rows, terr, phase, total):
    height = rows.astype(jnp.float32)
    depth = jnp.maximum(height - 0.75 * total, 0.0) / (0.25 * total)
    amount = jnp.exp(-4.0 * depth * depth) * (rows >= terr).astype(jnp.float32)
    return (amount * jnp.cos(phase), amount * jnp.sin(phase))


def onehot_of(picks, count):
    return (picks[None, :] == lax.broadcasted_iota(jnp.int32, (count, picks.shape[0]), 0)).astype(
        jnp.float32
    )


def lookup(table, picks):
    return jnp.einsum(
        "pr,pc->rc", table, onehot_of(picks, table.shape[0]), precision=lax.Precision.HIGHEST
    )


def band(taps, offset):
    hit = offset[:, :, None] == lax.broadcasted_iota(jnp.int32, (1, 1, taps.shape[0]), 2)
    return jnp.sum(jnp.where(hit, taps[None, None, :], 0.0), axis=-1)


def apply_screen(wave, coef):
    new_re, new_im = cmul(wave[0], wave[1], coef[0], coef[1])
    return jnp.stack([new_re, new_im])


def turn_rows(rows):
    new_re, new_im = propagate(rows[0], rows[1], azimuth_chirp)
    return jnp.stack([new_re, new_im])


def turn_items(block):
    return turn_rows(block[:, 0])[:, None]


def to_rows(wave):
    n_az = lax.axis_size("az")
    h_dev = wave.shape[1]
    part_rows = h_dev // n_az
    shaped = wave.reshape(2, n_az, part_rows, wave.shape[2])
    moved = turn_items(lax.all_to_all(shaped, "az", split_axis=1, concat_axis=3, tiled=True))
    return moved.reshape(2, part_rows, moved.shape[3])


def rows_to_slab(rows):
    return lax.all_to_all(rows, "az", split_axis=2, concat_axis=1, tiled=True)


def across(wave):
    return rows_to_slab(to_rows(wave))


def to_tall(wave):
    flipped = jnp.swapaxes(wave, 1, 2)
    return lax.all_to_all(flipped, "ha", split_axis=1, concat_axis=2, tiled=True)


def to_slab(tall):
    flipped = lax.all_to_all(tall, "ha", split_axis=2, concat_axis=1, tiled=True)
    return jnp.swapaxes(flipped, 1, 2)


def down(tall):
    new_re, new_im = propagate(tall[0], tall[1], height_chirp)
    return jnp.stack([new_re, new_im])


def root_strip(wave, bottom):
    return broadcast(wave[:, :bottom, :], "ha", 0)


def beam_forward(values, half_beam, forward_band):
    wider = with_halo(values, (("az", 1),), half_beam)
    return jnp.dot(wider, forward_band, precision=lax.Precision.HIGHEST)


def beam_backward(values, half_beam, back_band):
    wider = with_halo(values, (("az", 1),), half_beam)
    return jnp.dot(wider, back_band, precision=lax.Precision.HIGHEST)


def local(field, terrain, profile_pick, profile_table, clutter_mask, pulse, beam, measured):
    highest = lax.Precision.HIGHEST
    n_slabs = lax.axis_size("ha")
    h_dev = field.shape[1]
    a_dev = field.shape[2]
    total_h = h_dev * n_slabs
    slab = lax.axis_index("ha")
    bottom = clutter_mask.shape[0]
    share_rows = bottom // n_slabs
    row_start = slab * share_rows
    mask = clutter_mask.astype(jnp.float32)
    taps_range = pulse.shape[0]
    half_range = (taps_range - 1) // 2
    row_grid = lax.broadcasted_iota(jnp.int32, (bottom, bottom), 0)
    col_grid = lax.broadcasted_iota(jnp.int32, (bottom, bottom), 1)
    rmat = band(pulse, col_grid - row_grid + half_range)
    half_beam = (beam.shape[0] - 1) // 2
    wide = a_dev + 2 * half_beam
    edge = lax.broadcasted_iota(jnp.int32, (wide, a_dev), 0)
    column = lax.broadcasted_iota(jnp.int32, (wide, a_dev), 1)
    forward_band = band(beam, edge - column)
    back_band = band(beam, column - edge + 2 * half_beam)
    slab_rows = slab * h_dev + lax.broadcasted_iota(jnp.int32, (h_dev, 1), 0)
    slab_phase = lookup(
        lax.dynamic_slice_in_dim(profile_table, slab * h_dev, h_dev, 1), profile_pick
    )
    slab_coef = screen_coef(slab_rows, terrain[None, :], slab_phase, total_h)
    steps_count = measured.shape[0]
    wave = field
    result = []
    for step in range(steps_count):
        wave = to_slab(down(to_tall(across(wave))))
        wave = apply_screen(wave, slab_coef)
        strip = root_strip(wave, bottom)
        low_re = strip[0]
        low_im = strip[1]
        power = mask * (low_re * low_re + low_im * low_im)
        target = measured[step]
        ranged = jnp.dot(rmat, power, precision=highest)
        model = beam_forward(ranged, half_beam, forward_band)
        misfit = model - target
        spread_back = beam_backward(misfit, half_beam, back_band)
        back = jnp.einsum("pr,pa->ra", rmat, spread_back, precision=highest)
        whole = jnp.stack([2.0 * mask * low_re * back, 2.0 * mask * low_im * back])
        result.append(lax.dynamic_slice_in_dim(whole, row_start, share_rows, 1))
    return (wave, jnp.stack(result))


def solution(mesh):
    return jax.shard_map(
        local,
        mesh=mesh,
        in_specs=(
            P(None, "ha", "az"),
            P("az"),
            P("az"),
            P(),
            P(None, "az"),
            P(),
            P(),
            P(None, None, "az"),
        ),
        out_specs=(P(None, "ha", "az"), P(None, None, "ha", "az")),
        check_vma=False,
    )
```

profile of v0, /device:TPU:1, one launch (start us, length us, event | category | flops | bytes accessed | tf_op | source)
XLA Modules:
  0.0 511.8 jit_solution(6664515977165057099)
XLA Ops:
  7.2 1.9 copy.267
  9.1 19.6 %all-to-all-start = ((f32[2,64,8,128]{3,2,0,1:T(8,128)}), f32[2,64,8,128]{3,2,0,1:T(8,128)S(1)}, u32[]{:S(2)}, u32[]{:S(2)}) async-start(f32[2,64,8,128]{3,2,0,1:T(8,128)} %copy.267), calls=%async_computation | async-start | bytes 1048576 | tf_op jit(solution)/shard_map/all_to_all | solution.py:144
  30.1 16.3 %all-to-all-done = f32[2,64,8,128]{3,2,0,1:T(8,128)S(1)} async-done(((f32[2,64,8,128]{3,2,0,1:T(8,128)}), f32[2,64,8,128]{3,2,0,1:T(8,128)S(1)}, u32[]{:S(2)}, u32[]{:S(2)}) %all-to-all-start) | async-done | bytes 524320 | tf_op jit(solution)/shard_map/all_to_all | solution.py:144
  46.6 0.6 convolution_bitcast_fusion.15
  48.7 0.6 convolution_bitcast_fusion.12
  49.5 7.7 %copy.272 = f32[2,8,8192]{1,0,2:T(2,128)} copy(f32[2,8,8192]{2,1,0:T(8,128)S(1)} %pad_maximum_fusion.1) | data formatting | bytes 1048576 | tf_op jit(solution)/shard_map/stack | solution.py:132
  57.2 13.0 %reshape.559 = f32[64,1,2048]{2,1,0:T(1,128)S(1)} reshape(f32[8192,2,8]{2,1,0:T(2,128)} %bitcast.382) | data formatting | bytes 1048576
  70.2 28.5 %all_to_all.132 = f32[64,1,2048]{2,1,0:T(1,128)S(1)} all-to-all(f32[64,1,2048]{2,1,0:T(1,128)S(1)} %reshape.559), channel_id=1, replica_groups=mesh['ha'=8,'az'=64] {'az'}, dimensions={0} | all-to-all | bytes 1048576 | tf_op jit(solution)/shard_map/all_to_all | solution.py:149
  99.2 1.9 reduce
  101.1 14.1 %reshape.560 = f32[8192,2,8]{2,1,0:T(2,128)} reshape(f32[64,2048]{1,0:T(8,128)S(1)} %reduce) | data formatting | bytes 1048576
  115.2 9.2 %copy.365 = f32[2,8,64,128]{3,1,2,0:T(8,128)S(1)} copy(f32[2,8,64,128]{1,0,3,2:T(2,128)} %bitcast.383) | data formatting | bytes 1048576 | tf_op jit(solution)/shard_map/all_to_all | solution.py:149
  124.4 1.0 copy.275
  125.4 7.0 %all-to-all-start.2 = ((f32[2,128,512]{2,0,1:T(2,128)}), f32[2,128,512]{2,0,1:T(2,128)S(1)}, u32[]{:S(2)}, u32[]{:S(2)}) async-start(f32[2,128,512]{2,0,1:T(2,128)} %copy.275), calls=%async_computation.2 | async-start | bytes 1048576 | tf_op jit(solution)/shard_map/all_to_all | solution.py:158
  132.9 13.8 %all-to-all-done.2 = f32[2,128,512]{2,0,1:T(2,128)S(1)} async-done(((f32[2,128,512]{2,0,1:T(2,128)}), f32[2,128,512]{2,0,1:T(2,128)S(1)}, u32[]{:S(2)}, u32[]{:S(2)}) %all-to-all-start.2) | async-done | bytes 524320 | tf_op jit(solution)/shard_map/all_to_all | solution.py:158
  147.9 1.0 convolution_bitcast_fusion.7
  149.1 1.1 convolution_bitcast_fusion.6
  150.3 1.1 convolution_bitcast_fusion.5
  151.6 1.0 convolution_bitcast_fusion.4
  153.5 4.4 copy.288
  157.9 7.9 %reshape.561 = f32[8,1,16384]{2,1,0:T(1,128)} reshape(f32[4096,2,16]{2,1,0:T(2,128)} %bitcast.386) | data formatting | bytes 1048576
  165.7 4.8 all-to-all-start.3
  170.6 14.3 %all-to-all-done.3 = f32[8,1,16384]{2,1,0:T(1,128)S(1)} async-done(((f32[8,1,16384]{2,1,0:T(1,128)}), f32[8,1,16384]{2,1,0:T(1,128)S(1)}, u32[]{:S(2)}, u32[]{:S(2)}) %all-to-all-start.3) | async-done | bytes 524320 | tf_op jit(solution)/shard_map/all_to_all | solution.py:162
  184.9 1.9 reduce.1
  186.8 7.6 %reshape.562 = f32[4096,2,16]{2,1,0:T(2,128)} reshape(f32[8,16384]{1,0:T(8,128)S(1)} %reduce.1) | data formatting | bytes 1048576
  194.4 5.1 %copy.371 = f32[2,16,8,512]{3,1,2,0:T(8,128)S(1)} copy(f32[2,16,8,512]{1,0,3,2:T(2,128)} %bitcast.387) | data formatting | bytes 1048576 | tf_op jit(solution)/shard_map/all_to_all | solution.py:162
  199.7 1.3 multiply_subtract_fusion.9
  201.1 24.5 %all_to_all.133 = f32[2,64,8,128]{3,2,0,1:T(8,128)S(1)} all-to-all(f32[2,64,8,128]{3,2,0,1:T(8,128)S(1)} %pad_maximum_fusion.3), channel_id=1, replica_groups=mesh['ha'=8,'az'=64] {'az'}, dimensions={1} | all-to-all | bytes 1048576 | tf_op jit(solution)/shard_map/all_to_all | solution.py:144
  225.9 0.6 convolution_bitcast_fusion.11
  228.0 0.6 convolution_bitcast_fusion.8
  228.8 7.7 %copy.298 = f32[2,8,8192]{1,0,2:T(2,128)} copy(f32[2,8,8192]{2,1,0:T(8,128)S(1)} %pad_maximum_fusion.4) | data formatting | bytes 1048576 | tf_op jit(solution)/shard_map/stack | solution.py:132
  236.5 13.0 %reshape.563 = f32[64,1,2048]{2,1,0:T(1,128)S(1)} reshape(f32[8192,2,8]{2,1,0:T(2,128)} %bitcast.384) | data formatting | bytes 1048576
  249.5 22.8 %all_to_all.134 = f32[64,1,2048]{2,1,0:T(1,128)S(1)} all-to-all(f32[64,1,2048]{2,1,0:T(1,128)S(1)} %reshape.563), channel_id=1, replica_groups=mesh['ha'=8,'az'=64] {'az'}, dimensions={0} | all-to-all | bytes 1048576 | tf_op jit(solution)/shard_map/all_to_all | solution.py:149
  272.3 1.9 reduce.2
  274.2 14.1 %reshape.564 = f32[8192,2,8]{2,1,0:T(2,128)} reshape(f32[64,2048]{1,0:T(8,128)S(1)} %reduce.2) | data formatting | bytes 1048576
  288.3 9.2 %copy.376 = f32[2,8,64,128]{3,1,2,0:T(8,128)S(1)} copy(f32[2,8,64,128]{1,0,3,2:T(2,128)} %bitcast.385) | data formatting | bytes 1048576 | tf_op jit(solution)/shard_map/all_to_all | solution.py:149
  297.7 25.1 %all_to_all.135 = f32[2,128,512]{2,0,1:T(2,128)S(1)} all-to-all(f32[2,128,512]{2,0,1:T(2,128)S(1)} %copy.301), channel_id=1, replica_groups=mesh['ha'=8,'az'=64] {'ha'}, dimensions={1} | all-to-all | bytes 1048576 | tf_op jit(solution)/shard_map/all_to_all | solution.py:158
  323.9 1.0 convolution_bitcast_fusion.3
  325.1 1.1 convolution_bitcast_fusion.2
  326.4 1.1 convolution_bitcast_fusion.1
  327.6 1.0 convolution_bitcast_fusion
  329.6 4.4 copy.314
  333.9 7.9 %reshape.565 = f32[8,1,16384]{2,1,0:T(1,128)} reshape(f32[4096,2,16]{2,1,0:T(2,128)} %bitcast.388) | data formatting | bytes 1048576
  341.8 4.4 all-to-all-start.7
  347.3 0.7 fusion.34
  348.0 12.6 %all-to-all-done.7 = f32[8,1,16384]{2,1,0:T(1,128)S(1)} async-done(((f32[8,1,16384]{2,1,0:T(1,128)}), f32[8,1,16384]{2,1,0:T(1,128)S(1)}, u32[]{:S(2)}, u32[]{:S(2)}) %all-to-all-start.7) | async-done | bytes 524320 | tf_op jit(solution)/shard_map/all_to_all | solution.py:162
  360.6 1.9 reduce.3
  362.5 7.6 %reshape.566 = f32[4096,2,16]{2,1,0:T(2,128)} reshape(f32[8,16384]{1,0:T(8,128)S(1)} %reduce.3) | data formatting | bytes 1048576
  370.1 5.2 %copy.382 = f32[2,16,8,512]{3,1,2,0:T(8,128)S(1)} copy(f32[2,16,8,512]{1,0,3,2:T(2,128)} %bitcast.389) | data formatting | bytes 1048576 | tf_op jit(solution)/shard_map/all_to_all | solution.py:162
  375.5 1.4 subtract_bitcast_fusion
  376.8 0.7 fusion.33
  378.0 0.8 pad_maximum_fusion
  378.8 65.5 %all-reduce.3.cloned.1.call-done = (f32[2,128,128]{2,1,0:T(8,128)}, f32[2,128,128]{2,1,0:T(8,128)}) async-done(((f32[2,128,128]{2,1,0:T(8,128)}, f32[2,128,128]{2,1,0:T(8,128)}), (f32[2,128,128]{2,1,0:T(8,128)}, f32[2,128,128]{2,1,0:T(8,128)})) %all-reduce.3.cloned.1.call-update) | async-done | bytes 262160 | tf_op jit(solution)/shard_map/psum | solution.py:14
  444.3 1.2 fusion.70
  445.5 1.2 fusion.75
  446.7 6.1 %collective-permute-start = (f32[128,15]{0,1:T(8,128)S(1)}, f32[128,15]{0,1:T(8,128)S(1)}, u32[]{:S(2)}, u32[]{:S(2)}) collective-permute-start(f32[128,15]{0,1:T(8,128)S(1)} %get-tuple-element.64), channel_id=1, source_target_pairs={{0,1},{1,2},{2,3},{3,4},{4,5},{5,6},{6,7},{7,8},{8,9},{9,10},{10,1... | collective-permute-start | bytes 23048 | tf_op jit(solution)/shard_map/ppermute | solution.py:24
  452.8 7.4 %collective-permute-start.1 = (f32[128,15]{0,1:T(8,128)S(1)}, f32[128,15]{0,1:T(8,128)S(1)}, u32[]{:S(2)}, u32[]{:S(2)}) collective-permute-start(f32[128,15]{0,1:T(8,128)S(1)} %get-tuple-element.65), channel_id=1, source_target_pairs={{1,0},{2,1},{3,2},{4,3},{5,4},{6,5},{7,6},{8,7},{9,8},{10,9},{11,1... | collective-permute-start | bytes 23048 | tf_op jit(solution)/shard_map/ppermute | solution.py:26
  460.2 1.9 collective-permute-start.4
  462.1 11.5 %collective-permute-start.5 = (f32[128,15]{0,1:T(8,128)S(1)}, f32[128,15]{0,1:T(8,128)S(1)}, u32[]{:S(2)}, u32[]{:S(2)}) collective-permute-start(f32[128,15]{0,1:T(8,128)S(1)} %get-tuple-element.69), channel_id=1, source_target_pairs={{1,0},{2,1},{3,2},{4,3},{5,4},{6,5},{7,6},{8,7},{9,8},{10,9},{11,1... | collective-permute-start | bytes 23048 | tf_op jit(solution)/shard_map/ppermute | solution.py:26
  474.1 1.9 collective-permute-start.2
  476.0 11.5 %collective-permute-start.3 = (f32[128,15]{0,1:T(8,128)S(1)}, f32[128,15]{0,1:T(8,128)S(1)}, u32[]{:S(2)}, u32[]{:S(2)}) collective-permute-start(f32[128,15]{0,1:T(8,128)S(1)} %get-tuple-element.63), channel_id=1, source_target_pairs={{1,0},{2,1},{3,2},{4,3},{5,4},{6,5},{7,6},{8,7},{9,8},{10,9},{11,1... | collective-permute-start | bytes 23048 | tf_op jit(solution)/shard_map/ppermute | solution.py:26
  488.0 1.9 collective-permute-start.6
  489.9 11.5 %collective-permute-start.7 = (f32[128,15]{0,1:T(8,128)S(1)}, f32[128,15]{0,1:T(8,128)S(1)}, u32[]{:S(2)}, u32[]{:S(2)}) collective-permute-start(f32[128,15]{0,1:T(8,128)S(1)} %get-tuple-element.67), channel_id=1, source_target_pairs={{1,0},{2,1},{3,2},{4,3},{5,4},{6,5},{7,6},{8,7},{9,8},{10,9},{11,1... | collective-permute-start | bytes 23048 | tf_op jit(solution)/shard_map/ppermute | solution.py:26
  502.7 1.2 multiply_bitcast_fusion.2
  503.9 0.6 pad_maximum_fusion.16
  (121 shorter events, 15.2 us)
Async XLA Ops:
  7.2 192.6 %copy-start = (f32[16,4096]{1,0:T(8,128)S(1)}, f32[16,4096]{1,0:T(8,128)}, u32[]{:S(2)}) copy-start(f32[16,4096]{1,0:T(8,128)} %param.11) | copy-start | bytes 786436
  9.1 37.3 %all-to-all-start = ((f32[2,64,8,128]{3,2,0,1:T(8,128)}), f32[2,64,8,128]{3,2,0,1:T(8,128)S(1)}, u32[]{:S(2)}, u32[]{:S(2)}) async-start(f32[2,64,8,128]{3,2,0,1:T(8,128)} %copy.267), calls=%async_computation | async-start | bytes 1048576 | tf_op jit(solution)/shard_map/all_to_all | solution.py:144
  125.4 21.4 %all-to-all-start.2 = ((f32[2,128,512]{2,0,1:T(2,128)}), f32[2,128,512]{2,0,1:T(2,128)S(1)}, u32[]{:S(2)}, u32[]{:S(2)}) async-start(f32[2,128,512]{2,0,1:T(2,128)} %copy.275), calls=%async_computation.2 | async-start | bytes 1048576 | tf_op jit(solution)/shard_map/all_to_all | solution.py:158
  165.7 19.2 %all-to-all-start.3 = ((f32[8,1,16384]{2,1,0:T(1,128)}), f32[8,1,16384]{2,1,0:T(1,128)S(1)}, u32[]{:S(2)}, u32[]{:S(2)}) async-start(f32[8,1,16384]{2,1,0:T(1,128)} %reshape.561), calls=%async_computation.3 | async-start | bytes 1048576 | tf_op jit(solution)/shard_map/all_to_all | solution.py:162
  186.8 12.9 %copy-start.4 = (s32[128]{0:T(128)S(1)}, s32[128]{0:T(128)}, u32[]{:S(2)}) copy-start(s32[128]{0:T(128)} %param.9) | copy-start | bytes 1540
  186.8 12.9 %copy-start.5 = (s32[128]{0:T(128)S(1)}, s32[128]{0:T(128)}, u32[]{:S(2)}) copy-start(s32[128]{0:T(128)} %param.10) | copy-start | bytes 1540
  329.5 17.0 %copy-start.3 = (f32[2,128,128]{2,1,0:T(8,128)S(1)}, f32[2,128,128]{2,1,0:T(8,128)}, u32[]{:S(2)}) copy-start(f32[2,128,128]{2,1,0:T(8,128)} %param.15) | copy-start | bytes 393220
  333.9 12.9 %copy-start.6 = (f32[31]{0:T(128)S(1)}, f32[31]{0:T(128)}, u32[]{:S(2)}) copy-start(f32[31]{0:T(128)} %param.14) | copy-start | bytes 376
  341.8 18.8 %all-to-all-start.7 = ((f32[8,1,16384]{2,1,0:T(1,128)}), f32[8,1,16384]{2,1,0:T(1,128)S(1)}, u32[]{:S(2)}, u32[]{:S(2)}) async-start(f32[8,1,16384]{2,1,0:T(1,128)} %reshape.565), calls=%async_computation.7 | async-start | bytes 1048576 | tf_op jit(solution)/shard_map/all_to_all | solution.py:162
  346.2 98.1 %all-reduce.3.cloned.1.call-start = ((), (), s32[]{:S(2)}) async-start(), calls=%async_computation.8 | async-start | bytes 524288 | tf_op jit(solution)/shard_map/psum | solution.py:14
  370.1 7.5 %copy-start.7 = (f32[63]{0:T(128)S(1)}, f32[63]{0:T(128)}, u32[]{:S(2)}) copy-start(f32[63]{0:T(128)} %param.13) | copy-start | bytes 760
  370.1 74.3 %copy-start.2 = (s32[128,128]{1,0:T(8,128)S(1)}, s32[128,128]{1,0:T(8,128)}, u32[]{:S(2)}) copy-start(s32[128,128]{1,0:T(8,128)} %param.12) | copy-start | bytes 196612
  370.1 134.5 %copy-start.1 = (f32[16,4096]{1,0:T(8,128)S(1)}, f32[16,4096]{1,0:T(8,128)}, u32[]{:S(2)}) copy-start(f32[16,4096]{1,0:T(8,128)} %param.11) | copy-start | bytes 786436
  446.7 26.9 %collective-permute-start = (f32[128,15]{0,1:T(8,128)S(1)}, f32[128,15]{0,1:T(8,128)S(1)}, u32[]{:S(2)}, u32[]{:S(2)}) collective-permute-start(f32[128,15]{0,1:T(8,128)S(1)} %get-tuple-element.64), channel_id=1, source_target_pairs={{0,1},{1,2},{2,3},{3,4},{4,5},{5,6},{6,7},{7,8},{8,9},{9,10},{10,1... | collective-permute-start | bytes 23048 | tf_op jit(solution)/shard_map/ppermute | solution.py:24
  452.8 20.9 %collective-permute-start.1 = (f32[128,15]{0,1:T(8,128)S(1)}, f32[128,15]{0,1:T(8,128)S(1)}, u32[]{:S(2)}, u32[]{:S(2)}) collective-permute-start(f32[128,15]{0,1:T(8,128)S(1)} %get-tuple-element.65), channel_id=1, source_target_pairs={{1,0},{2,1},{3,2},{4,3},{5,4},{6,5},{7,6},{8,7},{9,8},{10,9},{11,1... | collective-permute-start | bytes 23048 | tf_op jit(solution)/shard_map/ppermute | solution.py:26
  460.2 27.3 %collective-permute-start.4 = (f32[128,15]{0,1:T(8,128)S(1)}, f32[128,15]{0,1:T(8,128)S(1)}, u32[]{:S(2)}, u32[]{:S(2)}) collective-permute-start(f32[128,15]{0,1:T(8,128)S(1)} %get-tuple-element.68), channel_id=1, source_target_pairs={{0,1},{1,2},{2,3},{3,4},{4,5},{5,6},{6,7},{7,8},{8,9},{9,10},{10,1... | collective-permute-start | bytes 23048 | tf_op jit(solution)/shard_map/ppermute | solution.py:24
  462.1 25.4 %collective-permute-start.5 = (f32[128,15]{0,1:T(8,128)S(1)}, f32[128,15]{0,1:T(8,128)S(1)}, u32[]{:S(2)}, u32[]{:S(2)}) collective-permute-start(f32[128,15]{0,1:T(8,128)S(1)} %get-tuple-element.69), channel_id=1, source_target_pairs={{1,0},{2,1},{3,2},{4,3},{5,4},{6,5},{7,6},{8,7},{9,8},{10,9},{11,1... | collective-permute-start | bytes 23048 | tf_op jit(solution)/shard_map/ppermute | solution.py:26
  474.1 27.3 %collective-permute-start.2 = (f32[128,15]{0,1:T(8,128)S(1)}, f32[128,15]{0,1:T(8,128)S(1)}, u32[]{:S(2)}, u32[]{:S(2)}) collective-permute-start(f32[128,15]{0,1:T(8,128)S(1)} %get-tuple-element.62), channel_id=1, source_target_pairs={{0,1},{1,2},{2,3},{3,4},{4,5},{5,6},{6,7},{7,8},{8,9},{9,10},{10,1... | collective-permute-start | bytes 23048 | tf_op jit(solution)/shard_map/ppermute | solution.py:24
  476.0 25.4 %collective-permute-start.3 = (f32[128,15]{0,1:T(8,128)S(1)}, f32[128,15]{0,1:T(8,128)S(1)}, u32[]{:S(2)}, u32[]{:S(2)}) collective-permute-start(f32[128,15]{0,1:T(8,128)S(1)} %get-tuple-element.63), channel_id=1, source_target_pairs={{1,0},{2,1},{3,2},{4,3},{5,4},{6,5},{7,6},{8,7},{9,8},{10,9},{11,1... | collective-permute-start | bytes 23048 | tf_op jit(solution)/shard_map/ppermute | solution.py:26
  488.0 14.2 %collective-permute-start.6 = (f32[128,15]{0,1:T(8,128)S(1)}, f32[128,15]{0,1:T(8,128)S(1)}, u32[]{:S(2)}, u32[]{:S(2)}) collective-permute-start(f32[128,15]{0,1:T(8,128)S(1)} %get-tuple-element.66), channel_id=1, source_target_pairs={{0,1},{1,2},{2,3},{3,4},{4,5},{5,6},{6,7},{7,8},{8,9},{9,10},{10,1... | collective-permute-start | bytes 23048 | tf_op jit(solution)/shard_map/ppermute | solution.py:24
  489.9 12.3 %collective-permute-start.7 = (f32[128,15]{0,1:T(8,128)S(1)}, f32[128,15]{0,1:T(8,128)S(1)}, u32[]{:S(2)}, u32[]{:S(2)}) collective-permute-start(f32[128,15]{0,1:T(8,128)S(1)} %get-tuple-element.67), channel_id=1, source_target_pairs={{1,0},{2,1},{3,2},{4,3},{5,4},{6,5},{7,6},{8,7},{9,8},{10,9},{11,1... | collective-permute-start | bytes 23048 | tf_op jit(solution)/shard_map/ppermute | solution.py:26
Sparse Core Ops, SparseCore 0:
  377.7 66.6 all-reduce.2
where the time goes:
time: 522 us; the launch traced here: 512 us
  local copies, waits for them, and re-layouts  146 us (28%)
  waiting for transfers between devices  123 us (24%)
  blocking collectives  101 us (19%)
  starting transfers between devices  89.8 us (17%)
  matrix products  20.1 us (4%)
  other arithmetic  16.4 us (3%)
  between operations  15.5 us (3%)
    unnamed x26, local copies, waits for them, and re-layouts  85.3 us
    psum x1, waiting for transfers between devices, broadcast(): return lax.psum(block, axis)  65.5 us
    all_to_all x2, blocking collectives, rows_to_slab(): return lax.all_to_all(rows, 'az', split_axis=2, concat_axis=1, tiled=True)  51.3 us
    ppermute x4, starting transfers between devices, with_halo(): lax.ppermute(head, axis, [((i + 1) % count, i) for i in range(count)])  41.9 us
    all_to_all x2, waiting for transfers between devices, to_slab(): lax.all_to_all(tall, 'ha', split_axis=2, concat_axis=1, tiled=True)  26.9 us
    all_to_all x1, blocking collectives, to_tall(): lax.all_to_all(flipped, 'ha', split_axis=1, concat_axis=2, tiled=True)  25.1 us
    all_to_all x1, blocking collectives, to_rows(): lax.all_to_all(shaped, 'az', split_axis=1, concat_axis=3, tiled=True)  24.5 us
    all_to_all x1, starting transfers between devices, to_rows(): lax.all_to_all(shaped, 'az', split_axis=1, concat_axis=3, tiled=True)  19.6 us
  transfers between devices with their start and end apart: 13, of which 5 were waited for; matrix products, arithmetic and copies ran while one was open for 1% of the time, Pallas kernels for 0%

commit v1 on v0

v1 whole, which is shorter than its diff:
```python
import functools
import math

import jax
import jax.numpy as jnp
import numpy as np
from jax import lax
from jax.experimental import pallas as pl
from jax.experimental.pallas import tpu as pltpu
from jax.sharding import PartitionSpec as P

NH, NA = 4096, 8192
PH, PA = 8, 64
ROWS = PH * PA
LANES = 128
BOT = 128
height_chirp = 1
azimuth_chirp = 3
INV = pow(azimuth_chirp, -1, 2 * NA)
HIGHEST = lax.Precision.HIGHEST


def gauss(count, spread):
    index = np.arange(count, dtype=np.int64)
    return np.sum(np.exp(-1j * np.pi * ((spread * index * index) % (2 * count)) / count)) / count


GAIN = gauss(NH, height_chirp) * gauss(NA, azimuth_chirp)


def row_matrices():
    turn = 2.0 * np.pi * ((INV * np.outer(np.arange(PA), np.arange(PA))) % PA) / PA
    re, im = np.cos(turn), -np.sin(turn)
    split = np.block([[re, -im], [im, re]])
    mixed = split.reshape(2 * PA, 2, PA).transpose(0, 2, 1).reshape(2 * PA, 2 * PA)
    return split.astype(np.float32), mixed.astype(np.float32)


SPLIT_DFT, MIXED_DFT = row_matrices()


def pair_choice():
    table = np.zeros((4, LANES, LANES), np.float32)
    for part in range(4):
        for q in range(2):
            for o in range(8):
                for j in range(2):
                    table[part, 64 * q + 2 * o + j, 16 * o + 2 * (2 * part + q) + j] = 1.0
    return table.reshape(4 * LANES, LANES)


PAIRS = pair_choice()


def dot(left, right):
    return jnp.dot(left, right, precision=HIGHEST, preferred_element_type=jnp.float32)


def lane_of(shape):
    return lax.broadcasted_iota(jnp.int32, shape, len(shape) - 1)


def row_of(shape):
    return lax.broadcasted_iota(jnp.int32, shape, len(shape) - 2)


def dft4(re, im):
    sr, si = re[0] + re[2], im[0] + im[2]
    dr, di = re[0] - re[2], im[0] - im[2]
    tr, ti = re[1] + re[3], im[1] + im[3]
    ur, ui = re[1] - re[3], im[1] - im[3]
    return [sr + tr, dr + ui, sr - tr, dr - ui], [si + ti, di - ur, si - ti, di + ur]


def dft8(re, im):
    half = math.sqrt(0.5)
    er, ei = dft4(re[0::2], im[0::2])
    pr, pi = dft4(re[1::2], im[1::2])
    tr = [pr[0], half * (pr[1] + pi[1]), pi[2], half * (pi[3] - pr[3])]
    ti = [pi[0], half * (pi[1] - pr[1]), -pr[2], -half * (pr[3] + pi[3])]
    out_re = [er[k] + tr[k] for k in range(4)] + [er[k] - tr[k] for k in range(4)]
    out_im = [ei[k] + ti[k] for k in range(4)] + [ei[k] - ti[k] for k in range(4)]
    return out_re, out_im


def dft8_group(held, group):
    low = 8 * group
    re = [held[i * 128 + low : i * 128 + low + 8, :] for i in range(8)]
    im = [held[i * 128 + 64 + low : i * 128 + 64 + low + 8, :] for i in range(8)]
    return dft8(re, im)


def flip_halves(block):
    turned = jnp.concatenate([block, block], axis=0).T
    return jnp.where(lane_of((64, LANES)) < 64, turned[:64], turned[64:])


def pack_kernel(place, field, terrain, pick, mask, turned, out):
    dh, da = place[0], place[1]
    lanes = lane_of((64, LANES))
    rows = row_of((64, LANES))
    pads = [
        terrain[...].astype(jnp.float32),
        pick[...].astype(jnp.float32),
        jnp.zeros((14, LANES), jnp.float32),
        mask[pl.ds(pl.multiple_of(16 * dh, 16), 16), :].astype(jnp.float32),
    ]
    stacked = jnp.concatenate([jnp.zeros((64, LANES), jnp.float32)] + pads + pads, axis=0)
    upright = stacked.T
    common = jnp.where(lanes < 96, upright[:64], upright[64:])
    lane8 = lane_of((8, LANES))
    head = jnp.zeros((8, LANES), jnp.float32)
    tail = jnp.zeros((8, LANES), jnp.float32)
    for s in range(2):
        for j in range(2):
            slot = 2 * s + j
            part = turned.at[s][pl.ds(dh + 8 * j, 8, stride=16), :]
            here = (lane8 >= 16 * slot) & (lane8 < 16 * slot + 16)
            first = part if slot == 0 else pltpu.roll(part, 16 * slot, 1)
            head = jnp.where(here, first, head)
            tail = jnp.where(here, pltpu.roll(part, 16 + 16 * slot, 1), tail)
    right = lax.rem(da + 1, PA)
    left = lax.rem(da + PA - 1, PA)
    for e in range(8):
        spread_tail = jnp.broadcast_to(tail[e : e + 1, :], (64, LANES))
        spread_head = jnp.broadcast_to(head[e : e + 1, :], (64, LANES))
        edge = jnp.where(rows == right, spread_tail, jnp.where(rows == left, spread_head, 0.0))
        for c in range(2):
            out[pl.ds(e * 192 + c, 64, stride=3), :] = flip_halves(
                field.at[c][pl.ds(e, 64, stride=8), :]
            )
        out[pl.ds(e * 192 + 2, 64, stride=3), :] = jnp.where(lanes < 64, edge, common)


def finish_send(held, twist_re, twist_im, lane_dft, out, mid_re, mid_im):
    for group in range(8):
        re, im = dft8_group(held, group)
        for k in range(8):
            at = slice(k * 64 + 8 * group, k * 64 + 8 * group + 8)
            tr, ti = twist_re[at, :], twist_im[at, :]
            mid_re[at, :] = re[k] * tr - im[k] * ti
            mid_im[at, :] = re[k] * ti + im[k] * tr
    from_re = dot(mid_re[...], lane_dft[...])
    from_im = dot(mid_im[...], lane_dft[...])
    out[pl.ds(0, ROWS, stride=2), :] = from_re[:, :LANES] - from_im[:, LANES:]
    out[pl.ds(1, ROWS, stride=2), :] = from_re[:, LANES:] + from_im[:, :LANES]


def first_kernel(got, chirp_re, chirp_im, twist_re, twist_im, lane_dft, split, out, held, mid_re, mid_im):
    for i in range(8):
        xr = got[pl.ds(i * 192, 64, stride=3), :]
        xi = got[pl.ds(i * 192 + 1, 64, stride=3), :]
        at = slice(i * 64, i * 64 + 64)
        dr, di = chirp_re[at, :], chirp_im[at, :]
        both = jnp.concatenate([xr * dr - xi * di, xr * di + xi * dr], axis=0)
        held[i * 128 : (i + 1) * 128, :] = dot(split[...], both)
    finish_send(held, twist_re, twist_im, lane_dft, out, mid_re, mid_im)


def middle_kernel(
    got, coef_re, coef_im, both_re, both_im, twist_re, twist_im, lane_dft, split, mixed,
    out, strip, held, mid_re, mid_im, next_in,
):
    for i in range(8):
        held[i * 128 : (i + 1) * 128, :] = dot(mixed[...], got[i * 128 : (i + 1) * 128, :])
    for group in range(8):
        re, im = dft8_group(held, group)
        low = 8 * group
        cr, ci = coef_re[low : low + 8, :], coef_im[low : low + 8, :]
        strip[0, low : low + 8, :] = re[0] * cr - im[0] * ci
        strip[1, low : low + 8, :] = re[0] * ci + im[0] * cr
        for k in range(8):
            at = slice(k * 64 + low, k * 64 + low + 8)
            cr, ci = both_re[at, :], both_im[at, :]
            next_in[k * 128 + low : k * 128 + low + 8, :] = re[k] * cr - im[k] * ci
            next_in[k * 128 + 64 + low : k * 128 + 64 + low + 8, :] = re[k] * ci + im[k] * cr
    for i in range(8):
        held[i * 128 : (i + 1) * 128, :] = dot(split[...], next_in[i * 128 : (i + 1) * 128, :])
    finish_send(held, twist_re, twist_im, lane_dft, out, mid_re, mid_im)


def last_kernel(place, got, coef_re, coef_im, strip, seen, pairs, mixed, out, held, low_re, low_im):
    f = place[1]
    for i in range(8):
        held[i * 128 : (i + 1) * 128, :] = dot(mixed[...], got[i * 128 : (i + 1) * 128, :])
    for group in range(8):
        re, im = dft8_group(held, group)
        low = 8 * group
        for k in range(8):
            at = slice(k * 64 + low, k * 64 + low + 8)
            cr, ci = coef_re[at, :], coef_im[at, :]
            new_re = re[k] * cr - im[k] * ci
            new_im = re[k] * ci + im[k] * cr
            out[pl.ds(3 * (k * 64 + low), 8, stride=3), :] = new_re
            out[pl.ds(3 * (k * 64 + low) + 1, 8, stride=3), :] = new_im
            if k == 0:
                low_re[low : low + 8, :] = new_re
                low_im[low : low + 8, :] = new_im
    lanes = lane_of((64, LANES))
    parts = [strip[0], strip[1], low_re[...], low_im[...]]
    chosen = dot(parts[0], pairs[0:LANES, :])
    for part in range(1, 4):
        chosen = chosen + dot(parts[part], pairs[part * LANES : (part + 1) * LANES, :])
    powers = jnp.zeros((64, LANES), jnp.float32)
    for s in range(2):
        power = seen[...] * (parts[2 * s] * parts[2 * s] + parts[2 * s + 1] * parts[2 * s + 1])
        base = 48 * s
        after = pltpu.roll(power, PA - 1, 0)
        before = pltpu.roll(power, 1, 0)
        near = power if base == 0 else pltpu.roll(power, base, 1)
        other = pltpu.roll(power, base + 16 + 64, 1)
        side = jnp.where(
            f < 32, pltpu.roll(after, base + 32, 1), pltpu.roll(before, (base + 32 + 64) % LANES, 1)
        )
        for slot, moved in enumerate((near, other, side)):
            at = base + 16 * slot
            powers = jnp.where((lanes >= at) & (lanes < at + 16), moved, powers)
    for o in range(8):
        shift = (96 - 16 * o) % LANES
        moved = chosen if shift == 0 else pltpu.roll(chosen, shift, 1)
        out[pl.ds(o * 192 + 2, 64, stride=3), :] = jnp.where(lanes < 96, powers, moved)


def unpack_kernel(place, got, mask, back_measured, range_pair, beam_pair, field_out, sources, turned):
    eh = place[0]
    for e in range(8):
        for c in range(2):
            field_out.at[c][pl.ds(e, 64, stride=8), :] = flip_halves(
                got[pl.ds(e * 192 + c, 64, stride=3), :]
            )
        aux = got[pl.ds(e * 192 + 2, 64, stride=3), :]
        turned[e * 128 : (e + 1) * 128, :] = jnp.concatenate([aux, aux], axis=0).T
    seen = mask[pl.ds(pl.multiple_of(16 * eh, 16), 16), :].astype(jnp.float32)
    lane8 = lane_of((8, LANES))
    for s in range(2):
        back = -back_measured[s]
        for slot in range(3):
            at = 48 * s + 16 * slot
            gathered = jnp.concatenate(
                [turned[e * 128 + at : e * 128 + at + 16, :] for e in range(8)], axis=0
            )
            ranged = dot(range_pair[...], gathered)
            back = back + dot(ranged, beam_pair[slot])
        for c in range(2):
            for j in range(2):
                at = 96 + 2 * (4 * s + 2 * c) + j
                near = turned[pl.ds(at, 8, stride=128), :]
                far = turned[pl.ds(at + 2, 8, stride=128), :]
                value = jnp.where(lane8 < 64, near, far)
                sources[s, c, 8 * j : 8 * j + 8, :] = (
                    2.0 * seen[8 * j : 8 * j + 8] * value * back[8 * j : 8 * j + 8]
                )


def prepare_kernel(
    place, got, profile, turned, beam_mix, chirp_re, chirp_im,
    coef_re, coef_im, both_re, both_im, seen, back_measured, edge,
):
    e, f = place[0], place[1]
    lanes = lane_of((64, LANES))
    rows = row_of((64, LANES))
    square = lane_of((LANES, LANES))
    down = row_of((LANES, LANES))
    total = jnp.zeros((64, LANES), jnp.float32)
    left = lax.rem(f + PA - 1, PA)
    right = lax.rem(f + 1, PA)
    first = got[pl.ds(2, 64, stride=3), :]
    for dh in range(8):
        aux = first if dh == 0 else got[pl.ds(dh * 192 + 2, 64, stride=3), :]
        j = lax.rem(square, 64) - 2 * dh
        wanted = 80 + 32 * (square // 64) + 8 * j + e
        choose = jnp.where((j >= 0) & (j < 2) & (down == wanted), 1.0, 0.0)
        total = total + jnp.dot(aux, choose, preferred_element_type=jnp.float32)
        edge[dh : dh + 1, :] = jnp.sum(jnp.where(rows == left, aux, 0.0), axis=0, keepdims=True)
        edge[8 + dh : 9 + dh, :] = jnp.sum(jnp.where(rows == right, aux, 0.0), axis=0, keepdims=True)
    seen[...] = total
    for s in range(2):
        for j in range(2):
            slot = 2 * s + j
            start = pl.multiple_of(16 * e + 8 * j, 8)
            own = dot(turned.at[s][pl.ds(start, 8), :], beam_mix[LANES : 2 * LANES, :])
            shift = (LANES - 16 * slot) % LANES
            near = edge[0:8, :] if shift == 0 else pltpu.roll(edge[0:8, :], shift, 1)
            far = edge[8:16, :] if shift == 0 else pltpu.roll(edge[8:16, :], shift, 1)
            own = own + dot(near, beam_mix[0:LANES, :])
            own = own + dot(far, beam_mix[2 * LANES : 3 * LANES, :])
            back_measured[s, 8 * j : 8 * j + 8, :] = own

    def column(lane):
        return jnp.sum(jnp.where(lanes == lane, first, 0.0), axis=1, keepdims=True)

    pick0, pick1 = column(65), column(97)
    onehot = jnp.where(lanes < 16, pick0, pick1 + 16.0) == lanes.astype(jnp.float32)
    onehot = jnp.where(onehot & (lanes < 32), 1.0, 0.0)
    ground = jnp.where(lanes < 64, column(64), column(96))
    tall = row_of((512, LANES))
    choose = jnp.where(tall == 8 * lax.rem(lane_of((512, LANES)), 64) + e, 1.0, 0.0)
    lane16 = lane_of((16, LANES))
    for i in range(8):
        phase = dot(profile[:, 512 * i : 512 * (i + 1)], choose)
        height = 512 * i + 8 * lax.rem(lane16, 64) + e
        depth = jnp.maximum(height.astype(jnp.float32) - 0.75 * NH, 0.0) / (0.25 * NH)
        amount = abs(GAIN) * jnp.exp(-4.0 * depth * depth)
        angle = phase + float(np.angle(GAIN))
        pair = []
        for value in (amount * jnp.cos(angle), amount * jnp.sin(angle)):
            lower = jnp.where(lane16 < 64, value, 0.0)
            upper = jnp.where(lane16 < 64, 0.0, value)
            pair.append(
                dot(onehot, jnp.concatenate([lower, upper, jnp.zeros((96, LANES), jnp.float32)], axis=0))
            )
        at = slice(i * 64, i * 64 + 64)
        above = (512 * i + 8 * lax.rem(lanes, 64) + e).astype(jnp.float32) >= ground
        sr = jnp.where(above, pair[0], 0.0)
        si = jnp.where(above, pair[1], 0.0)
        dr, di = chirp_re[at, :], chirp_im[at, :]
        cr, ci = sr * dr - si * di, sr * di + si * dr
        coef_re[at, :] = cr
        coef_im[at, :] = ci
        both_re[at, :] = cr * dr - ci * di
        both_im[at, :] = cr * di + ci * dr


def turns(steps, modulus):
    angle = (steps % modulus).astype(jnp.float32) * (2.0 * math.pi / modulus)
    return jnp.cos(angle), jnp.sin(angle)


def layout_tables(e, f):
    row = lax.broadcasted_iota(jnp.int32, (ROWS, LANES), 0)
    lane = lax.broadcasted_iota(jnp.int32, (ROWS, LANES), 1)
    i, b = row // PA, row % PA
    q, r = lane // 64, lane % 64
    square_h = 64 * r * r + e * e + 1024 * i * e + 16 * r * e
    square_a = INV * (4096 * q * q + f * f + 128 * q * f) + ((256 * INV) % (2 * NA)) * b * f
    chirp = turns(2 * square_h + square_a, 2 * NA)
    twist = turns(-(16 * i * r + ((64 * INV) % NA) * b * q + 2 * i * e + (INV % NA) * b * f), NA)
    row = lax.broadcasted_iota(jnp.int32, (LANES, LANES), 0)
    lane = lax.broadcasted_iota(jnp.int32, (LANES, LANES), 1)
    q, r = row // 64, row % 64
    q2, r2 = lane // 64, lane % 64
    lane_dft = turns(
        -(128 * r2 * r + ((4096 * INV) % NA) * q2 * q + 16 * r2 * e + ((64 * INV) % NA) * q2 * f), NA
    )
    return chirp, twist, jnp.concatenate(lane_dft, axis=1)


def band(taps, offset):
    hit = offset[..., None] == lax.broadcasted_iota(jnp.int32, (1,) * offset.ndim + (taps.shape[0],), offset.ndim)
    return jnp.sum(jnp.where(hit, taps, 0.0), axis=-1)


def clutter_tables(pulse, beam, eh):
    half = (pulse.shape[0] - 1) // 2
    row = lax.broadcasted_iota(jnp.int32, (BOT, BOT), 0)
    col = lax.broadcasted_iota(jnp.int32, (BOT, BOT), 1)
    adjoint = band(pulse, row - col + half)
    own = lax.dynamic_slice_in_dim(adjoint, 16 * eh, 16, 0)
    moved = adjoint.reshape(16, 8, BOT).swapaxes(0, 1).reshape(BOT, BOT)
    range_pair = jnp.einsum("ir,hr->ih", own, moved, precision=HIGHEST)
    reach = (beam.shape[0] - 1) // 2
    row = lax.broadcasted_iota(jnp.int32, (3 * LANES, LANES), 0)
    col = lax.broadcasted_iota(jnp.int32, (3 * LANES, LANES), 1)
    block, inside = row // LANES, row % LANES
    at = jnp.where(block == 0, inside - 16, jnp.where(block == 1, inside, inside + LANES))
    valid = (block == 1) | (inside < 16)
    beam_mix = band(beam, jnp.where(valid, col - at + reach, -1))
    taps = beam.shape[0]
    first = lax.broadcasted_iota(jnp.int32, (taps, 2 * taps - 1), 0)
    shift = lax.broadcasted_iota(jnp.int32, (taps, 2 * taps - 1), 1) - (taps - 1)
    auto = jnp.sum(beam[:, None] * band(beam, first + shift), axis=0)
    slot = lax.broadcasted_iota(jnp.int32, (3, LANES, LANES), 0)
    at = lax.broadcasted_iota(jnp.int32, (3, LANES, LANES), 1)
    col = lax.broadcasted_iota(jnp.int32, (3, LANES, LANES), 2)
    azimuth = jnp.where(slot < 2, at + 64 * slot, jnp.where(at < 32, at + LANES, at - 64))
    beam_pair = band(auto, jnp.where(at < 64, azimuth - col + taps - 1, -1))
    return adjoint, range_pair, beam_mix, beam_pair


VMEM = pl.BlockSpec(memory_space=pltpu.VMEM)
SMEM = pl.BlockSpec(memory_space=pltpu.SMEM)


def f32(*shape):
    return jax.ShapeDtypeStruct(shape, jnp.float32)


def call(kernel, outs, scratch, args, smem=False, cost=2_000_000, interpret=False):
    specs = [SMEM if smem and n == 0 else VMEM for n in range(len(args))]
    return pl.pallas_call(
        kernel,
        out_shape=outs,
        in_specs=specs,
        out_specs=jax.tree.map(lambda _: VMEM, outs),
        scratch_shapes=[pltpu.VMEM(shape, jnp.float32) for shape in scratch],
        cost_estimate=pl.CostEstimate(flops=cost * 100, bytes_accessed=cost, transcendentals=0),
        interpret=interpret,
    )(*args)


def stage_pack(place, field, terrain, pick, mask, measured, adjoint, **kw):
    turned = jnp.einsum("hr,sra->sha", adjoint, measured, precision=HIGHEST)
    args = (place, field, terrain[None], pick[None], mask, turned)
    return call(pack_kernel, f32(3 * ROWS, LANES), [], args, smem=True, **kw), turned


def stage_first(got, chirp, twist, lane_dft, **kw):
    args = (got, *chirp, *twist, lane_dft, jnp.asarray(SPLIT_DFT))
    scratch = [(2 * ROWS, LANES), (ROWS, LANES), (ROWS, LANES)]
    return call(first_kernel, f32(2 * ROWS, LANES), scratch, args, **kw)


def stage_prepare(place, got, profile, turned, beam_mix, chirp, **kw):
    outs = tuple(f32(ROWS, LANES) for _ in range(4)) + (f32(64, LANES), f32(2, 16, LANES))
    args = (place, got, profile, turned, beam_mix, *chirp)
    return call(prepare_kernel, outs, [(16, LANES)], args, smem=True, **kw)


def stage_middle(got, coef, both, twist, lane_dft, **kw):
    args = (got, *coef, *both, *twist, lane_dft, jnp.asarray(SPLIT_DFT), jnp.asarray(MIXED_DFT))
    scratch = [(2 * ROWS, LANES), (ROWS, LANES), (ROWS, LANES), (2 * ROWS, LANES)]
    return call(middle_kernel, (f32(2 * ROWS, LANES), f32(2, 64, LANES)), scratch, args, **kw)


def stage_last(place, got, coef, strip, seen, **kw):
    args = (place, got, *coef, strip, seen, jnp.asarray(PAIRS), jnp.asarray(MIXED_DFT))
    scratch = [(2 * ROWS, LANES), (64, LANES), (64, LANES)]
    return call(last_kernel, f32(3 * ROWS, LANES), scratch, args, smem=True, **kw)


def stage_unpack(place, got, mask, back_measured, range_pair, beam_pair, **kw):
    outs = (f32(2, NH // PH, LANES), f32(2, 2, 16, LANES))
    args = (place, got, mask, back_measured, range_pair, beam_pair)
    return call(unpack_kernel, outs, [(8 * LANES, LANES)], args, smem=True, **kw)


def swap(rows):
    width = rows.shape[0] // ROWS
    shaped = rows.reshape((ROWS, 2, LANES) if width == 2 else (ROWS, 1, width * LANES))
    moved = lax.all_to_all(shaped, ("ha", "az"), split_axis=0, concat_axis=0, tiled=True)
    return moved.reshape(rows.shape)


def local(field, terrain, profile_pick, profile_table, clutter_mask, pulse, beam, measured):
    e = lax.axis_index("ha")
    f = lax.axis_index("az")
    place = jnp.stack([e, f]).astype(jnp.int32)
    adjoint, range_pair, beam_mix, beam_pair = clutter_tables(pulse, beam, e)
    chirp, twist, lane_dft = layout_tables(e, f)
    sent, turned = stage_pack(place, field, terrain, profile_pick, clutter_mask, measured, adjoint)
    got = swap(sent)
    sent = stage_first(got, chirp, twist, lane_dft)
    prepared = stage_prepare(place, got, profile_table, turned, beam_mix, chirp)
    coef, both, seen, back_measured = prepared[0:2], prepared[2:4], prepared[4], prepared[5]
    got = swap(sent)
    sent, strip = stage_middle(got, coef, both, twist, lane_dft)
    got = swap(sent)
    sent = stage_last(place, got, coef, strip, seen)
    got = swap(sent)
    return stage_unpack(place, got, clutter_mask, back_measured, range_pair, beam_pair)


def solution(mesh):
    return jax.shard_map(
        local,
        mesh=mesh,
        in_specs=(
            P(None, "ha", "az"),
            P("az"),
            P("az"),
            P(),
            P(None, "az"),
            P(),
            P(),
            P(None, None, "az"),
        ),
        out_specs=(P(None, "ha", "az"), P(None, None, "ha", "az")),
        check_vma=False,
    )
```

time: 522 us -> 175 us (0.34); the launches traced: 512 us -> 174 us
  local copies, waits for them, and re-layouts: 146 us -> 3.43 us
  blocking collectives: 101 us -> 0 us
  waiting for transfers between devices: 123 us -> 82.5 us
  starting transfers between devices: 89.8 us -> 50.1 us
  Pallas kernels: 0 us -> 23.6 us
  matrix products: 20.1 us -> 1.73 us
  between operations: 15.5 us -> 0.86 us
    all_to_all x4 -> x0, blocking collectives: 101 us -> none  [the longest x2 51.3 us: rows_to_slab(): return lax.all_to_all(rows, 'az', split_axis=2, concat_axis=1, tiled=True)]
    unnamed x26 -> x12, local copies, waits for them, and re-layouts: 85.3 us -> 3.41 us
    psum x1 -> x0, waiting for transfers between devices: 65.5 us -> none  [broadcast(): return lax.psum(block, axis)]
    ppermute x8 -> x0, starting transfers between devices: 53.7 us -> none  [the longest x4 41.9 us: with_halo(): lax.ppermute(head, axis, [((i + 1) % count, i) for i in range(count)])]
    all_to_all x11 -> x0, local copies, waits for them, and re-layouts: 30.1 us -> none  [the longest x3 18.8 us: rows_to_slab(): return lax.all_to_all(rows, 'az', split_axis=2, concat_axis=1, tiled=True)]
    another operation x14 -> x0, local copies, waits for them, and re-layouts: 25.5 us -> none  [the longest x2 15.4 us: turn_rows(): return jnp.stack([new_re, new_im])]
    all_to_all x4, waiting for transfers between devices: 57.1 us -> 82.5 us  [swap(): lax.all_to_all(shaped, ('ha', 'az'), split_axis=0, concat_axis=0, tiled=T...]
    pallas_call x0 -> x6, Pallas kernels: none -> 23.6 us  [call(): pl.pallas_call(kernel, out_shape=outs, in_specs=specs, out_specs=jax.tree...]
  transfers between devices with their start and end apart: 13 -> 4, of which waited for: 5 -> 4; matrix products, arithmetic and copies ran while one was open for 1% -> 6% of each run, Pallas kernels for 0% -> 3%
where the time goes in v1:
time: 175 us; the launch traced here: 174 us
  waiting for transfers between devices  82.5 us (47%)
  starting transfers between devices  50.1 us (29%)
  Pallas kernels  23.6 us (13%)
  other arithmetic  12.3 us (7%)
  local copies, waits for them, and re-layouts  3.43 us (2%)
    all_to_all x4, waiting for transfers between devices, swap(): lax.all_to_all(shaped, ('ha', 'az'), split_axis=0, concat_axis=0, tiled=T...  82.5 us
    all_to_all x4, starting transfers between devices, swap(): lax.all_to_all(shaped, ('ha', 'az'), split_axis=0, concat_axis=0, tiled=T...  50.1 us
    pallas_call x6, Pallas kernels, call(): pl.pallas_call(kernel, out_shape=outs, in_specs=specs, out_specs=jax.tree...  23.6 us
    sin x2, other arithmetic, turns(): return (jnp.cos(angle), jnp.sin(angle))  5.3 us
    reduce_sum x4, other arithmetic, band(): return jnp.sum(jnp.where(hit, taps, 0.0), axis=-1)  4.57 us
  transfers between devices with their start and end apart: 4, of which 4 were waited for; matrix products, arithmetic and copies ran while one was open for 6% of the time, Pallas kernels for 3%

profile of v1, /device:TPU:1, one launch (start us, length us, event | category | flops | bytes accessed | tf_op | source)
XLA Modules:
  0.0 174.5 jit_solution(16164802283733894850)
XLA Ops:
  0.6 0.0 copy-start
  0.7 0.6 pad_add_fusion.place
  1.3 1.1 select_reduce_fusion.2
  2.5 0.0 copy-done
  2.5 0.9 convolution_bitcast_fusion.turned
  3.4 2.4 %shard_map.122 = f32[1536,128]{1,0:T(8,128)} custom-call(s32[2]{0:T(128)} %pad_add_fusion.place, f32[2,512,128]{2,1,0:T(8,128)} %field.1, s32[1,128]{1,0:T(1,128)} %bitcast.34, s32[1,128]{1,0:T(1,128)} %bitcast.35, s32[128,128]{1,0:T(8,128)} %mask.3, f32[2,128,128]{2,1,0:T(8,128)} %convolution_bitcast_fusion.turned), custom_call_target="tpu_custom_call" | custom-call | flops 200000000 | bytes 2000000 | tf_op jit(solution)/shard_map/pallas_call | solution.py:390
  5.8 22.1 %all-to-all-start = ((f32[512,1,384]{2,1,0:T(1,128)}), f32[512,1,384]{2,1,0:T(1,128)S(1)}, u32[]{:S(2)}, u32[]{:S(2)}) async-start(f32[512,1,384]{2,1,0:T(1,128)} %bitcast.26), calls=%async_computation | async-start | bytes 1572864 | tf_op jit(solution)/shard_map/all_to_all | solution.py:440
  28.0 0.4 fusion.37
  28.4 0.7 pad_maximum_fusion.lane_dft
  29.1 2.6 %fusion.23 = (f32[512,128]{1,0:T(8,128)}, f32[512,128]{1,0:T(8,128)}) fusion(s32[]{:T(128)S(6)} %mul.206, s32[]{:T(128)S(6)} %mul.203, s32[128]{0:T(128)S(1)} %get-tuple-element.32, s32[128]{0:T(128)S(1)} %get-tuple-element.34, pred[128]{0:T(512)(128)(4,1)S(1)} %get-tuple-element.30, s32[512]{0:T(512)S(1)} %get-tuple-element.25, ...), kind=kLoop, calls=%fused_computation.61 | loop fusion | flops 1703936 | bytes 535816 | tf_op jit(solution)/shard_map/sin | solution.py:326
  31.7 2.7 %fusion.25 = (f32[512,128]{1,0:T(8,128)}, f32[512,128]{1,0:T(8,128)}) fusion(s32[]{:T(128)S(6)} %mul.193, s32[512]{0:T(512)S(1)} %get-tuple-element.25, s32[512]{0:T(512)S(1)} %get-tuple-element.26, pred[512]{0:T(512)(128)(4,1)S(1)} %get-tuple-element.29, s32[]{:T(128)S(6)} %mul.188, s32[]{:T(128)S(6)} %mul.187, s32[128]{0:T(128)S(1)} %get-tuple-element.32, ...), kind=kLoop, calls=%fused_computation.63 | loop fusion | flops 2228224 | bytes 535832 | tf_op jit(solution)/shard_map/sin | solution.py:326
  34.4 21.1 %all-to-all-done = f32[512,1,384]{2,1,0:T(1,128)S(1)} async-done(((f32[512,1,384]{2,1,0:T(1,128)}), f32[512,1,384]{2,1,0:T(1,128)S(1)}, u32[]{:S(2)}, u32[]{:S(2)}) %all-to-all-start) | async-done | bytes 786464 | tf_op jit(solution)/shard_map/all_to_all | solution.py:440
  55.5 0.0 copy-start.1
  55.5 0.9 copy-done.1
  56.4 3.9 %shard_map.123 = f32[1024,128]{1,0:T(8,128)} custom-call(f32[1536,128]{1,0:T(8,128)} %bitcast.23, f32[512,128]{1,0:T(8,128)} %get-tuple-element.21.chirp_re, f32[512,128]{1,0:T(8,128)} %get-tuple-element.20.chirp_im, f32[512,128]{1,0:T(8,128)} %get-tuple-element.19.twist_re, f32[512,128]{1,0:T(8,128)} %get-tuple-element.18.twist_im, ...), custom_call_target="tpu_custom_call" | custom-call | flops 200000000 | bytes 2000000 | tf_op jit(solution)/shard_map/pallas_call | solution.py:390
  60.3 0.0 copy-start.5
  60.3 9.6 %all-to-all-start.1 = ((f32[512,2,128]{2,1,0:T(2,128)}), f32[512,2,128]{2,1,0:T(2,128)S(1)}, u32[]{:S(2)}, u32[]{:S(2)}) async-start(f32[512,2,128]{2,1,0:T(2,128)} %bitcast.28), calls=%async_computation.1 | async-start | bytes 1048576 | tf_op jit(solution)/shard_map/all_to_all | solution.py:440
  70.0 0.4 fusion.22
  70.4 0.0 copy-done.5
  70.4 1.3 select_reduce_fusion.1.beam_mix
  71.7 6.0 %shard_map.124 = (f32[512,128]{1,0:T(8,128)}, f32[512,128]{1,0:T(8,128)}, f32[512,128]{1,0:T(8,128)}, f32[512,128]{1,0:T(8,128)}, f32[64,128]{1,0:T(8,128)}, /*index=5*/f32[2,16,128]{2,1,0:T(8,128)}) custom-call(s32[2]{0:T(128)} %pad_add_fusion.place, f32[1536,128]{1,0:T(8,128)} %bitcast.24, f32[16,4096]{1,0:T(8,128)} %profile.1, ...), custom_call_target="tpu_custom_call" | custom-call | flops 200000000 | bytes 2000000 | tf_op jit(solution)/shard_map/pallas_call | solution.py:390
  77.7 14.6 %all-to-all-done.1 = f32[512,2,128]{2,1,0:T(2,128)S(1)} async-done(((f32[512,2,128]{2,1,0:T(2,128)}), f32[512,2,128]{2,1,0:T(2,128)S(1)}, u32[]{:S(2)}, u32[]{:S(2)}) %all-to-all-start.1) | async-done | bytes 524320 | tf_op jit(solution)/shard_map/all_to_all | solution.py:440
  92.3 0.0 copy-start.4
  92.3 0.8 copy-done.4
  93.1 4.7 %shard_map.125 = (f32[1024,128]{1,0:T(8,128)}, f32[2,64,128]{2,1,0:T(8,128)}) custom-call(f32[1024,128]{1,0:T(8,128)} %bitcast.30, f32[512,128]{1,0:T(8,128)} %get-tuple-element.10.coef_re, f32[512,128]{1,0:T(8,128)} %get-tuple-element.11.coef_im, f32[512,128]{1,0:T(8,128)} %get-tuple-element.12.both_re, f32[512,128]{1,0:T(8,128)} %get-tuple-element.13.both_im, ...), custom_call_target="tpu_custom_call" | custom-call | flops 200000000 | bytes 2000000 | tf_op jit(solution)/shard_map/pallas_call | solution.py:390
  97.8 9.2 %all-to-all-start.2 = ((f32[512,2,128]{2,1,0:T(2,128)}), f32[512,2,128]{2,1,0:T(2,128)S(1)}, u32[]{:S(2)}, u32[]{:S(2)}) async-start(f32[512,2,128]{2,1,0:T(2,128)} %bitcast.32), calls=%async_computation.2 | async-start | bytes 1048576 | tf_op jit(solution)/shard_map/all_to_all | solution.py:440
  107.0 22.3 %all-to-all-done.2 = f32[512,2,128]{2,1,0:T(2,128)S(1)} async-done(((f32[512,2,128]{2,1,0:T(2,128)}), f32[512,2,128]{2,1,0:T(2,128)S(1)}, u32[]{:S(2)}, u32[]{:S(2)}) %all-to-all-start.2) | async-done | bytes 524320 | tf_op jit(solution)/shard_map/all_to_all | solution.py:440
  129.3 0.0 copy-start.3
  129.3 0.8 copy-done.3
  130.1 3.5 %shard_map.126 = f32[1536,128]{1,0:T(8,128)} custom-call(s32[2]{0:T(128)} %pad_add_fusion.place, f32[1024,128]{1,0:T(8,128)} %bitcast.29, f32[512,128]{1,0:T(8,128)} %get-tuple-element.10.coef_re, f32[512,128]{1,0:T(8,128)} %get-tuple-element.11.coef_im, f32[2,64,128]{2,1,0:T(8,128)} %get-tuple-element.15.strip, f32[64,128]{1,0:T(8,128)} %get-tuple-element.16.seen, ...), custom_call_target="tpu_custom_call" | custom-call | flops 200000000 | bytes 2000000 | tf_op jit(solution)/shard_map/pallas_call | solution.py:390
  133.6 9.2 %all-to-all-start.3 = ((f32[512,1,384]{2,1,0:T(1,128)}), f32[512,1,384]{2,1,0:T(1,128)S(1)}, u32[]{:S(2)}, u32[]{:S(2)}) async-start(f32[512,1,384]{2,1,0:T(1,128)} %bitcast.25), calls=%async_computation.3 | async-start | bytes 1572864 | tf_op jit(solution)/shard_map/all_to_all | solution.py:440
  142.9 0.2 select_reduce_fusion.3
  143.1 0.1 multiply_reduce_fusion
  143.1 0.8 fusion.38.range_pair
  144.0 0.1 add_select_fusion.2
  144.1 1.9 %select_reduce_fusion.beam_pair = f32[3,128,128]{2,1,0:T(8,128)} fusion(f32[61]{0:T(128)S(1)} %multiply_reduce_fusion, s32[3,128,128]{2,1,0:T(8,128)S(1)} %add_select_fusion.2), kind=kLoop, calls=%fused_computation | loop fusion | flops 8945664 | bytes 393460 | tf_op jit(solution)/shard_map/reduce_sum | solution.py:350
  146.0 24.4 %all-to-all-done.3 = f32[512,1,384]{2,1,0:T(1,128)S(1)} async-done(((f32[512,1,384]{2,1,0:T(1,128)}), f32[512,1,384]{2,1,0:T(1,128)S(1)}, u32[]{:S(2)}, u32[]{:S(2)}) %all-to-all-start.3) | async-done | bytes 786464 | tf_op jit(solution)/shard_map/all_to_all | solution.py:440
  170.5 0.0 copy-start.2
  170.5 0.9 copy-done.2
  171.4 3.1 %shard_map.127 = (f32[2,512,128]{2,1,0:T(8,128)}, f32[2,2,16,128]{3,2,1,0:T(8,128)}) custom-call(s32[2]{0:T(128)} %pad_add_fusion.place, f32[1536,128]{1,0:T(8,128)} %bitcast.27, s32[128,128]{1,0:T(8,128)} %mask.3, f32[2,16,128]{2,1,0:T(8,128)} %get-tuple-element.17.back_measured, f32[16,128]{1,0:T(8,128)} %fusion.38.range_pair, ...), custom_call_target="tpu_custom_call" | custom-call | flops 200000000 | bytes 2000000 | tf_op jit(solution)/shard_map/pallas_call | solution.py:390
  (17 shorter events, 0.1 us)
Async XLA Ops:
  0.6 1.8 %copy-start = (f32[2,128,128]{2,1,0:T(8,128)S(1)}, f32[2,128,128]{2,1,0:T(8,128)}, u32[]{:S(2)}) copy-start(f32[2,128,128]{2,1,0:T(8,128)} %param.18) | copy-start | bytes 393220
  5.8 49.7 %all-to-all-start = ((f32[512,1,384]{2,1,0:T(1,128)}), f32[512,1,384]{2,1,0:T(1,128)S(1)}, u32[]{:S(2)}, u32[]{:S(2)}) async-start(f32[512,1,384]{2,1,0:T(1,128)} %bitcast.26), calls=%async_computation | async-start | bytes 1572864 | tf_op jit(solution)/shard_map/all_to_all | solution.py:440
  55.5 0.9 copy-start.1
  60.3 10.1 %copy-start.5 = (f32[31]{0:T(128)S(1)}, f32[31]{0:T(128)}, u32[]{:S(2)}) copy-start(f32[31]{0:T(128)} %param.17) | copy-start | bytes 376
  60.3 32.0 %all-to-all-start.1 = ((f32[512,2,128]{2,1,0:T(2,128)}), f32[512,2,128]{2,1,0:T(2,128)S(1)}, u32[]{:S(2)}, u32[]{:S(2)}) async-start(f32[512,2,128]{2,1,0:T(2,128)} %bitcast.28), calls=%async_computation.1 | async-start | bytes 1048576 | tf_op jit(solution)/shard_map/all_to_all | solution.py:440
  92.3 0.8 copy-start.4
  97.8 31.5 %all-to-all-start.2 = ((f32[512,2,128]{2,1,0:T(2,128)}), f32[512,2,128]{2,1,0:T(2,128)S(1)}, u32[]{:S(2)}, u32[]{:S(2)}) async-start(f32[512,2,128]{2,1,0:T(2,128)} %bitcast.32), calls=%async_computation.2 | async-start | bytes 1048576 | tf_op jit(solution)/shard_map/all_to_all | solution.py:440
  129.3 0.8 copy-start.3
  133.6 36.8 %all-to-all-start.3 = ((f32[512,1,384]{2,1,0:T(1,128)}), f32[512,1,384]{2,1,0:T(1,128)S(1)}, u32[]{:S(2)}, u32[]{:S(2)}) async-start(f32[512,1,384]{2,1,0:T(1,128)} %bitcast.25), calls=%async_computation.3 | async-start | bytes 1572864 | tf_op jit(solution)/shard_map/all_to_all | solution.py:440
  170.5 0.9 copy-start.2

commit v2 on v1

--- a/solution.py
+++ b/solution.py
@@ -18,6 +18,7 @@
 azimuth_chirp = 3
 INV = pow(azimuth_chirp, -1, 2 * NA)
 HIGHEST = lax.Precision.HIGHEST
+GRANT = 8 * 2**20
 
 
 def gauss(count, spread):
@@ -34,6 +35,40 @@
     split = np.block([[re, -im], [im, re]])
     mixed = split.reshape(2 * PA, 2, PA).transpose(0, 2, 1).reshape(2 * PA, 2 * PA)
     return split.astype(np.float32), mixed.astype(np.float32)
+
+
+def halves(value):
+    high = value.astype(jnp.bfloat16)
+    return high, (value - high.astype(jnp.float32)).astype(jnp.bfloat16)
+
+
+def rounded_halves(value):
+    high = lax.reduce_precision(value, 8, 7)
+    return high.astype(jnp.bfloat16), (value - high).astype(jnp.bfloat16)
+
+
+def matrix_left(value, split=rounded_halves):
+    high, low = split(value)
+    return jnp.concatenate([high, high, low], axis=1)
+
+
+def matrix_right(value):
+    high, low = rounded_halves(value)
+    return jnp.concatenate([high, high, low], axis=0)
+
+
+def data_left(value):
+    high, low = halves(value)
+    return jnp.concatenate([high, low, high], axis=1)
+
+
+def data_right(value):
+    high, low = halves(value)
+    return jnp.concatenate([high, low, high], axis=0)
+
+
+def product(left, right):
+    return jnp.dot(left, right, preferred_element_type=jnp.float32)
 
 
 SPLIT_DFT, MIXED_DFT = row_matrices()
@@ -95,8 +130,17 @@
     return jnp.where(lane_of((64, LANES)) < 64, turned[:64], turned[64:])
 
 
-def pack_kernel(place, field, terrain, pick, mask, turned, out):
+def pack_kernel(place, field, terrain, pick, mask, measured, pulse, out, turned, taps):
     dh, da = place[0], place[1]
+    taps[...] = jnp.zeros_like(taps)
+    taps[:, 0 : pulse.shape[1]] = pulse[...]
+    half = (pulse.shape[1] - 1) // 2
+    wide = jnp.broadcast_to(taps[...], (BOT, 2 * LANES))
+    adjoint = pltpu.roll(wide, 2 * LANES - half, 1, stride=1, stride_axis=0)[:, :LANES]
+    both = jnp.concatenate([measured[0], measured[1]], axis=1)
+    result = product(matrix_left(adjoint.T, halves), data_right(both))
+    turned[0] = result[:, :LANES]
+    turned[1] = result[:, LANES:]
     lanes = lane_of((64, LANES))
     rows = row_of((64, LANES))
     pads = [
@@ -132,37 +176,44 @@
         out[pl.ds(e * 192 + 2, 64, stride=3), :] = jnp.where(lanes < 64, edge, common)
 
 
-def finish_send(held, twist_re, twist_im, lane_dft, out, mid_re, mid_im):
+def finish_send(held, twist_re, twist_im, lane_dft, out, mid):
     for group in range(8):
         re, im = dft8_group(held, group)
         for k in range(8):
             at = slice(k * 64 + 8 * group, k * 64 + 8 * group + 8)
             tr, ti = twist_re[at, :], twist_im[at, :]
-            mid_re[at, :] = re[k] * tr - im[k] * ti
-            mid_im[at, :] = re[k] * ti + im[k] * tr
-    from_re = dot(mid_re[...], lane_dft[...])
-    from_im = dot(mid_im[...], lane_dft[...])
-    out[pl.ds(0, ROWS, stride=2), :] = from_re[:, :LANES] - from_im[:, LANES:]
-    out[pl.ds(1, ROWS, stride=2), :] = from_re[:, LANES:] + from_im[:, :LANES]
-
-
-def first_kernel(got, chirp_re, chirp_im, twist_re, twist_im, lane_dft, split, out, held, mid_re, mid_im):
-    for i in range(8):
+            mid[at, :LANES] = re[k] * tr - im[k] * ti
+            mid[at, LANES:] = re[k] * ti + im[k] * tr
+    result = product(data_left(mid[...]), lane_dft[...])
+    out[pl.ds(0, ROWS, stride=2), :] = result[:, :LANES]
+    out[pl.ds(1, ROWS, stride=2), :] = result[:, LANES:]
+
+
+def row_dft(matrix, blocks, held):
+    for i in range(0, 8, 2):
+        pair = jnp.concatenate([blocks(i), blocks(i + 1)], axis=1)
+        result = product(matrix[...], data_right(pair))
+        held[i * 128 : (i + 1) * 128, :] = result[:, :LANES]
+        held[(i + 1) * 128 : (i + 2) * 128, :] = result[:, LANES:]
+
+
+def first_kernel(got, chirp_re, chirp_im, twist_re, twist_im, lane_dft, split, out, held, mid):
+    def block(i):
         xr = got[pl.ds(i * 192, 64, stride=3), :]
         xi = got[pl.ds(i * 192 + 1, 64, stride=3), :]
         at = slice(i * 64, i * 64 + 64)
         dr, di = chirp_re[at, :], chirp_im[at, :]
-        both = jnp.concatenate([xr * dr - xi * di, xr * di + xi * dr], axis=0)
-        held[i * 128 : (i + 1) * 128, :] = dot(split[...], both)
-    finish_send(held, twist_re, twist_im, lane_dft, out, mid_re, mid_im)
+        return jnp.concatenate([xr * dr - xi * di, xr * di + xi * dr], axis=0)
+
+    row_dft(split, block, held)
+    finish_send(held, twist_re, twist_im, lane_dft, out, mid)
 
 
 def middle_kernel(
     got, coef_re, coef_im, both_re, both_im, twist_re, twist_im, lane_dft, split, mixed,
-    out, strip, held, mid_re, mid_im, next_in,
+    out, strip, held, mid, next_in,
 ):
-    for i in range(8):
-        held[i * 128 : (i + 1) * 128, :] = dot(mixed[...], got[i * 128 : (i + 1) * 128, :])
+    row_dft(mixed, lambda i: got[i * 128 : (i + 1) * 128, :], held)
     for group in range(8):
         re, im = dft8_group(held, group)
         low = 8 * group
@@ -174,15 +225,13 @@
             cr, ci = both_re[at, :], both_im[at, :]
             next_in[k * 128 + low : k * 128 + low + 8, :] = re[k] * cr - im[k] * ci
             next_in[k * 128 + 64 + low : k * 128 + 64 + low + 8, :] = re[k] * ci + im[k] * cr
-    for i in range(8):
-        held[i * 128 : (i + 1) * 128, :] = dot(split[...], next_in[i * 128 : (i + 1) * 128, :])
-    finish_send(held, twist_re, twist_im, lane_dft, out, mid_re, mid_im)
+    row_dft(split, lambda i: next_in[i * 128 : (i + 1) * 128, :], held)
+    finish_send(held, twist_re, twist_im, lane_dft, out, mid)
 
 
 def last_kernel(place, got, coef_re, coef_im, strip, seen, pairs, mixed, out, held, low_re, low_im):
     f = place[1]
-    for i in range(8):
-        held[i * 128 : (i + 1) * 128, :] = dot(mixed[...], got[i * 128 : (i + 1) * 128, :])
+    row_dft(mixed, lambda i: got[i * 128 : (i + 1) * 128, :], held)
     for group in range(8):
         re, im = dft8_group(held, group)
         low = 8 * group
@@ -198,9 +247,8 @@
                 low_im[low : low + 8, :] = new_im
     lanes = lane_of((64, LANES))
     parts = [strip[0], strip[1], low_re[...], low_im[...]]
-    chosen = dot(parts[0], pairs[0:LANES, :])
-    for part in range(1, 4):
-        chosen = chosen + dot(parts[part], pairs[part * LANES : (part + 1) * LANES, :])
+    high, low = halves(jnp.concatenate(parts, axis=1))
+    chosen = product(high, pairs[...]) + product(low, pairs[...])
     powers = jnp.zeros((64, LANES), jnp.float32)
     for s in range(2):
         power = seen[...] * (parts[2 * s] * parts[2 * s] + parts[2 * s + 1] * parts[2 * s + 1])
@@ -232,15 +280,18 @@
         turned[e * 128 : (e + 1) * 128, :] = jnp.concatenate([aux, aux], axis=0).T
     seen = mask[pl.ds(pl.multiple_of(16 * eh, 16), 16), :].astype(jnp.float32)
     lane8 = lane_of((8, LANES))
+    gathered = []
     for s in range(2):
-        back = -back_measured[s]
         for slot in range(3):
             at = 48 * s + 16 * slot
-            gathered = jnp.concatenate(
-                [turned[e * 128 + at : e * 128 + at + 16, :] for e in range(8)], axis=0
+            gathered.append(
+                jnp.concatenate([turned[e * 128 + at : e * 128 + at + 16, :] for e in range(8)], axis=0)
             )
-            ranged = dot(range_pair[...], gathered)
-            back = back + dot(ranged, beam_pair[slot])
+    ranged = product(range_pair[...], data_right(jnp.concatenate(gathered, axis=1)))
+    ranged = jnp.concatenate([ranged[:, : 3 * LANES], ranged[:, 3 * LANES :]], axis=0)
+    both_steps = product(data_left(ranged), beam_pair[...])
+    for s in range(2):
+        back = both_steps[16 * s : 16 * s + 16] - back_measured[s]
         for c in range(2):
             for j in range(2):
                 at = 96 + 2 * (4 * s + 2 * c) + j
@@ -342,7 +393,9 @@
     lane_dft = turns(
         -(128 * r2 * r + ((4096 * INV) % NA) * q2 * q + 16 * r2 * e + ((64 * INV) % NA) * q2 * f), NA
     )
-    return chirp, twist, jnp.concatenate(lane_dft, axis=1)
+    re, im = lane_dft
+    whole = jnp.concatenate([jnp.concatenate([re, im], axis=1), jnp.concatenate([-im, re], axis=1)], axis=0)
+    return chirp, twist, matrix_right(whole)
 
 
 def band(taps, offset):
@@ -374,7 +427,7 @@
     col = lax.broadcasted_iota(jnp.int32, (3, LANES, LANES), 2)
     azimuth = jnp.where(slot < 2, at + 64 * slot, jnp.where(at < 32, at + LANES, at - 64))
     beam_pair = band(auto, jnp.where(at < 64, azimuth - col + taps - 1, -1))
-    return adjoint, range_pair, beam_mix, beam_pair
+    return matrix_left(range_pair), beam_mix, matrix_right(beam_pair.reshape(3 * LANES, LANES))
 
 
 VMEM = pl.BlockSpec(memory_space=pltpu.VMEM)
@@ -385,8 +438,16 @@
     return jax.ShapeDtypeStruct(shape, jnp.float32)
 
 
-def call(kernel, outs, scratch, args, smem=False, cost=2_000_000, interpret=False):
-    specs = [SMEM if smem and n == 0 else VMEM for n in range(len(args))]
+def placed(kernel, *refs):
+    return kernel((lax.axis_index("ha"), lax.axis_index("az")), *refs)
+
+
+def call(kernel, outs, scratch, args, place=None, cost=2_000_000, interpret=False):
+    specs = [VMEM] * len(args)
+    if place == "here":
+        kernel = functools.partial(placed, kernel)
+    elif place is not None:
+        specs, args = [SMEM] + specs, (place, *args)
     return pl.pallas_call(
         kernel,
         out_shape=outs,
@@ -394,44 +455,53 @@
         out_specs=jax.tree.map(lambda _: VMEM, outs),
         scratch_shapes=[pltpu.VMEM(shape, jnp.float32) for shape in scratch],
         cost_estimate=pl.CostEstimate(flops=cost * 100, bytes_accessed=cost, transcendentals=0),
+        compiler_params=pltpu.CompilerParams(vmem_limit_bytes=GRANT),
         interpret=interpret,
     )(*args)
 
 
-def stage_pack(place, field, terrain, pick, mask, measured, adjoint, **kw):
-    turned = jnp.einsum("hr,sra->sha", adjoint, measured, precision=HIGHEST)
-    args = (place, field, terrain[None], pick[None], mask, turned)
-    return call(pack_kernel, f32(3 * ROWS, LANES), [], args, smem=True, **kw), turned
+def split_matrix():
+    return matrix_left(jnp.asarray(SPLIT_DFT))
+
+
+def mixed_matrix():
+    return matrix_left(jnp.asarray(MIXED_DFT))
+
+
+def stage_pack(place, field, terrain, pick, mask, measured, pulse, **kw):
+    args = (field, terrain[None], pick[None], mask, measured, pulse[None])
+    outs = (f32(3 * ROWS, LANES), f32(2, BOT, LANES))
+    return call(pack_kernel, outs, [(1, 2 * LANES)], args, place, **kw)
 
 
 def stage_first(got, chirp, twist, lane_dft, **kw):
-    args = (got, *chirp, *twist, lane_dft, jnp.asarray(SPLIT_DFT))
-    scratch = [(2 * ROWS, LANES), (ROWS, LANES), (ROWS, LANES)]
+    args = (got, *chirp, *twist, lane_dft, split_matrix())
+    scratch = [(2 * ROWS, LANES), (ROWS, 2 * LANES)]
     return call(first_kernel, f32(2 * ROWS, LANES), scratch, args, **kw)
 
 
 def stage_prepare(place, got, profile, turned, beam_mix, chirp, **kw):
     outs = tuple(f32(ROWS, LANES) for _ in range(4)) + (f32(64, LANES), f32(2, 16, LANES))
-    args = (place, got, profile, turned, beam_mix, *chirp)
-    return call(prepare_kernel, outs, [(16, LANES)], args, smem=True, **kw)
+    args = (got, profile, turned, beam_mix, *chirp)
+    return call(prepare_kernel, outs, [(16, LANES)], args, place, **kw)
 
 
 def stage_middle(got, coef, both, twist, lane_dft, **kw):
-    args = (got, *coef, *both, *twist, lane_dft, jnp.asarray(SPLIT_DFT), jnp.asarray(MIXED_DFT))
-    scratch = [(2 * ROWS, LANES), (ROWS, LANES), (ROWS, LANES), (2 * ROWS, LANES)]
+    args = (got, *coef, *both, *twist, lane_dft, split_matrix(), mixed_matrix())
+    scratch = [(2 * ROWS, LANES), (ROWS, 2 * LANES), (2 * ROWS, LANES)]
     return call(middle_kernel, (f32(2 * ROWS, LANES), f32(2, 64, LANES)), scratch, args, **kw)
 
 
 def stage_last(place, got, coef, strip, seen, **kw):
-    args = (place, got, *coef, strip, seen, jnp.asarray(PAIRS), jnp.asarray(MIXED_DFT))
+    args = (got, *coef, strip, seen, jnp.asarray(PAIRS).astype(jnp.bfloat16), mixed_matrix())
     scratch = [(2 * ROWS, LANES), (64, LANES), (64, LANES)]
-    return call(last_kernel, f32(3 * ROWS, LANES), scratch, args, smem=True, **kw)
+    return call(last_kernel, f32(3 * ROWS, LANES), scratch, args, place, **kw)
 
 
 def stage_unpack(place, got, mask, back_measured, range_pair, beam_pair, **kw):
     outs = (f32(2, NH // PH, LANES), f32(2, 2, 16, LANES))
-    args = (place, got, mask, back_measured, range_pair, beam_pair)
-    return call(unpack_kernel, outs, [(8 * LANES, LANES)], args, smem=True, **kw)
+    args = (got, mask, back_measured, range_pair, beam_pair)
+    return call(unpack_kernel, outs, [(8 * LANES, LANES)], args, place, **kw)
 
 
 def swap(rows):
@@ -444,10 +514,10 @@
 def local(field, terrain, profile_pick, profile_table, clutter_mask, pulse, beam, measured):
     e = lax.axis_index("ha")
     f = lax.axis_index("az")
-    place = jnp.stack([e, f]).astype(jnp.int32)
-    adjoint, range_pair, beam_mix, beam_pair = clutter_tables(pulse, beam, e)
+    place = "here"
+    range_pair, beam_mix, beam_pair = clutter_tables(pulse, beam, e)
     chirp, twist, lane_dft = layout_tables(e, f)
-    sent, turned = stage_pack(place, field, terrain, profile_pick, clutter_mask, measured, adjoint)
+    sent, turned = stage_pack(place, field, terrain, profile_pick, clutter_mask, measured, pulse)
     got = swap(sent)
     sent = stage_first(got, chirp, twist, lane_dft)
     prepared = stage_prepare(place, got, profile_table, turned, beam_mix, chirp)

time: 175 us -> 167 us (0.954)
  Pallas kernels: 23.6 us -> 11.4 us
  local copies, waits for them, and re-layouts: 3.43 us -> 9.64 us
  other arithmetic: 12.3 us -> 6.23 us
  waiting for transfers between devices: 82.5 us -> 87.4 us
    pallas_call x6, Pallas kernels: 23.6 us -> 11.4 us  [call(): pl.pallas_call(kernel, out_shape=outs, in_specs=specs, out_specs=jax.tree...]
    unnamed x12 -> x38, local copies, waits for them, and re-layouts: 3.41 us -> 9.62 us
    all_to_all x4, waiting for transfers between devices: 82.5 us -> 87.4 us  [swap(): lax.all_to_all(shaped, ('ha', 'az'), split_axis=0, concat_axis=0, tiled=T...]
    sin x2 -> x3, other arithmetic: 5.3 us -> 2.86 us  [turns(): return (jnp.cos(angle), jnp.sin(angle))]
    reduce_sum x4, other arithmetic: 4.57 us -> 2.53 us  [band(): return jnp.sum(jnp.where(hit, taps, 0.0), axis=-1)]
  transfers between devices with their start and end apart: 4 -> 4, of which waited for: 4 -> 4; matrix products, arithmetic and copies ran while one was open for 6% -> 4% of each run, Pallas kernels for 3% -> 2%
where the time goes in v2:
time: 167 us; the launch traced here: 166 us
  waiting for transfers between devices  87.4 us (52%)
  starting transfers between devices  50.3 us (30%)
  Pallas kernels  11.4 us (7%)
  local copies, waits for them, and re-layouts  9.64 us (6%)
  other arithmetic  6.23 us (4%)
    all_to_all x4, waiting for transfers between devices, swap(): lax.all_to_all(shaped, ('ha', 'az'), split_axis=0, concat_axis=0, tiled=T...  87.4 us
    all_to_all x4, starting transfers between devices, swap(): lax.all_to_all(shaped, ('ha', 'az'), split_axis=0, concat_axis=0, tiled=T...  50.3 us
    pallas_call x6, Pallas kernels, call(): pl.pallas_call(kernel, out_shape=outs, in_specs=specs, out_specs=jax.tree...  11.4 us
    unnamed x38, local copies, waits for them, and re-layouts  9.62 us
  transfers between devices with their start and end apart: 4, of which 4 were waited for; matrix products, arithmetic and copies ran while one was open for 4% of the time, Pallas kernels for 2%

profile of v2, /device:TPU:1, one launch (start us, length us, event | category | flops | bytes accessed | tf_op | source)
XLA Modules:
  0.0 166.1 jit_solution(17098909381251197071)
XLA Ops:
  0.6 0.0 copy-start.10
  0.6 0.8 copy-done.10
  1.5 0.0 copy-start.12
  1.5 0.7 copy-done.12
  2.1 0.0 copy-start.14
  2.1 1.0 copy-done.14
  3.2 0.0 copy-start.15
  3.2 0.9 copy-done.15
  4.1 0.0 copy-start.16
  4.1 0.7 copy-done.16
  4.7 0.0 copy-start.17
  4.7 0.7 copy-done.17
  5.4 1.4 shard_map.122
  6.8 0.0 copy-start.8
  6.8 0.7 copy-done.8
  7.5 22.1 %all-to-all-start = ((f32[512,1,384]{2,1,0:T(1,128)}), f32[512,1,384]{2,1,0:T(1,128)S(1)}, u32[]{:S(2)}, u32[]{:S(2)}) async-start(f32[512,1,384]{2,1,0:T(1,128)} %bitcast.3), calls=%async_computation | async-start | bytes 1572864 | tf_op jit(solution)/shard_map/all_to_all | solution.py:510
  29.7 0.4 fusion.37
  30.1 0.0 copy-start.1
  30.2 1.2 fusion.25
  31.4 1.2 fusion.27
  32.7 24.5 %all-to-all-done = f32[512,1,384]{2,1,0:T(1,128)S(1)} async-done(((f32[512,1,384]{2,1,0:T(1,128)}), f32[512,1,384]{2,1,0:T(1,128)S(1)}, u32[]{:S(2)}, u32[]{:S(2)}) %all-to-all-start) | async-done | bytes 786464 | tf_op jit(solution)/shard_map/all_to_all | solution.py:510
  57.2 0.0 copy-done.1
  57.2 1.6 shard_map.123
  58.8 0.0 copy-start.18
  58.8 9.6 %all-to-all-start.1 = ((f32[512,2,128]{2,1,0:T(2,128)}), f32[512,2,128]{2,1,0:T(2,128)S(1)}, u32[]{:S(2)}, u32[]{:S(2)}) async-start(f32[512,2,128]{2,1,0:T(2,128)} %bitcast.5), calls=%async_computation.1 | async-start | bytes 1048576 | tf_op jit(solution)/shard_map/all_to_all | solution.py:510
  68.4 0.0 copy-start.2
  68.4 0.4 fusion.24
  68.8 0.0 copy-done.18
  68.8 0.7 select_reduce_fusion.1.refs_3_
  69.5 0.0 copy-done.2
  69.5 0.0 copy-start.9
  69.5 0.9 copy-done.9
  70.4 0.0 copy-start
  70.4 3.5 %shard_map.124 = (f32[512,128]{1,0:T(8,128)S(1)}, f32[512,128]{1,0:T(8,128)S(1)}, f32[512,128]{1,0:T(8,128)S(1)}, f32[512,128]{1,0:T(8,128)S(1)}, f32[64,128]{1,0:T(8,128)S(1)}, /*index=5*/f32[2,16,128]{2,1,0:T(8,128)S(1)}) custom-call(f32[1536,128]{1,0:T(8,128)S(1)} %bitcast.20, f32[16,4096]{1,0:T(8,128)S(1)} %copy-done.2, f32[2,128,128]{2,1,0:T(8,128)S(1)} %copy-done.9, ...), custom_call_target="tpu_custom_call" | custom-call | flops 200000000 | bytes 2000000 | tf_op jit(solution)/shard_map/pallas_call | solution.py:451
  74.0 0.0 copy-start.3
  74.0 0.7 copy-done.3
  74.7 0.0 copy-start.5
  74.7 0.7 copy-done.5
  75.4 15.4 %all-to-all-done.1 = f32[512,2,128]{2,1,0:T(2,128)S(1)} async-done(((f32[512,2,128]{2,1,0:T(2,128)}), f32[512,2,128]{2,1,0:T(2,128)S(1)}, u32[]{:S(2)}, u32[]{:S(2)}) %all-to-all-start.1) | async-done | bytes 524320 | tf_op jit(solution)/shard_map/all_to_all | solution.py:510
  90.8 0.0 copy-done
  90.8 0.0 copy-start.4
  90.8 0.9 copy-done.4
  91.7 0.0 copy-start.6
  91.7 0.9 copy-done.6
  92.7 2.0 %shard_map.125 = (f32[1024,128]{1,0:T(8,128)}, f32[2,64,128]{2,1,0:T(8,128)S(1)}) custom-call(f32[1024,128]{1,0:T(8,128)S(1)} %bitcast.22, f32[512,128]{1,0:T(8,128)S(1)} %get-tuple-element.14.coef_re.refs_1_, f32[512,128]{1,0:T(8,128)S(1)} %get-tuple-element.15.coef_im.refs_2_, f32[512,128]{1,0:T(8,128)S(1)} %copy-done.4, f32[512,128]{1,0:T(8,128)S(1)} %copy-done.6, ...), custom_call_target="tpu_custom_call" | custom-call | flops 200000000 | bytes 2000000 | tf_op jit(solution)/shard_map/pallas_call | solution.py:451
  94.6 0.0 copy-start.13
  94.6 0.0 copy-start.7
  94.6 9.3 %all-to-all-start.2 = ((f32[512,2,128]{2,1,0:T(2,128)}), f32[512,2,128]{2,1,0:T(2,128)S(1)}, u32[]{:S(2)}, u32[]{:S(2)}) async-start(f32[512,2,128]{2,1,0:T(2,128)} %bitcast.7), calls=%async_computation.2 | async-start | bytes 1048576 | tf_op jit(solution)/shard_map/all_to_all | solution.py:510
  104.0 0.0 copy-done.13
  104.0 0.5 select_reduce_fusion.2
  104.5 0.2 reduce-precision_convert_fusion.2
  104.8 21.6 %all-to-all-done.2 = f32[512,2,128]{2,1,0:T(2,128)S(1)} async-done(((f32[512,2,128]{2,1,0:T(2,128)}), f32[512,2,128]{2,1,0:T(2,128)S(1)}, u32[]{:S(2)}, u32[]{:S(2)}) %all-to-all-start.2) | async-done | bytes 524320 | tf_op jit(solution)/shard_map/all_to_all | solution.py:510
  126.4 0.0 copy-done.7
  126.4 1.6 shard_map.126
  127.9 9.2 %all-to-all-start.3 = ((f32[512,1,384]{2,1,0:T(1,128)}), f32[512,1,384]{2,1,0:T(1,128)S(1)}, u32[]{:S(2)}, u32[]{:S(2)}) async-start(f32[512,1,384]{2,1,0:T(1,128)} %bitcast.9), calls=%async_computation.3 | async-start | bytes 1572864 | tf_op jit(solution)/shard_map/all_to_all | solution.py:510
  137.1 0.0 copy-start.11
  137.2 0.2 select_reduce_fusion.3
  137.3 0.1 multiply_reduce_fusion
  137.4 0.1 add_select_fusion.2
  137.6 1.2 select_reduce_fusion
  138.9 25.9 %all-to-all-done.3 = f32[512,1,384]{2,1,0:T(1,128)S(1)} async-done(((f32[512,1,384]{2,1,0:T(1,128)}), f32[512,1,384]{2,1,0:T(1,128)S(1)}, u32[]{:S(2)}, u32[]{:S(2)}) %all-to-all-start.3) | async-done | bytes 786464 | tf_op jit(solution)/shard_map/all_to_all | solution.py:510
  164.8 0.0 copy-done.11
  164.8 1.3 shard_map.127
  (22 shorter events, 0.2 us)
Async XLA Ops:
  0.6 0.8 copy-start.10
  1.5 0.7 copy-start.12
  2.1 1.0 copy-start.14
  3.2 0.9 copy-start.15
  4.1 0.7 copy-start.16
  4.7 0.7 copy-start.17
  6.8 0.7 copy-start.8
  7.5 49.7 %all-to-all-start = ((f32[512,1,384]{2,1,0:T(1,128)}), f32[512,1,384]{2,1,0:T(1,128)S(1)}, u32[]{:S(2)}, u32[]{:S(2)}) async-start(f32[512,1,384]{2,1,0:T(1,128)} %bitcast.3), calls=%async_computation | async-start | bytes 1572864 | tf_op jit(solution)/shard_map/all_to_all | solution.py:510
  30.1 27.0 %copy-start.1 = (bf16[128,384]{1,0:T(8,128)(2,1)S(1)}, bf16[128,384]{1,0:T(8,128)(2,1)}, u32[]{:S(2)}) copy-start(bf16[128,384]{1,0:T(8,128)(2,1)} %constant.213.split) | copy-start | bytes 294916
  58.8 10.1 %copy-start.18 = (f32[31]{0:T(128)S(1)}, f32[31]{0:T(128)}, u32[]{:S(2)}) copy-start(f32[31]{0:T(128)} %param.17) | copy-start | bytes 376
  58.8 32.0 %all-to-all-start.1 = ((f32[512,2,128]{2,1,0:T(2,128)}), f32[512,2,128]{2,1,0:T(2,128)S(1)}, u32[]{:S(2)}, u32[]{:S(2)}) async-start(f32[512,2,128]{2,1,0:T(2,128)} %bitcast.5), calls=%async_computation.1 | async-start | bytes 1048576 | tf_op jit(solution)/shard_map/all_to_all | solution.py:510
  68.4 1.1 copy-start.2
  69.5 0.9 copy-start.9
  70.4 20.4 %copy-start = (bf16[128,384]{1,0:T(8,128)(2,1)S(1)}, bf16[128,384]{1,0:T(8,128)(2,1)}, u32[]{:S(2)}) copy-start(bf16[128,384]{1,0:T(8,128)(2,1)} %constant.218.mixed.refs_6_) | copy-start | bytes 294916
  74.0 0.7 copy-start.3
  74.7 0.7 copy-start.5
  90.8 1.0 copy-start.4
  91.7 0.9 copy-start.6
  94.6 9.4 %copy-start.13 = (f32[63]{0:T(128)S(1)}, f32[63]{0:T(128)}, u32[]{:S(2)}) copy-start(f32[63]{0:T(128)} %param.16) | copy-start | bytes 760
  94.6 31.7 %copy-start.7 = (bf16[512,128]{1,0:T(8,128)(2,1)S(1)}, bf16[512,128]{1,0:T(8,128)(2,1)}, u32[]{:S(2)}) copy-start(bf16[512,128]{1,0:T(8,128)(2,1)} %constant.219.refs_5_) | copy-start | bytes 393220
  94.6 31.7 %all-to-all-start.2 = ((f32[512,2,128]{2,1,0:T(2,128)}), f32[512,2,128]{2,1,0:T(2,128)S(1)}, u32[]{:S(2)}, u32[]{:S(2)}) async-start(f32[512,2,128]{2,1,0:T(2,128)} %bitcast.7), calls=%async_computation.2 | async-start | bytes 1048576 | tf_op jit(solution)/shard_map/all_to_all | solution.py:510
  127.9 36.9 %all-to-all-start.3 = ((f32[512,1,384]{2,1,0:T(1,128)}), f32[512,1,384]{2,1,0:T(1,128)S(1)}, u32[]{:S(2)}, u32[]{:S(2)}) async-start(f32[512,1,384]{2,1,0:T(1,128)} %bitcast.9), calls=%async_computation.3 | async-start | bytes 1572864 | tf_op jit(solution)/shard_map/all_to_all | solution.py:510
  137.1 27.7 %copy-start.11 = (s32[128,128]{1,0:T(8,128)S(1)}, s32[128,128]{1,0:T(8,128)}, u32[]{:S(2)}) copy-start(s32[128,128]{1,0:T(8,128)} %refs_1_.3) | copy-start | bytes 196612

commit v3 on v0

v3 whole, which is shorter than its diff:
```python
import functools
import math

import jax
import jax.numpy as jnp
import numpy as np
from jax import lax
from jax.experimental import pallas as pl
from jax.experimental.pallas import tpu as pltpu
from jax.sharding import PartitionSpec as P

NH, NA = 4096, 8192
PH, PA = 8, 64
ROWS = PH * PA
LANES = 128
BOT = 128
PART = 144
height_chirp = 1
azimuth_chirp = 3
INV = pow(azimuth_chirp, -1, 2 * NA)
HIGHEST = lax.Precision.HIGHEST
GRANT = 8 * 2**20
WIDE_GRANT = 60 * 2**20


def gauss(count, spread):
    index = np.arange(count, dtype=np.int64)
    return np.sum(np.exp(-1j * np.pi * ((spread * index * index) % (2 * count)) / count)) / count


GAIN = gauss(NH, height_chirp) * gauss(NA, azimuth_chirp)


def halves(value):
    high = value.astype(jnp.bfloat16)
    return high, (value - high.astype(jnp.float32)).astype(jnp.bfloat16)


def rounded_halves(value):
    high = lax.reduce_precision(value, 8, 7)
    return high.astype(jnp.bfloat16), (value - high).astype(jnp.bfloat16)


def matrix_left(value):
    high, low = rounded_halves(value)
    return jnp.concatenate([high, high, low], axis=1)


def matrix_right(value):
    high, low = rounded_halves(value)
    return jnp.concatenate([high, high, low], axis=0)


def data_left(value):
    high, low = halves(value)
    return jnp.concatenate([high, low, high], axis=1)


def data_right(value):
    high, low = halves(value)
    return jnp.concatenate([high, low, high], axis=0)


def product(left, right):
    return jnp.dot(left, right, preferred_element_type=jnp.float32)


def dot(left, right):
    return jnp.dot(left, right, precision=HIGHEST, preferred_element_type=jnp.float32)


def roots(count, spread):
    index = np.arange(count)
    return np.exp(-2j * np.pi * ((spread * np.outer(index, index)) % count) / count)


def row_matrix(spread):
    table = roots(PA, spread)
    whole = np.block([[table.real, -table.imag], [table.imag, table.real]]).astype(np.float32)
    return matrix_left(jnp.asarray(whole))


def lane_matrix(table):
    whole = np.block([[table.real, table.imag], [-table.imag, table.real]]).astype(np.float32)
    return matrix_right(jnp.asarray(whole))


def height_lanes():
    return lane_matrix(np.kron(roots(8, 1), np.eye(16)))


def azimuth_lanes():
    return lane_matrix(np.kron(np.eye(8), roots(16, INV)))


def tiles():
    table = np.zeros((LANES, 4, 8, 16), np.float32)
    for o in range(4):
        for k in range(16):
            table[16 * o + k, o, :, k] = 1.0
    return jnp.asarray(table.reshape(LANES, 4 * LANES)).astype(jnp.bfloat16)


def lane_of(shape):
    return lax.broadcasted_iota(jnp.int32, shape, len(shape) - 1)


def row_of(shape):
    return lax.broadcasted_iota(jnp.int32, shape, len(shape) - 2)


def cmul(ar, ai, br, bi):
    return ar * br - ai * bi, ar * bi + ai * br


def dft4(re, im):
    sr, si = re[0] + re[2], im[0] + im[2]
    dr, di = re[0] - re[2], im[0] - im[2]
    tr, ti = re[1] + re[3], im[1] + im[3]
    ur, ui = re[1] - re[3], im[1] - im[3]
    return [sr + tr, dr + ui, sr - tr, dr - ui], [si + ti, di - ur, si - ti, di + ur]


def dft8(re, im):
    half = math.sqrt(0.5)
    er, ei = dft4(re[0::2], im[0::2])
    pr, pi = dft4(re[1::2], im[1::2])
    tr = [pr[0], half * (pr[1] + pi[1]), pi[2], half * (pi[3] - pr[3])]
    ti = [pi[0], half * (pi[1] - pr[1]), -pr[2], -half * (pr[3] + pi[3])]
    out_re = [er[k] + tr[k] for k in range(4)] + [er[k] - tr[k] for k in range(4)]
    out_im = [ei[k] + ti[k] for k in range(4)] + [ei[k] - ti[k] for k in range(4)]
    return out_re, out_im


def dft8_azimuth(re, im):
    out_re, out_im = dft8(re, im)
    order = [(INV * k) % 8 for k in range(8)]
    return [out_re[k] for k in order], [out_im[k] for k in order]


def shift(value, amount):
    amount = amount % LANES
    return value if amount == 0 else pltpu.roll(value, amount, 1)


def trade(parts):
    group = lane_of(parts[0].shape) // 16
    parts = list(parts)
    for bit in (1, 2, 4):
        keep = (group & bit) == 0
        for a in range(8):
            if a & bit == 0:
                low, high = parts[a], parts[a | bit]
                parts[a] = jnp.where(keep, low, shift(high, 16 * bit))
                parts[a | bit] = jnp.where(keep, shift(low, -16 * bit), high)
    return parts


def row_dft(matrix, source, held):
    for i in range(0, 8, 2):
        pair = jnp.concatenate([source(i), source(i + 1)], axis=1)
        result = product(matrix[...], data_right(pair))
        held[i * 128 : (i + 1) * 128, :] = result[:, :LANES]
        held[(i + 1) * 128 : (i + 2) * 128, :] = result[:, LANES:]


def block_of(ref):
    return lambda i: ref[i * 128 : (i + 1) * 128, :]


def re_rows(i, low):
    return slice(i * 128 + low, i * 128 + low + 8)


def im_rows(i, low):
    return slice(i * 128 + 64 + low, i * 128 + 64 + low + 8)


def flat_rows(i, low):
    return slice(i * 64 + low, i * 64 + low + 8)


def pack_kernel(field, out):
    for c in range(2):
        for part in range(8):
            rows = [field.at[c][pl.ds(64 * part + g, 8, stride=8), :] for g in range(8)]
            for e, value in enumerate(trade(rows)):
                at = e * 128 + c * 64 + 8 * part
                out[at : at + 8, :] = value


def columns_kernel(
    place, got, chirp_re, chirp_im, outer_re, outer_im, inner_re, inner_im, last_re, last_im, split, lanes_dft,
    pick, terrain, out, work, held, mid,
):
    e = place[0]
    for group in range(8):
        low = 8 * group
        re, im = [], []
        for i in range(8):
            at = flat_rows(i, low)
            r, m = cmul(got[re_rows(i, low), :], got[im_rows(i, low), :], chirp_re[at, :], chirp_im[at, :])
            re.append(r)
            im.append(m)
        re, im = dft8(re, im)
        for i in range(8):
            at = flat_rows(i, low)
            r, m = cmul(re[i], im[i], outer_re[at, :], outer_im[at, :])
            work[re_rows(i, low), :] = r
            work[im_rows(i, low), :] = m
    row_dft(split, block_of(work), held)
    ir, ii = inner_re[...], inner_im[...]
    for i in range(8):
        at = slice(i * 64, i * 64 + 64)
        r, m = cmul(held[i * 128 : i * 128 + 64, :], held[i * 128 + 64 : i * 128 + 128, :], ir, ii)
        mid[at, :LANES] = r
        mid[at, LANES:] = m
    result = product(data_left(mid[...]), lanes_dft[...])
    r, m = cmul(result[:, :LANES], result[:, LANES:], last_re[...], last_im[...])
    out[pl.ds(0, ROWS, stride=3), :] = r
    out[pl.ds(1, ROWS, stride=3), :] = m
    lane8 = lane_of((8, LANES))
    picks = pltpu.roll(jnp.broadcast_to(pick[...].astype(jnp.float32), (8, LANES)), LANES - 16 * e, 1)
    lows = pltpu.roll(
        jnp.broadcast_to(terrain[...].astype(jnp.float32), (8, LANES)), lax.rem(LANES + 16 - 16 * e, LANES), 1
    )
    aux = jnp.where(lane8 < 16, picks, jnp.where(lane8 < 32, lows, 0.0))
    out[pl.ds(2, ROWS, stride=3), :] = jnp.broadcast_to(aux[None], (PA, 8, LANES)).reshape(ROWS, LANES)


def select_profile(picks, table):
    bits = picks.astype(jnp.int32)
    level = [table[p : p + 1, :] for p in range(16)]
    for bit in (1, 2, 4, 8):
        test = (bits & bit) != 0
        level = [jnp.where(test, level[k + 1], level[k]) for k in range(0, len(level), 2)]
    return level[0]


def rows_kernel(
    place, got, chirp_re, chirp_im, outer_re, outer_im, inner_re, inner_im, back_re, back_im, split, lanes_dft,
    tile, screen_re, screen_im, out, work, held, mid, picks, lows, low_strip,
):
    e, f = place[0], place[1]

    def chirped(i):
        at = slice(i * 64, i * 64 + 64)
        r, m = cmul(
            got[pl.ds(i * 192, 64, stride=3), :],
            got[pl.ds(i * 192 + 1, 64, stride=3), :],
            chirp_re[at, :],
            chirp_im[at, :],
        )
        return jnp.concatenate([r, m], axis=0)

    row_dft(split, chirped, held)
    for i in range(8):
        parts = [got[pl.ds(i * 192 + 2 + 3 * o, 16, stride=12), :] for o in range(4)]
        upright = jnp.concatenate(parts + parts, axis=0).T
        spread = product(upright[:32].astype(jnp.bfloat16), tile[...])
        for o in range(4):
            at = (i // 4 + 2 * o) * 64 + 16 * (i % 4)
            picks[at : at + 16, :] = spread[:16, o * LANES : (o + 1) * LANES]
            lows[at : at + 16, :] = spread[16:, o * LANES : (o + 1) * LANES]
    for group in range(8):
        low = 8 * group
        re, im = [], []
        for i in range(8):
            at = flat_rows(i, low)
            r, m = cmul(held[re_rows(i, low), :], held[im_rows(i, low), :], outer_re[at, :], outer_im[at, :])
            re.append(r)
            im.append(m)
        re, im = dft8_azimuth(re, im)
        for i in range(8):
            r, m = cmul(re[i], im[i], inner_re[i : i + 1, :], inner_im[i : i + 1, :])
            mid[flat_rows(i, low), :LANES] = r
            mid[flat_rows(i, low), LANES:] = m
    result = product(data_left(mid[...]), lanes_dft[...])
    lane8 = lane_of((8, LANES))
    height = (e + 8 * f + 512 * (lane8 // 16)).astype(jnp.float32)
    for n in range(0, ROWS, 8):
        at = slice(n, n + 8)
        above = height >= lows[at, :]
        sr = jnp.where(above, select_profile(picks[at, :], screen_re), 0.0)
        si = jnp.where(above, select_profile(picks[at, :], screen_im), 0.0)
        br, bi = back_re[at, :], back_im[at, :]
        r, m = cmul(sr, si, br, bi)
        r, m = cmul(result[at, :LANES], result[at, LANES:], r, m)
        low_strip[at, :] = jnp.where(lane8 < 16, r, shift(m, 16))
        r, m = cmul(r, m, br, bi)
        mid[at, :LANES] = r
        mid[at, LANES:] = m
    result = product(data_left(mid[...]), lanes_dft[...])
    for group in range(8):
        low = 8 * group
        re, im = [], []
        for i in range(8):
            at = flat_rows(i, low)
            r, m = cmul(result[at, :LANES], result[at, LANES:], inner_re[i : i + 1, :], inner_im[i : i + 1, :])
            re.append(r)
            im.append(m)
        re, im = dft8_azimuth(re, im)
        for i in range(8):
            at = flat_rows(i, low)
            r, m = cmul(re[i], im[i], outer_re[at, :], outer_im[at, :])
            work[re_rows(i, low), :] = r
            work[im_rows(i, low), :] = m
    row_dft(split, block_of(work), held)
    for i in range(8):
        at = slice(i * 64, i * 64 + 64)
        r, m = cmul(
            held[i * 128 : i * 128 + 64, :], held[i * 128 + 64 : i * 128 + 128, :], chirp_re[at, :], chirp_im[at, :]
        )
        out[pl.ds(i * 192, 64, stride=3), :] = r
        out[pl.ds(i * 192 + 1, 64, stride=3), :] = m
    lane16 = lane_of((16, LANES))
    for i in range(8):
        block = low_strip[i * 64 : i * 64 + 64, :]
        upright = jnp.concatenate([block, block], axis=0).T
        for part in range(4):
            re = shift(upright[:16], -16 * part)
            im = shift(upright[16:32], 16 - 16 * part)
            to = 4 * (i % 2) + part
            out[pl.ds(to * 192 + 2 + 3 * (i // 2), 16, stride=12), :] = jnp.where(
                lane16 < 16, re, jnp.where(lane16 < 32, im, 0.0)
            )


def final_kernel(
    got, chirp_re, chirp_im, outer_re, outer_im, inner_re, inner_im, coef_re, coef_im, split, lanes_dft,
    seen, range_pair, out, work, held, mid,
):
    for i in range(8):
        at = slice(i * 64, i * 64 + 64)
        r, m = cmul(
            got[pl.ds(i * 192, 64, stride=3), :],
            got[pl.ds(i * 192 + 1, 64, stride=3), :],
            chirp_re[at, :],
            chirp_im[at, :],
        )
        mid[at, :LANES] = r
        mid[at, LANES:] = m
    result = product(data_left(mid[...]), lanes_dft[...])
    ir, ii = inner_re[...], inner_im[...]
    for i in range(8):
        at = slice(i * 64, i * 64 + 64)
        r, m = cmul(result[at, :LANES], result[at, LANES:], ir, ii)
        work[i * 128 : i * 128 + 64, :] = r
        work[i * 128 + 64 : i * 128 + 128, :] = m
    row_dft(split, block_of(work), held)
    strip_re, strip_im = [], []
    for group in range(8):
        low = 8 * group
        re, im = [], []
        for i in range(8):
            at = flat_rows(i, low)
            r, m = cmul(held[re_rows(i, low), :], held[im_rows(i, low), :], outer_re[at, :], outer_im[at, :])
            re.append(r)
            im.append(m)
        re, im = dft8(re, im)
        for i in range(8):
            at = flat_rows(i, low)
            r, m = cmul(re[i], im[i], coef_re[at, :], coef_im[at, :])
            out[i * PART + low : i * PART + low + 8, :] = r
            out[i * PART + 64 + low : i * PART + 64 + low + 8, :] = m
            if i == 0 and group < 2:
                strip_re.append(r)
                strip_im.append(m)
    lane16 = lane_of((16, LANES))
    first_re = jnp.zeros((16, LANES), jnp.float32)
    first_im = jnp.zeros((16, LANES), jnp.float32)
    for i in range(8):
        aux = got[pl.ds(i * 192 + 2, 16, stride=3), :]
        here = lane16 // 16 == i
        first_re = jnp.where(here, shift(aux, 16 * i), first_re)
        first_im = jnp.where(here, shift(aux, 16 * i - 16), first_im)
    parts = [(first_re, first_im), (jnp.concatenate(strip_re, axis=0), jnp.concatenate(strip_im, axis=0))]
    power = [seen[...] * (re * re + im * im) for re, im in parts]
    tall = []
    for g in range(8):
        second = jnp.where(lane16 < 32, shift(power[1], 16 - 16 * g), 0.0)
        tall.append(jnp.where(lane16 < 16, shift(power[0], -16 * g), second))
    ranged = product(range_pair[...], data_right(jnp.concatenate(tall, axis=0)))
    for s in range(2):
        spread = jnp.zeros((16, LANES), jnp.float32)
        for g in range(8):
            moved = shift(ranged[16 * g : 16 * g + 16, :], 16 * g - 16 * s)
            spread = jnp.where(lane16 // 16 == g, moved, spread)
        for n, value in enumerate((spread, *parts[s])):
            for i in range(8):
                at = i * PART + 128 + 2 * (3 * s + n)
                out[at : at + 2, :] = value[2 * i : 2 * i + 2, :]
    for i in range(8):
        out[i * PART + 140 : i * PART + 144, :] = jnp.zeros((4, LANES), jnp.float32)


def strips_kernel(got, measured, edges, strips, rows):
    parts = [got[e * PART + 128 : e * PART + 144, :] for e in range(8)]
    for g, value in enumerate(trade(parts)):
        rows[pl.ds(g, 16, stride=8), :] = value
    for s in range(2):
        edges[16 * s : 16 * s + 16, :] = rows[48 * s : 48 * s + 16, :]
        edges[32 + 16 * s : 48 + 16 * s, :] = measured[s]
        strips[32 * s : 32 * s + 32, :] = rows[48 * s + 16 : 48 * s + 48, :]


def unpack_kernel(got, field_out):
    for c in range(2):
        for part in range(8):
            at = c * 64 + 8 * part
            values = trade([got[e * PART + at : e * PART + at + 8, :] for e in range(8)])
            for g, value in enumerate(values):
                field_out.at[c][pl.ds(64 * part + g, 8, stride=8), :] = value


def sources_kernel(place, left, own, right, strips, mask, beams, sources):
    near = jnp.concatenate([left[:32, :], own[:32, :], right[:32, :]], axis=1)
    far = jnp.concatenate([left[32:, :], own[32:, :], right[32:, :]], axis=1)
    back = product(data_left(jnp.concatenate([near, far], axis=1)), beams[...])
    seen = mask[pl.ds(pl.multiple_of(16 * place[0], 16), 16), :].astype(jnp.float32)
    for s in range(2):
        for c in range(2):
            at = 32 * s + 16 * c
            sources[s, c] = 2.0 * seen * strips[at : at + 16, :] * back[16 * s : 16 * s + 16, :]


def prepare_kernel(
    place, profile, pick, terrain, mask, chirp_re, chirp_im, screen_re, screen_im, coef_re, coef_im, seen, turned,
):
    e, f = place[0], place[1]
    lane16 = lane_of((16, LANES))
    group = lane16 // 16
    wide = lane_of((16, 512))
    phase = jnp.zeros((16, LANES), jnp.float32)
    for g in range(8):
        chosen = jnp.where(wide == e + 8 * f, profile[:, 512 * g : 512 * (g + 1)], 0.0)
        phase = jnp.where(group == g, jnp.sum(chosen, axis=1, keepdims=True), phase)

    def screen(height, angle):
        depth = jnp.maximum(height.astype(jnp.float32) - 0.75 * NH, 0.0) / (0.25 * NH)
        amount = abs(GAIN) * jnp.exp(-4.0 * depth * depth)
        turn = angle + float(np.angle(GAIN))
        return amount * jnp.cos(turn), amount * jnp.sin(turn)

    sr, si = screen(e + 8 * f + 512 * group, phase)
    screen_re[...] = sr
    screen_im[...] = si
    picks = jnp.zeros((8, LANES), jnp.float32)
    lows = jnp.zeros((8, LANES), jnp.float32)
    masks = jnp.zeros((16, LANES), jnp.float32)
    group8 = lane_of((8, LANES)) // 16
    wide_pick = jnp.broadcast_to(pick[...].astype(jnp.float32), (8, LANES))
    wide_low = jnp.broadcast_to(terrain[...].astype(jnp.float32), (8, LANES))
    for g in range(8):
        amount = lax.rem(LANES + 16 * g - 16 * e, LANES)
        picks = jnp.where(group8 == g, pltpu.roll(wide_pick, amount, 1), picks)
        lows = jnp.where(group8 == g, pltpu.roll(wide_low, amount, 1), lows)
        part = mask[pl.ds(g, 16, stride=8), :].astype(jnp.float32)
        masks = jnp.where(group == g, pltpu.roll(part, amount, 1), masks)
    seen[...] = masks
    square_row = row_of((LANES, LANES))
    square_lane = lane_of((LANES, LANES))
    wanted = jnp.broadcast_to(picks[0:1, :], (LANES, LANES))
    match = ((square_row % 16).astype(jnp.float32) == wanted) & (square_row // 16 == square_lane // 16)
    onehot = jnp.where(match, 1.0, 0.0)
    for n in range(NH // LANES):
        block = profile[:, LANES * n : LANES * (n + 1)]
        turned[LANES * n : LANES * (n + 1), :] = jnp.concatenate([block] * 8, axis=0).T
    lanes = lane_of((64, LANES))
    rows = row_of((64, LANES))
    for i in range(8):
        mixed = jnp.zeros((64, LANES), jnp.float32)
        for g in range(8):
            mixed = jnp.where(lanes // 16 == g, turned[pl.ds(512 * i + g, 64, stride=8), :], mixed)
        height = 512 * i + 8 * rows + lanes // 16
        sr, si = screen(height, dot(mixed, onehot))
        above = height.astype(jnp.float32) >= jnp.broadcast_to(lows[0:1, :], (64, LANES))
        at = slice(i * 64, i * 64 + 64)
        r, m = cmul(jnp.where(above, sr, 0.0), jnp.where(above, si, 0.0), chirp_re[at, :], chirp_im[at, :])
        coef_re[at, :] = r
        coef_im[at, :] = m


def turns(steps, modulus):
    angle = (steps % modulus).astype(jnp.float32) * (2.0 * math.pi / modulus)
    return jnp.cos(angle), jnp.sin(angle)


def layout_tables():
    row = lax.broadcasted_iota(jnp.int32, (ROWS, LANES), 0)
    lane = lax.broadcasted_iota(jnp.int32, (ROWS, LANES), 1)
    i, j, g, t = row // PA, row % PA, lane // 16, lane % 16
    square_row = lax.broadcasted_iota(jnp.int32, (PA, LANES), 0)
    group = lax.broadcasted_iota(jnp.int32, (PA, LANES), 1) // 16
    block = lax.broadcasted_iota(jnp.int32, (8, LANES), 0)
    inside = lax.broadcasted_iota(jnp.int32, (8, LANES), 1) % 16
    heights = (
        turns(64 * j * j + g * g + 1024 * i * g + 16 * j * g, 2 * NH),
        turns(-i * (8 * j + g), NH),
        turns(-square_row * group, 512),
        turns(i * i + 64 * j * j + 16 * i * j + 1024 * i * g, 2 * NH),
    )
    natural = (256 * i * i + t * t + 4096 * i * j + 256 * j * t + 32 * i * t) % (2 * NA)
    reverse = (j * j + 4096 * i * i + 128 * i * j + 1024 * j * t) % (2 * NA)
    azimuths = (
        turns(INV * natural, 2 * NA),
        turns(-(INV % NA) * (j * (16 * i + t)), NA),
        turns(-(INV % 128) * block * inside, 128),
        turns(INV * reverse, 2 * NA),
    )
    return heights, azimuths


def band(taps, offset):
    hit = offset[..., None] == lax.broadcasted_iota(jnp.int32, (1,) * offset.ndim + (taps.shape[0],), offset.ndim)
    return jnp.sum(jnp.where(hit, taps, 0.0), axis=-1)


def clutter_tables(pulse, beam, measured, eh):
    half = (pulse.shape[0] - 1) // 2
    row = lax.broadcasted_iota(jnp.int32, (BOT, BOT), 0)
    col = lax.broadcasted_iota(jnp.int32, (BOT, BOT), 1)
    adjoint = band(pulse, row - col + half)
    moved = adjoint.reshape(16, 8, BOT).swapaxes(0, 1).reshape(BOT, BOT)
    range_pair = jnp.einsum("ir,hr->ih", moved, moved, precision=HIGHEST)
    own = lax.dynamic_slice_in_dim(adjoint, 16 * eh, 16, 0)
    turned = jnp.einsum("hr,sra->sha", own, measured, precision=HIGHEST)
    taps = beam.shape[0]
    reach = (taps - 1) // 2
    at = lax.broadcasted_iota(jnp.int32, (3 * LANES, LANES), 0) - LANES
    col = lax.broadcasted_iota(jnp.int32, (3 * LANES, LANES), 1)
    first = lax.broadcasted_iota(jnp.int32, (taps, 2 * taps - 1), 0)
    ahead = lax.broadcasted_iota(jnp.int32, (taps, 2 * taps - 1), 1) - (taps - 1)
    auto = jnp.sum(beam[:, None] * band(beam, first + ahead), axis=0)
    pair = band(auto, at - col + taps - 1)
    back = band(beam, col - at + reach)
    return matrix_left(range_pair), turned, matrix_right(jnp.concatenate([pair, -back], axis=0))


VMEM = pl.BlockSpec(memory_space=pltpu.VMEM)
SMEM = pl.BlockSpec(memory_space=pltpu.SMEM)


def f32(*shape):
    return jax.ShapeDtypeStruct(shape, jnp.float32)


def placed(kernel, *refs):
    return kernel((lax.axis_index("ha"), lax.axis_index("az")), *refs)


def call(kernel, outs, scratch, args, place=None, cost=2_000_000, grant=GRANT, interpret=False):
    specs = [VMEM] * len(args)
    if place == "here":
        kernel = functools.partial(placed, kernel)
    elif place is not None:
        specs, args = [SMEM] + specs, (place, *args)
    return pl.pallas_call(
        kernel,
        out_shape=outs,
        in_specs=specs,
        out_specs=jax.tree.map(lambda _: VMEM, outs),
        scratch_shapes=[pltpu.VMEM(shape, jnp.float32) for shape in scratch],
        cost_estimate=pl.CostEstimate(flops=cost * 100, bytes_accessed=cost, transcendentals=0),
        compiler_params=pltpu.CompilerParams(vmem_limit_bytes=grant),
        interpret=interpret,
    )(*args)


WORK = [(2 * ROWS, LANES), (2 * ROWS, LANES), (ROWS, 2 * LANES)]


def stage_pack(field, **kw):
    return call(pack_kernel, f32(2 * ROWS, LANES), [], (field,), grant=WIDE_GRANT, **kw)


def stage_columns(place, got, heights, pick, terrain, **kw):
    chirp, outer, inner, last = heights
    args = (got, *chirp, *outer, *inner, *last, row_matrix(1), height_lanes(), pick[None], terrain[None])
    return call(columns_kernel, f32(3 * ROWS, LANES), WORK, args, place, **kw)


def stage_rows(place, got, azimuths, screen, **kw):
    chirp, outer, inner, back = azimuths
    args = (got, *chirp, *outer, *inner, *back, row_matrix(INV), azimuth_lanes(), tiles(), *screen)
    return call(rows_kernel, f32(3 * ROWS, LANES), WORK + [(ROWS, LANES)] * 3, args, place, **kw)


def stage_final(got, heights, coef, seen, range_pair, **kw):
    _, outer, inner, chirp = heights
    args = (got, *chirp, *outer, *inner, *coef, row_matrix(1), height_lanes(), seen, range_pair)
    return call(final_kernel, f32(8 * PART, LANES), WORK, args, **kw)


def stage_strips(got, turned, **kw):
    return call(strips_kernel, (f32(64, LANES), f32(64, LANES)), [(BOT, LANES)], (got, turned), **kw)


def stage_unpack(got, **kw):
    return call(unpack_kernel, f32(2, NH // PH, LANES), [], (got,), **kw)


def stage_sources(place, left, own, right, strips, mask, beams, **kw):
    return call(sources_kernel, f32(2, 2, 16, LANES), [], (left, own, right, strips, mask, beams), place, **kw)


def stage_prepare(place, profile, pick, terrain, mask, heights, **kw):
    outs = (f32(16, LANES), f32(16, LANES), f32(ROWS, LANES), f32(ROWS, LANES), f32(16, LANES))
    args = (profile, pick[None], terrain[None], mask, *heights[0])
    return call(prepare_kernel, outs, [(NH, LANES)], args, place, **kw)


def swap_all(rows):
    shaped = rows.reshape(ROWS, 1, 3 * LANES)
    moved = lax.all_to_all(shaped, ("ha", "az"), split_axis=0, concat_axis=0, tiled=True)
    return moved.reshape(rows.shape)


def swap_heights(rows):
    shaped = rows.reshape(PH, rows.shape[0] // PH, LANES)
    return lax.all_to_all(shaped, "ha", split_axis=0, concat_axis=0, tiled=True).reshape(rows.shape)


def local(field, terrain, profile_pick, profile_table, clutter_mask, pulse, beam, measured):
    place = "here"
    range_pair, turned, beams = clutter_tables(pulse, beam, measured, lax.axis_index("ha"))
    heights, azimuths = layout_tables()
    got = swap_heights(stage_pack(field))
    got = swap_all(stage_columns(place, got, heights, profile_pick, terrain))
    prepared = stage_prepare(place, profile_table, profile_pick, terrain, clutter_mask, heights)
    got = swap_all(stage_rows(place, got, azimuths, prepared[0:2]))
    got = swap_heights(stage_final(got, heights, prepared[2:4], prepared[4], range_pair))
    edges, strips = stage_strips(got, turned)
    left = lax.ppermute(edges, "az", [(i, (i + 1) % PA) for i in range(PA)])
    right = lax.ppermute(edges, "az", [((i + 1) % PA, i) for i in range(PA)])
    field_out = stage_unpack(got)
    return field_out, stage_sources(place, left, edges, right, strips, clutter_mask, beams)


def solution(mesh):
    return jax.shard_map(
        local,
        mesh=mesh,
        in_specs=(
            P(None, "ha", "az"),
            P("az"),
            P("az"),
            P(),
            P(None, "az"),
            P(),
            P(),
            P(None, None, "az"),
        ),
        out_specs=(P(None, "ha", "az"), P(None, None, "ha", "az")),
        check_vma=False,
    )
```

time: 522 us -> 162 us (0.31); the launches traced: 512 us -> 162 us
  local copies, waits for them, and re-layouts: 146 us -> 12.5 us
  blocking collectives: 101 us -> 0 us
  waiting for transfers between devices: 123 us -> 65.4 us
  starting transfers between devices: 89.8 us -> 54.5 us
  matrix products: 20.1 us -> 0.43 us
  Pallas kernels: 0 us -> 15.4 us
  between operations: 15.5 us -> 1.02 us
    all_to_all x4 -> x0, blocking collectives: 101 us -> none  [the longest x2 51.3 us: rows_to_slab(): return lax.all_to_all(rows, 'az', split_axis=2, concat_axis=1, tiled=True)]
    unnamed x26 -> x68, local copies, waits for them, and re-layouts: 85.3 us -> 12.5 us
    psum x1 -> x0, waiting for transfers between devices: 65.5 us -> none  [broadcast(): return lax.psum(block, axis)]
    ppermute x8 -> x2, starting transfers between devices: 53.7 us -> 13.4 us  [the longest x1 10.1 us: local(): right = lax.ppermute(edges, 'az', [((i + 1) % PA, i) for i in range(PA)])]
    all_to_all x11 -> x0, local copies, waits for them, and re-layouts: 30.1 us -> none  [the longest x3 18.8 us: rows_to_slab(): return lax.all_to_all(rows, 'az', split_axis=2, concat_axis=1, tiled=True)]
    another operation x14 -> x0, local copies, waits for them, and re-layouts: 25.5 us -> none  [the longest x2 15.4 us: turn_rows(): return jnp.stack([new_re, new_im])]
    dot_general x25 -> x2, matrix products: 20.1 us -> 0.43 us  [the longest x1 0.27 us: clutter_tables(): range_pair = jnp.einsum('ir,hr->ih', moved, moved, precision=HIGHEST)]
    pallas_call x0 -> x8, Pallas kernels: none -> 15.4 us  [call(): pl.pallas_call(kernel, out_shape=outs, in_specs=specs, out_specs=jax.tree...]
  transfers between devices with their start and end apart: 13 -> 6, of which waited for: 5 -> 4; matrix products, arithmetic and copies ran while one was open for 1% -> 8% of each run, Pallas kernels for 0% -> 3%
where the time goes in v3:
time: 162 us
  waiting for transfers between devices  65.4 us (40%)
  starting transfers between devices  54.5 us (34%)
  Pallas kernels  15.4 us (10%)
  local copies, waits for them, and re-layouts  12.5 us (8%)
  other arithmetic  12.2 us (8%)
    all_to_all x2, waiting for transfers between devices, swap_all(): lax.all_to_all(shaped, ('ha', 'az'), split_axis=0, concat_axis=0, tiled=T...  45.7 us
    all_to_all x2, starting transfers between devices, swap_all(): lax.all_to_all(shaped, ('ha', 'az'), split_axis=0, concat_axis=0, tiled=T...  26 us
    all_to_all x2, waiting for transfers between devices, swap_heights(): lax.all_to_all(shaped, 'ha', split_axis=0, concat_axis=0, tiled=True)  19.7 us
    pallas_call x8, Pallas kernels, call(): pl.pallas_call(kernel, out_shape=outs, in_specs=specs, out_specs=jax.tree...  15.4 us
    all_to_all x2, starting transfers between devices, swap_heights(): lax.all_to_all(shaped, 'ha', split_axis=0, concat_axis=0, tiled=True)  15.1 us
    unnamed x68, local copies, waits for them, and re-layouts  12.5 us
    ppermute x1, starting transfers between devices, local(): right = lax.ppermute(edges, 'az', [((i + 1) % PA, i) for i in range(PA)])  10.1 us
    sin x3, other arithmetic, turns(): return (jnp.cos(angle), jnp.sin(angle))  8.51 us
  transfers between devices with their start and end apart: 6, of which 4 were waited for; matrix products, arithmetic and copies ran while one was open for 8% of the time, Pallas kernels for 3%

profile of v3, /device:TPU:1, one launch (start us, length us, event | category | flops | bytes accessed | tf_op | source)
XLA Modules:
  0.0 161.5 jit_solution(15961349710219480338)
XLA Ops:
  0.6 0.0 copy-start
  0.6 3.3 %shard_map.158 = f32[1024,128]{1,0:T(8,128)} custom-call(f32[2,512,128]{2,1,0:T(8,128)} %field.1), custom_call_target="tpu_custom_call" | custom-call | flops 200000000 | bytes 2000000 | tf_op jit(solution)/shard_map/pallas_call | solution.py:558
  4.0 10.2 %all-to-all-start = ((f32[8,128,128]{2,1,0:T(8,128)}), f32[8,128,128]{2,1,0:T(8,128)S(1)}, u32[]{:S(2)}, u32[]{:S(2)}) async-start(f32[8,128,128]{2,1,0:T(8,128)} %bitcast.31), calls=%async_computation | async-start | bytes 1048576 | tf_op jit(solution)/shard_map/all_to_all | solution.py:621
  14.2 0.0 copy-start.27
  14.3 0.2 fusion.54
  14.5 0.0 copy-start.8
  14.6 0.0 copy-start.1
  14.6 0.0 copy-start.6
  14.6 0.0 copy-start.21
  14.6 0.0 copy-start.23
  14.6 8.2 %fusion.38 = (f32[512,128]{1,0:T(8,128)S(1)}, f32[512,128]{1,0:T(8,128)S(1)}, f32[512,128]{1,0:T(8,128)}, f32[512,128]{1,0:T(8,128)}, f32[512,128]{1,0:T(8,128)}...) fusion(s32[128]{0:T(128)S(1)} %get-tuple-element.53, ...), kind=kLoop, calls=%fused_computation.107 | loop fusion | flops 9895936 | bytes 3157248 | tf_op jit(solution)/shard_map/sin | solution.py:486
  22.8 0.0 copy-done.27
  22.8 5.8 %all-to-all-done = f32[8,128,128]{2,1,0:T(8,128)S(1)} async-done(((f32[8,128,128]{2,1,0:T(8,128)}), f32[8,128,128]{2,1,0:T(8,128)S(1)}, u32[]{:S(2)}, u32[]{:S(2)}) %all-to-all-start) | async-done | bytes 524320 | tf_op jit(solution)/shard_map/all_to_all | solution.py:621
  28.6 0.0 copy-done.1
  28.6 1.7 %shard_map.159 = f32[1536,128]{1,0:T(8,128)} custom-call(f32[1024,128]{1,0:T(8,128)S(1)} %bitcast.26, f32[512,128]{1,0:T(8,128)S(1)} %get-tuple-element.32.refs_1_.refs_4_, f32[512,128]{1,0:T(8,128)S(1)} %get-tuple-element.36.refs_2_.refs_5_, f32[512,128]{1,0:T(8,128)S(1)} %get-tuple-element.34.refs_3_.outer_re, ...), custom_call_target="tpu_custom_call" | custom-call | flops 200000000 | bytes 2000000 | tf_op jit(solution)/shard_map/pallas_call | solution.py:558
  30.3 16.3 %all-to-all-start.1 = ((f32[512,1,384]{2,1,0:T(1,128)}), f32[512,1,384]{2,1,0:T(1,128)S(1)}, u32[]{:S(2)}, u32[]{:S(2)}) async-start(f32[512,1,384]{2,1,0:T(1,128)} %bitcast.4), calls=%async_computation.1 | async-start | bytes 1572864 | tf_op jit(solution)/shard_map/all_to_all | solution.py:615
  46.6 0.0 copy-start.14
  46.6 0.9 copy-done.14
  47.6 0.8 copy-done.15
  48.4 0.7 copy-done.22
  49.1 0.7 copy-done.24
  49.7 1.9 %shard_map.160 = (f32[16,128]{1,0:T(8,128)S(1)}, f32[16,128]{1,0:T(8,128)S(1)}, f32[512,128]{1,0:T(8,128)S(1)}, f32[512,128]{1,0:T(8,128)S(1)}, f32[16,128]{1,0:T(8,128)S(1)}) custom-call(f32[16,4096]{1,0:T(8,128)S(1)} %copy-done.14, s32[1,128]{1,0:T(1,128)S(1)} %bitcast.28, s32[1,128]{1,0:T(1,128)S(1)} %bitcast.30, s32[128,128]{1,0:T(8,128)S(1)} %copy-done.15, ...), custom_call_target="tpu_custom_call" | custom-call | flops 200000000 | bytes 2000000 | tf_op jit(solution)/shard_map/pallas_call | solution.py:558
  51.6 0.0 copy-start.10
  51.7 0.7 copy-done.10
  52.4 0.7 copy-done.12
  53.0 0.6 copy-done.19
  53.6 0.0 copy-done.28
  53.6 0.0 copy-done.32
  53.6 0.1 fusion.61
  53.8 20.4 %all-to-all-done.1 = f32[512,1,384]{2,1,0:T(1,128)S(1)} async-done(((f32[512,1,384]{2,1,0:T(1,128)}), f32[512,1,384]{2,1,0:T(1,128)S(1)}, u32[]{:S(2)}, u32[]{:S(2)}) %all-to-all-start.1) | async-done | bytes 786464 | tf_op jit(solution)/shard_map/all_to_all | solution.py:615
  74.1 0.9 copy-done.2
  75.1 0.9 copy-done.3
  76.0 0.9 copy-done.4
  77.0 0.9 copy-done.5
  77.9 1.0 copy-done.7
  78.9 0.9 copy-done.17
  79.8 0.9 copy-done.18
  80.7 0.7 copy-done.20
  81.4 3.1 %shard_map.161 = f32[1536,128]{1,0:T(8,128)} custom-call(f32[1536,128]{1,0:T(8,128)S(1)} %bitcast.23, f32[512,128]{1,0:T(8,128)S(1)} %copy-done.3, f32[512,128]{1,0:T(8,128)S(1)} %copy-done.4, f32[512,128]{1,0:T(8,128)S(1)} %copy-done.2, f32[512,128]{1,0:T(8,128)S(1)} %copy-done.5, f32[8,128]{1,0:T(8,128)S(1)} %get-tuple-element.41.refs_5_, ...), custom_call_target="tpu_custom_call" | custom-call | flops 200000000 | bytes 2000000 | tf_op jit(solution)/shard_map/pallas_call | solution.py:558
  84.5 9.8 %all-to-all-start.2 = ((f32[512,1,384]{2,1,0:T(1,128)}), f32[512,1,384]{2,1,0:T(1,128)S(1)}, u32[]{:S(2)}, u32[]{:S(2)}) async-start(f32[512,1,384]{2,1,0:T(1,128)} %bitcast.6), calls=%async_computation.2 | async-start | bytes 1572864 | tf_op jit(solution)/shard_map/all_to_all | solution.py:615
  94.3 0.0 copy-start.26
  94.3 0.0 copy-start.9
  94.3 0.0 copy-start.11
  94.4 0.5 select_reduce_fusion.2
  94.9 0.3 reduce-precision_convert_fusion.1
  95.2 0.1 subtract_add_fusion.1
  95.3 1.3 select_reduce_fusion.1
  96.6 25.3 %all-to-all-done.2 = f32[512,1,384]{2,1,0:T(1,128)S(1)} async-done(((f32[512,1,384]{2,1,0:T(1,128)}), f32[512,1,384]{2,1,0:T(1,128)S(1)}, u32[]{:S(2)}, u32[]{:S(2)}) %all-to-all-start.2) | async-done | bytes 786464 | tf_op jit(solution)/shard_map/all_to_all | solution.py:615
  122.0 2.0 %shard_map.162 = f32[1152,128]{1,0:T(8,128)} custom-call(f32[1536,128]{1,0:T(8,128)S(1)} %bitcast.22, f32[512,128]{1,0:T(8,128)S(1)} %get-tuple-element.33.refs_7_.chirp_re, f32[512,128]{1,0:T(8,128)S(1)} %get-tuple-element.37.refs_8_.chirp_im, f32[512,128]{1,0:T(8,128)S(1)} %get-tuple-element.34.refs_3_.outer_re, ...), custom_call_target="tpu_custom_call" | custom-call | flops 200000000 | bytes 2000000 | tf_op jit(solution)/shard_map/pallas_call | solution.py:558
  124.0 4.8 %all-to-all-start.3 = ((f32[8,144,128]{2,1,0:T(8,128)}), f32[8,144,128]{2,1,0:T(8,128)S(1)}, u32[]{:S(2)}, u32[]{:S(2)}) async-start(f32[8,144,128]{2,1,0:T(8,128)} %bitcast.11), calls=%async_computation.3 | async-start | bytes 1179648 | tf_op jit(solution)/shard_map/all_to_all | solution.py:621
  128.9 0.2 select_reduce_fusion.3
  129.0 0.1 multiply_reduce_fusion
  129.1 1.3 select_reduce_fusion
  130.4 0.1 reduce-precision_convert_fusion
  130.5 0.2 convolution_bitcast_fusion.measured
  130.7 13.9 %all-to-all-done.3 = f32[8,144,128]{2,1,0:T(8,128)S(1)} async-done(((f32[8,144,128]{2,1,0:T(8,128)}), f32[8,144,128]{2,1,0:T(8,128)S(1)}, u32[]{:S(2)}, u32[]{:S(2)}) %all-to-all-start.3) | async-done | bytes 589856 | tf_op jit(solution)/shard_map/all_to_all | solution.py:621
  144.6 0.2 shard_map.164
  144.9 3.4 %collective-permute-start = (f32[64,128]{1,0:T(8,128)S(1)}, f32[64,128]{1,0:T(8,128)S(1)}, u32[]{:S(2)}, u32[]{:S(2)}) collective-permute-start(f32[64,128]{1,0:T(8,128)S(1)} %get-tuple-element.14.refs_1_), channel_id=1, source_target_pairs={{0,1},{1,2},{2,3},{3,4},{4,5},{5,6},{6,7},{7,8},{8,9},{9,10},{10,1... | collective-permute-start | bytes 98312 | tf_op jit(solution)/shard_map/ppermute | solution.py:634
  148.2 10.1 %collective-permute-start.1 = (f32[64,128]{1,0:T(8,128)S(1)}, f32[64,128]{1,0:T(8,128)S(1)}, u32[]{:S(2)}, u32[]{:S(2)}) collective-permute-start(f32[64,128]{1,0:T(8,128)S(1)} %get-tuple-element.14.refs_1_), channel_id=1, source_target_pairs={{1,0},{2,1},{3,2},{4,3},{5,4},{6,5},{7,6},{8,7},{9,8},{10,9},{11,1... | collective-permute-start | bytes 98312 | tf_op jit(solution)/shard_map/ppermute | solution.py:635
  158.3 0.0 copy-start.16
  158.3 2.3 %shard_map.163 = f32[2,512,128]{2,1,0:T(8,128)} custom-call(f32[1152,128]{1,0:T(8,128)S(1)} %bitcast.25), custom_call_target="tpu_custom_call" | custom-call | flops 200000000 | bytes 2000000 | tf_op jit(solution)/shard_map/pallas_call | solution.py:558
  160.7 0.0 collective-permute-done.refs_0_
  160.7 0.0 collective-permute-done.1.refs_2_
  160.7 0.8 shard_map.165
  (52 shorter events, 0.2 us)
Async XLA Ops:
  0.6 129.9 %copy-start = (f32[2,128,128]{2,1,0:T(8,128)S(1)}, f32[2,128,128]{2,1,0:T(8,128)}, u32[]{:S(2)}) copy-start(f32[2,128,128]{2,1,0:T(8,128)} %param.22) | copy-start | bytes 393220
  4.0 24.6 %all-to-all-start = ((f32[8,128,128]{2,1,0:T(8,128)}), f32[8,128,128]{2,1,0:T(8,128)S(1)}, u32[]{:S(2)}, u32[]{:S(2)}) async-start(f32[8,128,128]{2,1,0:T(8,128)} %bitcast.31), calls=%async_computation | async-start | bytes 1048576 | tf_op jit(solution)/shard_map/all_to_all | solution.py:621
  14.2 8.6 %copy-start.27 = (pred[128]{0:T(512)(128)(4,1)}, pred[128]{0:T(512)(128)(4,1)S(1)}, u32[]{:S(2)}) copy-start(pred[128]{0:T(512)(128)(4,1)S(1)} %get-tuple-element.50) | copy-start | bytes 388
  14.2 8.5 %copy-start.29 = (s32[128]{0:T(128)}, s32[128]{0:T(128)S(1)}, u32[]{:S(2)}) copy-start(s32[128]{0:T(128)S(1)} %get-tuple-element.53) | copy-start | bytes 1540
  14.3 8.5 %copy-start.31 = (s32[128]{0:T(128)}, s32[128]{0:T(128)S(1)}, u32[]{:S(2)}) copy-start(s32[128]{0:T(128)S(1)} %get-tuple-element.54) | copy-start | bytes 1540
  14.5 14.1 %copy-start.8 = (f32[64,128]{1,0:T(8,128)}, f32[64,128]{1,0:T(8,128)S(1)}, u32[]{:S(2)}) copy-start(f32[64,128]{1,0:T(8,128)S(1)} %get-tuple-element.43.refs_5_.inner_re) | copy-start | bytes 98308
  14.6 14.1 %copy-start.1 = (bf16[768,256]{1,0:T(8,128)(2,1)S(1)}, bf16[768,256]{1,0:T(8,128)(2,1)}, u32[]{:S(2)}) copy-start(bf16[768,256]{1,0:T(8,128)(2,1)} %constant.233.refs_10_.lanes_dft) | copy-start | bytes 1179652
  14.6 14.1 %copy-start.6 = (bf16[128,384]{1,0:T(8,128)(2,1)S(1)}, bf16[128,384]{1,0:T(8,128)(2,1)}, u32[]{:S(2)}) copy-start(bf16[128,384]{1,0:T(8,128)(2,1)} %constant.228.refs_9_.split) | copy-start | bytes 294916
  14.6 14.0 %copy-start.21 = (s32[128]{0:T(128)S(1)}, s32[128]{0:T(128)}, u32[]{:S(2)}) copy-start(s32[128]{0:T(128)} %param.17) | copy-start | bytes 1540
  14.6 14.0 %copy-start.23 = (s32[128]{0:T(128)S(1)}, s32[128]{0:T(128)}, u32[]{:S(2)}) copy-start(s32[128]{0:T(128)} %param.16) | copy-start | bytes 1540
  30.3 43.8 %all-to-all-start.1 = ((f32[512,1,384]{2,1,0:T(1,128)}), f32[512,1,384]{2,1,0:T(1,128)S(1)}, u32[]{:S(2)}, u32[]{:S(2)}) async-start(f32[512,1,384]{2,1,0:T(1,128)} %bitcast.4), calls=%async_computation.1 | async-start | bytes 1572864 | tf_op jit(solution)/shard_map/all_to_all | solution.py:615
  46.6 1.0 copy-start.14
  47.6 0.8 copy-start.15
  48.4 0.7 copy-start.22
  49.1 0.7 copy-start.24
  49.7 3.9 %copy-start.28 = (pred[128]{0:T(512)(128)(4,1)S(1)}, pred[128]{0:T(512)(128)(4,1)}, u32[]{:S(2)}) copy-start(pred[128]{0:T(512)(128)(4,1)} %copy-done.27) | copy-start | bytes 388
  49.7 3.9 %copy-start.30 = (s32[128]{0:T(128)S(1)}, s32[128]{0:T(128)}, u32[]{:S(2)}) copy-start(s32[128]{0:T(128)} %copy-done.29) | copy-start | bytes 1540
  49.7 3.9 %copy-start.32 = (s32[128]{0:T(128)S(1)}, s32[128]{0:T(128)}, u32[]{:S(2)}) copy-start(s32[128]{0:T(128)} %copy-done.31) | copy-start | bytes 1540
  51.6 0.7 copy-start.10
  52.4 0.7 copy-start.12
  53.0 0.6 copy-start.19
  74.1 1.0 copy-start.2
  75.1 0.9 copy-start.3
  76.0 0.9 copy-start.4
  77.0 0.9 copy-start.5
  77.9 1.0 copy-start.7
  78.9 0.9 copy-start.17
  79.8 0.9 copy-start.18
  80.7 0.7 copy-start.20
  84.5 9.8 %copy-start.33 = (f32[63]{0:T(128)S(1)}, f32[63]{0:T(128)}, u32[]{:S(2)}) copy-start(f32[63]{0:T(128)} %param.20) | copy-start | bytes 760
  84.5 37.4 %all-to-all-start.2 = ((f32[512,1,384]{2,1,0:T(1,128)}), f32[512,1,384]{2,1,0:T(1,128)S(1)}, u32[]{:S(2)}, u32[]{:S(2)}) async-start(f32[512,1,384]{2,1,0:T(1,128)} %bitcast.6), calls=%async_computation.2 | async-start | bytes 1572864 | tf_op jit(solution)/shard_map/all_to_all | solution.py:615
  94.3 1.0 copy-start.26
  94.3 27.7 %copy-start.9 = (f32[64,128]{1,0:T(8,128)S(1)}, f32[64,128]{1,0:T(8,128)}, u32[]{:S(2)}) copy-start(f32[64,128]{1,0:T(8,128)} %copy-done.8) | copy-start | bytes 98308
  94.3 27.7 %copy-start.11 = (f32[512,128]{1,0:T(8,128)S(1)}, f32[512,128]{1,0:T(8,128)}, u32[]{:S(2)}) copy-start(f32[512,128]{1,0:T(8,128)} %copy-done.10) | copy-start | bytes 786436
  94.3 27.6 %copy-start.13 = (f32[512,128]{1,0:T(8,128)S(1)}, f32[512,128]{1,0:T(8,128)}, u32[]{:S(2)}) copy-start(f32[512,128]{1,0:T(8,128)} %copy-done.12) | copy-start | bytes 786436
  124.0 4.8 %copy-start.25 = (f32[384,128]{1,0:T(8,128)S(1)}, f32[384,128]{1,0:T(8,128)}, u32[]{:S(2)}) copy-start(f32[384,128]{1,0:T(8,128)} %select_reduce_fusion.1) | copy-start | bytes 589828
  124.0 20.6 %all-to-all-start.3 = ((f32[8,144,128]{2,1,0:T(8,128)}), f32[8,144,128]{2,1,0:T(8,128)S(1)}, u32[]{:S(2)}, u32[]{:S(2)}) async-start(f32[8,144,128]{2,1,0:T(8,128)} %bitcast.11), calls=%async_computation.3 | async-start | bytes 1179648 | tf_op jit(solution)/shard_map/all_to_all | solution.py:621
  144.9 15.8 %collective-permute-start = (f32[64,128]{1,0:T(8,128)S(1)}, f32[64,128]{1,0:T(8,128)S(1)}, u32[]{:S(2)}, u32[]{:S(2)}) collective-permute-start(f32[64,128]{1,0:T(8,128)S(1)} %get-tuple-element.14.refs_1_), channel_id=1, source_target_pairs={{0,1},{1,2},{2,3},{3,4},{4,5},{5,6},{6,7},{7,8},{8,9},{9,10},{10,1... | collective-permute-start | bytes 98312 | tf_op jit(solution)/shard_map/ppermute | solution.py:634
  148.2 12.4 %collective-permute-start.1 = (f32[64,128]{1,0:T(8,128)S(1)}, f32[64,128]{1,0:T(8,128)S(1)}, u32[]{:S(2)}, u32[]{:S(2)}) collective-permute-start(f32[64,128]{1,0:T(8,128)S(1)} %get-tuple-element.14.refs_1_), channel_id=1, source_target_pairs={{1,0},{2,1},{3,2},{4,3},{5,4},{6,5},{7,6},{8,7},{9,8},{10,9},{11,1... | collective-permute-start | bytes 98312 | tf_op jit(solution)/shard_map/ppermute | solution.py:635
  158.3 2.3 %copy-start.16 = (s32[128,128]{1,0:T(8,128)S(1)}, s32[128,128]{1,0:T(8,128)}, u32[]{:S(2)}) copy-start(s32[128,128]{1,0:T(8,128)} %refs_4_.1) | copy-start | bytes 196612

commit v4 on v3

--- a/solution.py
+++ b/solution.py
@@ -82,7 +82,13 @@
 
 def lane_matrix(table):
     whole = np.block([[table.real, table.imag], [-table.imag, table.real]]).astype(np.float32)
-    return matrix_right(jnp.asarray(whole))
+    return jnp.concatenate(rounded_halves(jnp.asarray(whole)), axis=0)
+
+
+def lane_product(value, lanes_dft):
+    high = lanes_dft[: 2 * LANES, :]
+    stacked = jnp.concatenate([high, high, lanes_dft[2 * LANES :, :]], axis=0)
+    return product(data_left(value), stacked)
 
 
 def height_lanes():
@@ -181,19 +187,18 @@
 
 
 def pack_kernel(field, out):
-    for c in range(2):
-        for part in range(8):
-            rows = [field.at[c][pl.ds(64 * part + g, 8, stride=8), :] for g in range(8)]
-            for e, value in enumerate(trade(rows)):
-                at = e * 128 + c * 64 + 8 * part
-                out[at : at + 8, :] = value
+    for part in range(field.shape[1] // 64):
+        rows = [field.at[0][pl.ds(64 * part + g, 8, stride=8), :] for g in range(8)]
+        for e, value in enumerate(trade(rows)):
+            out[e, 8 * part : 8 * part + 8, :] = value
 
 
 def columns_kernel(
     place, got, chirp_re, chirp_im, outer_re, outer_im, inner_re, inner_im, last_re, last_im, split, lanes_dft,
-    pick, terrain, out, work, held, mid,
+    pick, terrain, out, token, work, held, mid,
 ):
     e = place[0]
+    token[...] = jnp.zeros_like(token)
     for group in range(8):
         low = 8 * group
         re, im = [], []
@@ -215,7 +220,7 @@
         r, m = cmul(held[i * 128 : i * 128 + 64, :], held[i * 128 + 64 : i * 128 + 128, :], ir, ii)
         mid[at, :LANES] = r
         mid[at, LANES:] = m
-    result = product(data_left(mid[...]), lanes_dft[...])
+    result = lane_product(mid[...], lanes_dft)
     r, m = cmul(result[:, :LANES], result[:, LANES:], last_re[...], last_im[...])
     out[pl.ds(0, ROWS, stride=3), :] = r
     out[pl.ds(1, ROWS, stride=3), :] = m
@@ -238,22 +243,18 @@
 
 
 def rows_kernel(
-    place, got, chirp_re, chirp_im, outer_re, outer_im, inner_re, inner_im, back_re, back_im, split, lanes_dft,
-    tile, screen_re, screen_im, out, work, held, mid, picks, lows, low_strip,
+    place, got, split, tile, outer_re, outer_im, lanes_dft, back_re, back_im, inner_re, inner_im,
+    screen_re, screen_im, out, token, work, held, mid, picks, lows, low_strip,
 ):
     e, f = place[0], place[1]
-
-    def chirped(i):
-        at = slice(i * 64, i * 64 + 64)
-        r, m = cmul(
-            got[pl.ds(i * 192, 64, stride=3), :],
-            got[pl.ds(i * 192 + 1, 64, stride=3), :],
-            chirp_re[at, :],
-            chirp_im[at, :],
+    token[...] = jnp.zeros_like(token)
+
+    def received(i):
+        return jnp.concatenate(
+            [got[pl.ds(i * 192, 64, stride=3), :], got[pl.ds(i * 192 + 1, 64, stride=3), :]], axis=0
         )
-        return jnp.concatenate([r, m], axis=0)
-
-    row_dft(split, chirped, held)
+
+    row_dft(split, received, held)
     for i in range(8):
         parts = [got[pl.ds(i * 192 + 2 + 3 * o, 16, stride=12), :] for o in range(4)]
         upright = jnp.concatenate(parts + parts, axis=0).T
@@ -275,7 +276,7 @@
             r, m = cmul(re[i], im[i], inner_re[i : i + 1, :], inner_im[i : i + 1, :])
             mid[flat_rows(i, low), :LANES] = r
             mid[flat_rows(i, low), LANES:] = m
-    result = product(data_left(mid[...]), lanes_dft[...])
+    result = lane_product(mid[...], lanes_dft)
     lane8 = lane_of((8, LANES))
     height = (e + 8 * f + 512 * (lane8 // 16)).astype(jnp.float32)
     for n in range(0, ROWS, 8):
@@ -290,7 +291,7 @@
         r, m = cmul(r, m, br, bi)
         mid[at, :LANES] = r
         mid[at, LANES:] = m
-    result = product(data_left(mid[...]), lanes_dft[...])
+    result = lane_product(mid[...], lanes_dft)
     for group in range(8):
         low = 8 * group
         re, im = [], []
@@ -307,12 +308,8 @@
             work[im_rows(i, low), :] = m
     row_dft(split, block_of(work), held)
     for i in range(8):
-        at = slice(i * 64, i * 64 + 64)
-        r, m = cmul(
-            held[i * 128 : i * 128 + 64, :], held[i * 128 + 64 : i * 128 + 128, :], chirp_re[at, :], chirp_im[at, :]
-        )
-        out[pl.ds(i * 192, 64, stride=3), :] = r
-        out[pl.ds(i * 192 + 1, 64, stride=3), :] = m
+        out[pl.ds(i * 192, 64, stride=3), :] = held[i * 128 : i * 128 + 64, :]
+        out[pl.ds(i * 192 + 1, 64, stride=3), :] = held[i * 128 + 64 : i * 128 + 128, :]
     lane16 = lane_of((16, LANES))
     for i in range(8):
         block = low_strip[i * 64 : i * 64 + 64, :]
@@ -340,7 +337,7 @@
         )
         mid[at, :LANES] = r
         mid[at, LANES:] = m
-    result = product(data_left(mid[...]), lanes_dft[...])
+    result = lane_product(mid[...], lanes_dft)
     ir, ii = inner_re[...], inner_im[...]
     for i in range(8):
         at = slice(i * 64, i * 64 + 64)
@@ -405,12 +402,10 @@
 
 
 def unpack_kernel(got, field_out):
-    for c in range(2):
-        for part in range(8):
-            at = c * 64 + 8 * part
-            values = trade([got[e * PART + at : e * PART + at + 8, :] for e in range(8)])
-            for g, value in enumerate(values):
-                field_out.at[c][pl.ds(64 * part + g, 8, stride=8), :] = value
+    for part in range(got.shape[1] // 8):
+        values = trade([got[e, 8 * part : 8 * part + 8, :] for e in range(8)])
+        for g, value in enumerate(values):
+            field_out.at[0][pl.ds(64 * part + g, 8, stride=8), :] = value
 
 
 def sources_kernel(place, left, own, right, strips, mask, beams, sources):
@@ -424,9 +419,14 @@
             sources[s, c] = 2.0 * seen * strips[at : at + 16, :] * back[16 * s : 16 * s + 16, :]
 
 
-def prepare_kernel(
-    place, profile, pick, terrain, mask, chirp_re, chirp_im, screen_re, screen_im, coef_re, coef_im, seen, turned,
-):
+def screen(height, angle):
+    depth = jnp.maximum(height.astype(jnp.float32) - 0.75 * NH, 0.0) / (0.25 * NH)
+    amount = abs(GAIN) * jnp.exp(-4.0 * depth * depth)
+    turn = angle + float(np.angle(GAIN))
+    return amount * jnp.cos(turn), amount * jnp.sin(turn)
+
+
+def profiles_kernel(place, token, profile, screen_re, screen_im):
     e, f = place[0], place[1]
     lane16 = lane_of((16, LANES))
     group = lane16 // 16
@@ -435,16 +435,17 @@
     for g in range(8):
         chosen = jnp.where(wide == e + 8 * f, profile[:, 512 * g : 512 * (g + 1)], 0.0)
         phase = jnp.where(group == g, jnp.sum(chosen, axis=1, keepdims=True), phase)
-
-    def screen(height, angle):
-        depth = jnp.maximum(height.astype(jnp.float32) - 0.75 * NH, 0.0) / (0.25 * NH)
-        amount = abs(GAIN) * jnp.exp(-4.0 * depth * depth)
-        turn = angle + float(np.angle(GAIN))
-        return amount * jnp.cos(turn), amount * jnp.sin(turn)
-
     sr, si = screen(e + 8 * f + 512 * group, phase)
     screen_re[...] = sr
     screen_im[...] = si
+
+
+def prepare_kernel(
+    place, token, profile, pick, terrain, mask, chirp_re, chirp_im, coef_re, coef_im, seen, turned,
+):
+    e = place[0]
+    lane16 = lane_of((16, LANES))
+    group = lane16 // 16
     picks = jnp.zeros((8, LANES), jnp.float32)
     lows = jnp.zeros((8, LANES), jnp.float32)
     masks = jnp.zeros((16, LANES), jnp.float32)
@@ -486,29 +487,39 @@
     return jnp.cos(angle), jnp.sin(angle)
 
 
-def layout_tables():
+def digits():
     row = lax.broadcasted_iota(jnp.int32, (ROWS, LANES), 0)
     lane = lax.broadcasted_iota(jnp.int32, (ROWS, LANES), 1)
-    i, j, g, t = row // PA, row % PA, lane // 16, lane % 16
-    square_row = lax.broadcasted_iota(jnp.int32, (PA, LANES), 0)
+    return row // PA, row % PA, lane // 16, lane % 16
+
+
+def height_tables(e, f, zero):
+    i, j, g, t = digits()
+    row = lax.broadcasted_iota(jnp.int32, (PA, LANES), 0)
     group = lax.broadcasted_iota(jnp.int32, (PA, LANES), 1) // 16
+    return (
+        turns(64 * j * j + g * g + 1024 * i * g + 16 * j * g + zero, 2 * NH),
+        turns(zero - i * (8 * j + g), NH),
+        turns(zero - row * group, 512),
+        turns(
+            2 * (i * i + 64 * j * j + 16 * i * j + 1024 * i * g)
+            + INV * ((256 * e * e + t * t + 4096 * e * f + 256 * f * t + 32 * e * t) % (2 * NA))
+            + zero,
+            2 * NA,
+        ),
+    )
+
+
+def azimuth_tables(zero):
+    i, j, g, t = digits()
     block = lax.broadcasted_iota(jnp.int32, (8, LANES), 0)
     inside = lax.broadcasted_iota(jnp.int32, (8, LANES), 1) % 16
-    heights = (
-        turns(64 * j * j + g * g + 1024 * i * g + 16 * j * g, 2 * NH),
-        turns(-i * (8 * j + g), NH),
-        turns(-square_row * group, 512),
-        turns(i * i + 64 * j * j + 16 * i * j + 1024 * i * g, 2 * NH),
+    reverse = (j * j + 4096 * i * i + 128 * i * j + 1024 * j * t) % (2 * NA)
+    return (
+        turns(zero - (INV % NA) * (j * (16 * i + t)), NA),
+        turns(zero - (INV % 128) * block * inside, 128),
+        turns(INV * reverse + zero, 2 * NA),
     )
-    natural = (256 * i * i + t * t + 4096 * i * j + 256 * j * t + 32 * i * t) % (2 * NA)
-    reverse = (j * j + 4096 * i * i + 128 * i * j + 1024 * j * t) % (2 * NA)
-    azimuths = (
-        turns(INV * natural, 2 * NA),
-        turns(-(INV % NA) * (j * (16 * i + t)), NA),
-        turns(-(INV % 128) * block * inside, 128),
-        turns(INV * reverse, 2 * NA),
-    )
-    return heights, azimuths
 
 
 def band(taps, offset):
@@ -570,20 +581,39 @@
 WORK = [(2 * ROWS, LANES), (2 * ROWS, LANES), (ROWS, 2 * LANES)]
 
 
+def gridded(kernel, outs, value, in_block, out_block, in_map, out_map, grant, interpret=False):
+    return pl.pallas_call(
+        kernel,
+        out_shape=outs,
+        grid=(2, 2),
+        in_specs=[pl.BlockSpec(in_block, in_map)],
+        out_specs=pl.BlockSpec(out_block, out_map),
+        cost_estimate=pl.CostEstimate(flops=200_000_000, bytes_accessed=2_000_000, transcendentals=0),
+        compiler_params=pltpu.CompilerParams(vmem_limit_bytes=grant),
+        interpret=interpret,
+    )(value)
+
+
 def stage_pack(field, **kw):
-    return call(pack_kernel, f32(2 * ROWS, LANES), [], (field,), grant=WIDE_GRANT, **kw)
+    slab, mixed = (1, 256, LANES), (PH, 32, LANES)
+    outs = f32(PH, 2 * PA, LANES)
+    moved = gridded(
+        pack_kernel, outs, field, slab, mixed, lambda c, p: (c, p, 0), lambda c, p: (0, 2 * c + p, 0), WIDE_GRANT, **kw
+    )
+    return moved.reshape(2 * ROWS, LANES)
 
 
 def stage_columns(place, got, heights, pick, terrain, **kw):
     chirp, outer, inner, last = heights
     args = (got, *chirp, *outer, *inner, *last, row_matrix(1), height_lanes(), pick[None], terrain[None])
-    return call(columns_kernel, f32(3 * ROWS, LANES), WORK, args, place, **kw)
+    return call(columns_kernel, (f32(3 * ROWS, LANES), f32(8, LANES)), WORK, args, place, **kw)
 
 
 def stage_rows(place, got, azimuths, screen, **kw):
-    chirp, outer, inner, back = azimuths
-    args = (got, *chirp, *outer, *inner, *back, row_matrix(INV), azimuth_lanes(), tiles(), *screen)
-    return call(rows_kernel, f32(3 * ROWS, LANES), WORK + [(ROWS, LANES)] * 3, args, place, **kw)
+    outer, inner, back = azimuths
+    far = (row_matrix(INV), tiles(), *outer, azimuth_lanes(), *back)
+    args = (got, *far, *inner, *screen)
+    return call(rows_kernel, (f32(3 * ROWS, LANES), f32(8, LANES)), WORK + [(ROWS, LANES)] * 3, args, place, **kw)
 
 
 def stage_final(got, heights, coef, seen, range_pair, **kw):
@@ -597,16 +627,25 @@
 
 
 def stage_unpack(got, **kw):
-    return call(unpack_kernel, f32(2, NH // PH, LANES), [], (got,), **kw)
+    slab, mixed = (1, 256, LANES), (PH, 32, LANES)
+    outs = f32(2, NH // PH, LANES)
+    value = got.reshape(PH, PART, LANES)
+    return gridded(
+        unpack_kernel, outs, value, mixed, slab, lambda c, p: (0, 2 * c + p, 0), lambda c, p: (c, p, 0), GRANT, **kw
+    )
 
 
 def stage_sources(place, left, own, right, strips, mask, beams, **kw):
     return call(sources_kernel, f32(2, 2, 16, LANES), [], (left, own, right, strips, mask, beams), place, **kw)
 
 
-def stage_prepare(place, profile, pick, terrain, mask, heights, **kw):
-    outs = (f32(16, LANES), f32(16, LANES), f32(ROWS, LANES), f32(ROWS, LANES), f32(16, LANES))
-    args = (profile, pick[None], terrain[None], mask, *heights[0])
+def stage_profiles(place, token, profile, **kw):
+    return call(profiles_kernel, (f32(16, LANES), f32(16, LANES)), [], (token, profile), place, cost=200_000, **kw)
+
+
+def stage_prepare(place, token, profile, pick, terrain, mask, heights, **kw):
+    outs = (f32(ROWS, LANES), f32(ROWS, LANES), f32(16, LANES))
+    args = (token, profile, pick[None], terrain[None], mask, *heights[0])
     return call(prepare_kernel, outs, [(NH, LANES)], args, place, **kw)
 
 
@@ -624,12 +663,17 @@
 def local(field, terrain, profile_pick, profile_table, clutter_mask, pulse, beam, measured):
     place = "here"
     range_pair, turned, beams = clutter_tables(pulse, beam, measured, lax.axis_index("ha"))
-    heights, azimuths = layout_tables()
+    e, f = lax.axis_index("ha"), lax.axis_index("az")
     got = swap_heights(stage_pack(field))
-    got = swap_all(stage_columns(place, got, heights, profile_pick, terrain))
-    prepared = stage_prepare(place, profile_table, profile_pick, terrain, clutter_mask, heights)
-    got = swap_all(stage_rows(place, got, azimuths, prepared[0:2]))
-    got = swap_heights(stage_final(got, heights, prepared[2:4], prepared[4], range_pair))
+    sent, token = stage_columns(place, got, height_tables(e, f, 0), profile_pick, terrain)
+    azimuths = azimuth_tables(token[0, 0].astype(jnp.int32))
+    screens = stage_profiles(place, token, profile_table)
+    got = swap_all(sent)
+    sent, token = stage_rows(place, got, azimuths, screens)
+    heights = height_tables(e, f, token[0, 0].astype(jnp.int32))
+    prepared = stage_prepare(place, token, profile_table, profile_pick, terrain, clutter_mask, heights)
+    got = swap_all(sent)
+    got = swap_heights(stage_final(got, heights, prepared[0:2], prepared[2], range_pair))
     edges, strips = stage_strips(got, turned)
     left = lax.ppermute(edges, "az", [(i, (i + 1) % PA) for i in range(PA)])
     right = lax.ppermute(edges, "az", [((i + 1) % PA, i) for i in range(PA)])

time: 162 us -> 156 us (0.963)
  local copies, waits for them, and re-layouts: 12.5 us -> 2.77 us
    unnamed x68 -> x30, local copies, waits for them, and re-layouts: 12.5 us -> 1.73 us
    pallas_call x0 -> x2, Pallas kernels: none -> 5.85 us  [gridded(): pl.pallas_call(kernel, out_shape=outs, grid=(2, 2), in_specs=[pl.BlockSpe...]
    pallas_call x8 -> x7, Pallas kernels: 15.4 us -> 9.98 us  [call(): pl.pallas_call(kernel, out_shape=outs, in_specs=specs, out_specs=jax.tree...]
    all_to_all x2, waiting for transfers between devices: 19.7 us -> 24.5 us  [swap_heights(): lax.all_to_all(shaped, 'ha', split_axis=0, concat_axis=0, tiled=True)]
    all_to_all x2, waiting for transfers between devices: 45.7 us -> 42.2 us  [swap_all(): lax.all_to_all(shaped, ('ha', 'az'), split_axis=0, concat_axis=0, tiled=T...]
    sin x3 -> x6, other arithmetic: 8.51 us -> 9.78 us  [turns(): return (jnp.cos(angle), jnp.sin(angle))]
  transfers between devices with their start and end apart: 6 -> 6, of which waited for: 4 -> 4; matrix products, arithmetic and copies ran while one was open for 8% -> 9% of each run, Pallas kernels for 3% -> 3%
where the time goes in v4:
time: 156 us; the launch traced here: 155 us
  waiting for transfers between devices  66.8 us (43%)
  starting transfers between devices  54.2 us (35%)
  Pallas kernels  15.8 us (10%)
  other arithmetic  12.8 us (8%)
  local copies, waits for them, and re-layouts  2.77 us (2%)
  between operations  2.29 us (1%)
    all_to_all x2, waiting for transfers between devices, swap_all(): lax.all_to_all(shaped, ('ha', 'az'), split_axis=0, concat_axis=0, tiled=T...  42.2 us
    all_to_all x2, starting transfers between devices, swap_all(): lax.all_to_all(shaped, ('ha', 'az'), split_axis=0, concat_axis=0, tiled=T...  25.9 us
    all_to_all x2, waiting for transfers between devices, swap_heights(): lax.all_to_all(shaped, 'ha', split_axis=0, concat_axis=0, tiled=True)  24.5 us
    all_to_all x2, starting transfers between devices, swap_heights(): lax.all_to_all(shaped, 'ha', split_axis=0, concat_axis=0, tiled=True)  14.9 us
    ppermute x1, starting transfers between devices, local(): right = lax.ppermute(edges, 'az', [((i + 1) % PA, i) for i in range(PA)])  10.1 us
    pallas_call x7, Pallas kernels, call(): pl.pallas_call(kernel, out_shape=outs, in_specs=specs, out_specs=jax.tree...  9.98 us
    sin x6, other arithmetic, turns(): return (jnp.cos(angle), jnp.sin(angle))  9.78 us
    pallas_call x2, Pallas kernels, gridded(): pl.pallas_call(kernel, out_shape=outs, grid=(2, 2), in_specs=[pl.BlockSpe...  5.85 us
  transfers between devices with their start and end apart: 6, of which 4 were waited for; matrix products, arithmetic and copies ran while one was open for 9% of the time, Pallas kernels for 3%

profile of v4, /device:TPU:1, one launch (start us, length us, event | category | flops | bytes accessed | tf_op | source)
XLA Modules:
  0.0 155.1 jit_solution(6274259591026947467)
XLA Ops:
  0.6 0.0 copy-start
  0.6 3.7 %shard_map.158 = f32[8,128,128]{2,1,0:T(8,128)} custom-call(f32[2,512,128]{2,1,0:T(8,128)} %field.1), custom_call_target="tpu_custom_call" | custom-call | flops 200000000 | bytes 2000000 | tf_op jit(solution)/shard_map/pallas_call | solution.py:585
  4.3 10.2 %all-to-all-start = ((f32[8,128,128]{2,1,0:T(8,128)}), f32[8,128,128]{2,1,0:T(8,128)S(1)}, u32[]{:S(2)}, u32[]{:S(2)}) async-start(f32[8,128,128]{2,1,0:T(8,128)} %shard_map.158), calls=%async_computation | async-start | bytes 1048576 | tf_op jit(solution)/shard_map/all_to_all | solution.py:660
  14.6 0.2 fusion.74
  14.8 0.0 copy-start.2
  14.8 0.0 copy-start.3
  14.8 0.0 copy-start.10
  14.8 0.0 copy-start.11
  14.8 3.5 %fusion.61 = (f32[512,128]{1,0:T(8,128)S(1)}, f32[512,128]{1,0:T(8,128)S(1)}, f32[512,128]{1,0:T(8,128)S(1)}, f32[512,128]{1,0:T(8,128)S(1)}, f32[512,128]{1,0:T(8,128)S(1)}, /*index=5*/f32[512,128]{1,0:T(8,128)S(1)}) fusion(s32[]{:T(128)S(6)} %mul.288, s32[]{:T(128)S(6)} %mul.285, s32[]{:T(128)S(6)} %mul.284, s32[128]{0:T(128)S(1)} %get-tuple-element.61, ...), kind=kLoop, calls=%fused_computation.131 | loop fusion | flops 5505024 | bytes 1584400 | tf_op jit(solution)/shard_map/sin | solution.py:487
  18.3 10.6 %all-to-all-done = f32[8,128,128]{2,1,0:T(8,128)S(1)} async-done(((f32[8,128,128]{2,1,0:T(8,128)}), f32[8,128,128]{2,1,0:T(8,128)S(1)}, u32[]{:S(2)}, u32[]{:S(2)}) %all-to-all-start) | async-done | bytes 524320 | tf_op jit(solution)/shard_map/all_to_all | solution.py:660
  28.9 0.0 copy-done.2
  28.9 0.0 copy-done.3
  28.9 0.0 copy-done.10
  29.0 0.0 copy-done.11
  29.0 1.7 %shard_map.159 = (f32[1536,128]{1,0:T(8,128)}, f32[8,128]{1,0:T(8,128)S(1)}) custom-call(f32[1024,128]{1,0:T(8,128)S(1)} %bitcast.26, f32[512,128]{1,0:T(8,128)S(1)} %get-tuple-element.43.refs_1_, f32[512,128]{1,0:T(8,128)S(1)} %get-tuple-element.40.refs_2_, f32[512,128]{1,0:T(8,128)S(1)} %get-tuple-element.42.refs_3_, ...), custom_call_target="tpu_custom_call" | custom-call | flops 200000000 | bytes 2000000 | tf_op jit(solution)/shard_map/pallas_call | solution.py:569
  30.7 16.3 %all-to-all-start.1 = ((f32[512,1,384]{2,1,0:T(1,128)}), f32[512,1,384]{2,1,0:T(1,128)S(1)}, u32[]{:S(2)}, u32[]{:S(2)}) async-start(f32[512,1,384]{2,1,0:T(1,128)} %bitcast.3), calls=%async_computation.1 | async-start | bytes 1572864 | tf_op jit(solution)/shard_map/all_to_all | solution.py:654
  47.0 0.0 copy-done.14
  47.0 0.0 copy-start.4
  47.0 0.0 copy-start.8
  47.0 0.0 copy-start.9
  47.0 0.5 select_reduce_fusion.2
  47.5 0.5 slice.6
  48.7 0.0 copy-done.1
  48.7 0.2 shard_map.160
  48.9 0.1 fusion.84
  49.0 2.5 %fusion.49 = (f32[512,128]{1,0:T(8,128)S(1)}, f32[512,128]{1,0:T(8,128)S(1)}, f32[512,128]{1,0:T(8,128)S(1)}, f32[512,128]{1,0:T(8,128)S(1)}) fusion(s32[]{:T(128)} %bitcast.5, s32[128]{0:T(128)S(1)} %get-tuple-element.61, s32[128]{0:T(128)S(1)} %get-tuple-element.62, pred[128]{0:T(512)(128)(4,1)S(1)} %get-tuple-element.58, s32[512]{0:T(512)S(1)} %get-tuple-element.52, ...), kind=kLoop, calls=%fused_computation.119 | loop fusion | flops 3735552 | bytes 1058948 | tf_op jit(solution)/shard_map/sin | solution.py:487
  51.5 23.0 %all-to-all-done.1 = f32[512,1,384]{2,1,0:T(1,128)S(1)} async-done(((f32[512,1,384]{2,1,0:T(1,128)}), f32[512,1,384]{2,1,0:T(1,128)S(1)}, u32[]{:S(2)}, u32[]{:S(2)}) %all-to-all-start.1) | async-done | bytes 786464 | tf_op jit(solution)/shard_map/all_to_all | solution.py:654
  74.5 0.0 copy-done.4
  74.5 0.0 copy-done.8
  74.5 0.0 copy-done.9
  74.5 3.1 %shard_map.161 = (f32[1536,128]{1,0:T(8,128)}, f32[8,128]{1,0:T(8,128)S(1)}) custom-call(f32[1536,128]{1,0:T(8,128)S(1)} %bitcast.24, bf16[128,384]{1,0:T(8,128)(2,1)S(1)} %copy-done.9, bf16[128,512]{1,0:T(8,128)(2,1)S(1)} %copy-done.8, f32[512,128]{1,0:T(8,128)S(1)} %get-tuple-element.39.refs_3_, f32[512,128]{1,0:T(8,128)S(1)} %get-tuple-element.37.refs_4_, ...), custom_call_target="tpu_custom_call" | custom-call | flops 200000000 | bytes 2000000 | tf_op jit(solution)/shard_map/pallas_call | solution.py:569
  77.6 9.6 %all-to-all-start.2 = ((f32[512,1,384]{2,1,0:T(1,128)}), f32[512,1,384]{2,1,0:T(1,128)S(1)}, u32[]{:S(2)}, u32[]{:S(2)}) async-start(f32[512,1,384]{2,1,0:T(1,128)} %bitcast.6), calls=%async_computation.2 | async-start | bytes 1572864 | tf_op jit(solution)/shard_map/all_to_all | solution.py:654
  87.2 0.3 reduce-precision_convert_fusion.1
  87.5 0.1 subtract_add_fusion.1
  87.6 0.0 copy-done.13
  87.6 0.7 select_reduce_fusion.1
  88.3 0.5 slice.7
  89.5 0.0 copy-start.5
  89.5 0.0 copy-start.12
  89.5 3.4 %fusion.63 = (f32[512,128]{1,0:T(8,128)S(1)}, f32[512,128]{1,0:T(8,128)S(1)}, f32[512,128]{1,0:T(8,128)S(1)}, f32[512,128]{1,0:T(8,128)S(1)}, f32[512,128]{1,0:T(8,128)S(1)}, /*index=5*/f32[512,128]{1,0:T(8,128)S(1)}) fusion(s32[]{:T(128)} %bitcast.8, s32[]{:T(128)S(6)} %mul.288, s32[]{:T(128)S(6)} %mul.285, s32[]{:T(128)S(6)} %mul.284, ...), kind=kLoop, calls=%fused_computation.133 | loop fusion | flops 5636096 | bytes 1584404 | tf_op jit(solution)/shard_map/sin | solution.py:487
  92.9 0.0 copy-done.5
  92.9 0.0 copy-done.12
  92.9 1.9 %shard_map.162 = (f32[512,128]{1,0:T(8,128)S(1)}, f32[512,128]{1,0:T(8,128)S(1)}, f32[16,128]{1,0:T(8,128)S(1)}) custom-call(f32[8,128]{1,0:T(8,128)S(1)} %get-tuple-element.18.refs_0_, f32[16,4096]{1,0:T(8,128)S(1)} %copy-done.1, s32[1,128]{1,0:T(1,128)S(1)} %bitcast.28, s32[1,128]{1,0:T(1,128)S(1)} %bitcast.30, s32[128,128]{1,0:T(8,128)S(1)} %copy-done.5, ...), custom_call_target="tpu_custom_call" | custom-call | flops 200000000 | bytes 2000000 | tf_op jit(solution)/shard_map/pallas_call | solution.py:569
  94.8 0.0 copy-start.6
  94.8 0.7 copy-done.6
  95.5 0.2 fusion.72
  95.6 19.2 %all-to-all-done.2 = f32[512,1,384]{2,1,0:T(1,128)S(1)} async-done(((f32[512,1,384]{2,1,0:T(1,128)}), f32[512,1,384]{2,1,0:T(1,128)S(1)}, u32[]{:S(2)}, u32[]{:S(2)}) %all-to-all-start.2) | async-done | bytes 786464 | tf_op jit(solution)/shard_map/all_to_all | solution.py:654
  114.9 0.9 copy-done.7
  115.8 2.1 %shard_map.163 = f32[1152,128]{1,0:T(8,128)} custom-call(f32[1536,128]{1,0:T(8,128)S(1)} %bitcast.23, f32[512,128]{1,0:T(8,128)S(1)} %get-tuple-element.29.chirp_re, f32[512,128]{1,0:T(8,128)S(1)} %get-tuple-element.28.chirp_im, f32[512,128]{1,0:T(8,128)S(1)} %get-tuple-element.35.outer_re, f32[512,128]{1,0:T(8,128)S(1)} %get-tuple-element.34.outer_im, ...), custom_call_target="tpu_custom_call" | custom-call | flops 200000000 | bytes 2000000 | tf_op jit(solution)/shard_map/pallas_call | solution.py:569
  117.9 4.7 %all-to-all-start.3 = ((f32[8,144,128]{2,1,0:T(8,128)}), f32[8,144,128]{2,1,0:T(8,128)S(1)}, u32[]{:S(2)}, u32[]{:S(2)}) async-start(f32[8,144,128]{2,1,0:T(8,128)} %bitcast.12), calls=%async_computation.3 | async-start | bytes 1179648 | tf_op jit(solution)/shard_map/all_to_all | solution.py:660
  122.6 0.2 select_reduce_fusion.3
  122.8 0.1 multiply_reduce_fusion
  122.9 1.3 select_reduce_fusion
  124.2 0.1 reduce-precision_convert_fusion
  124.2 0.0 copy-done
  124.2 0.2 convolution_bitcast_fusion.measured
  124.4 13.9 %all-to-all-done.3.got = f32[8,144,128]{2,1,0:T(8,128)S(1)} async-done(((f32[8,144,128]{2,1,0:T(8,128)}), f32[8,144,128]{2,1,0:T(8,128)S(1)}, u32[]{:S(2)}, u32[]{:S(2)}) %all-to-all-start.3) | async-done | bytes 589856 | tf_op jit(solution)/shard_map/all_to_all | solution.py:660
  138.3 0.2 shard_map.165
  138.6 3.4 %collective-permute-start = (f32[64,128]{1,0:T(8,128)S(1)}, f32[64,128]{1,0:T(8,128)S(1)}, u32[]{:S(2)}, u32[]{:S(2)}) collective-permute-start(f32[64,128]{1,0:T(8,128)S(1)} %get-tuple-element.22.refs_1_), channel_id=1, source_target_pairs={{0,1},{1,2},{2,3},{3,4},{4,5},{5,6},{6,7},{7,8},{8,9},{9,10},{10,1... | collective-permute-start | bytes 98312 | tf_op jit(solution)/shard_map/ppermute | solution.py:678
  142.0 10.1 %collective-permute-start.1 = (f32[64,128]{1,0:T(8,128)S(1)}, f32[64,128]{1,0:T(8,128)S(1)}, u32[]{:S(2)}, u32[]{:S(2)}) collective-permute-start(f32[64,128]{1,0:T(8,128)S(1)} %get-tuple-element.22.refs_1_), channel_id=1, source_target_pairs={{1,0},{2,1},{3,2},{4,3},{5,4},{6,5},{7,6},{8,7},{9,8},{10,9},{11,1... | collective-permute-start | bytes 98312 | tf_op jit(solution)/shard_map/ppermute | solution.py:679
  152.1 2.2 %shard_map.164 = f32[2,512,128]{2,1,0:T(8,128)} custom-call(f32[8,144,128]{2,1,0:T(8,128)S(1)} %all-to-all-done.3.got), custom_call_target="tpu_custom_call" | custom-call | flops 200000000 | bytes 2000000 | tf_op jit(solution)/shard_map/pallas_call | solution.py:585
  154.2 0.0 collective-permute-done.refs_0_
  154.2 0.0 collective-permute-done.1.refs_2_
  154.2 0.8 shard_map.166
  (19 shorter events, 0.1 us)
Async XLA Ops:
  0.6 123.6 %copy-start = (f32[2,128,128]{2,1,0:T(8,128)S(1)}, f32[2,128,128]{2,1,0:T(8,128)}, u32[]{:S(2)}) copy-start(f32[2,128,128]{2,1,0:T(8,128)} %param.22) | copy-start | bytes 393220
  4.3 24.6 %all-to-all-start = ((f32[8,128,128]{2,1,0:T(8,128)}), f32[8,128,128]{2,1,0:T(8,128)S(1)}, u32[]{:S(2)}, u32[]{:S(2)}) async-start(f32[8,128,128]{2,1,0:T(8,128)} %shard_map.158), calls=%async_computation | async-start | bytes 1048576 | tf_op jit(solution)/shard_map/all_to_all | solution.py:660
  14.8 14.2 %copy-start.2 = (bf16[512,256]{1,0:T(8,128)(2,1)S(1)}, bf16[512,256]{1,0:T(8,128)(2,1)}, u32[]{:S(2)}) copy-start(bf16[512,256]{1,0:T(8,128)(2,1)} %constant.278.refs_10_.lanes_dft) | copy-start | bytes 786436
  14.8 14.2 %copy-start.3 = (bf16[128,384]{1,0:T(8,128)(2,1)S(1)}, bf16[128,384]{1,0:T(8,128)(2,1)}, u32[]{:S(2)}) copy-start(bf16[128,384]{1,0:T(8,128)(2,1)} %constant.273.refs_9_.split) | copy-start | bytes 294916
  14.8 14.2 %copy-start.10 = (s32[128]{0:T(128)S(1)}, s32[128]{0:T(128)}, u32[]{:S(2)}) copy-start(s32[128]{0:T(128)} %param.17) | copy-start | bytes 1540
  14.8 14.1 %copy-start.11 = (s32[128]{0:T(128)S(1)}, s32[128]{0:T(128)}, u32[]{:S(2)}) copy-start(s32[128]{0:T(128)} %param.16) | copy-start | bytes 1540
  30.7 16.3 %copy-start.14 = (f32[63]{0:T(128)S(1)}, f32[63]{0:T(128)}, u32[]{:S(2)}) copy-start(f32[63]{0:T(128)} %param.20) | copy-start | bytes 760
  30.7 18.0 %copy-start.1 = (f32[16,4096]{1,0:T(8,128)S(1)}, f32[16,4096]{1,0:T(8,128)}, u32[]{:S(2)}) copy-start(f32[16,4096]{1,0:T(8,128)} %refs_1_.3) | copy-start | bytes 786436
  30.7 43.8 %all-to-all-start.1 = ((f32[512,1,384]{2,1,0:T(1,128)}), f32[512,1,384]{2,1,0:T(1,128)S(1)}, u32[]{:S(2)}, u32[]{:S(2)}) async-start(f32[512,1,384]{2,1,0:T(1,128)} %bitcast.3), calls=%async_computation.1 | async-start | bytes 1572864 | tf_op jit(solution)/shard_map/all_to_all | solution.py:654
  47.0 27.5 %copy-start.4 = (bf16[512,256]{1,0:T(8,128)(2,1)S(1)}, bf16[512,256]{1,0:T(8,128)(2,1)}, u32[]{:S(2)}) copy-start(bf16[512,256]{1,0:T(8,128)(2,1)} %constant.289.refs_5_) | copy-start | bytes 786436
  47.0 27.5 %copy-start.8 = (bf16[128,512]{1,0:T(8,128)(2,1)S(1)}, bf16[128,512]{1,0:T(8,128)(2,1)}, u32[]{:S(2)}) copy-start(bf16[128,512]{1,0:T(8,128)(2,1)} %constant.284.refs_2_) | copy-start | bytes 393220
  47.0 27.5 %copy-start.9 = (bf16[128,384]{1,0:T(8,128)(2,1)S(1)}, bf16[128,384]{1,0:T(8,128)(2,1)}, u32[]{:S(2)}) copy-start(bf16[128,384]{1,0:T(8,128)(2,1)} %constant.283.refs_1_) | copy-start | bytes 294916
  77.6 10.0 %copy-start.13 = (f32[31]{0:T(128)S(1)}, f32[31]{0:T(128)}, u32[]{:S(2)}) copy-start(f32[31]{0:T(128)} %param.21) | copy-start | bytes 376
  77.6 37.2 %all-to-all-start.2 = ((f32[512,1,384]{2,1,0:T(1,128)}), f32[512,1,384]{2,1,0:T(1,128)S(1)}, u32[]{:S(2)}, u32[]{:S(2)}) async-start(f32[512,1,384]{2,1,0:T(1,128)} %bitcast.6), calls=%async_computation.2 | async-start | bytes 1572864 | tf_op jit(solution)/shard_map/all_to_all | solution.py:654
  89.5 3.4 %copy-start.5 = (s32[128,128]{1,0:T(8,128)S(1)}, s32[128,128]{1,0:T(8,128)}, u32[]{:S(2)}) copy-start(s32[128,128]{1,0:T(8,128)} %refs_4_.3) | copy-start | bytes 196612
  89.5 3.4 %copy-start.12 = (s32[128]{0:T(128)S(1)}, s32[128]{0:T(128)}, u32[]{:S(2)}) copy-start(s32[128]{0:T(128)} %param.16) | copy-start | bytes 1540
  94.8 0.7 copy-start.6
  114.9 1.0 copy-start.7
  117.9 20.5 %all-to-all-start.3 = ((f32[8,144,128]{2,1,0:T(8,128)}), f32[8,144,128]{2,1,0:T(8,128)S(1)}, u32[]{:S(2)}, u32[]{:S(2)}) async-start(f32[8,144,128]{2,1,0:T(8,128)} %bitcast.12), calls=%async_computation.3 | async-start | bytes 1179648 | tf_op jit(solution)/shard_map/all_to_all | solution.py:660
  138.6 15.7 %collective-permute-start = (f32[64,128]{1,0:T(8,128)S(1)}, f32[64,128]{1,0:T(8,128)S(1)}, u32[]{:S(2)}, u32[]{:S(2)}) collective-permute-start(f32[64,128]{1,0:T(8,128)S(1)} %get-tuple-element.22.refs_1_), channel_id=1, source_target_pairs={{0,1},{1,2},{2,3},{3,4},{4,5},{5,6},{6,7},{7,8},{8,9},{9,10},{10,1... | collective-permute-start | bytes 98312 | tf_op jit(solution)/shard_map/ppermute | solution.py:678
  142.0 12.3 %collective-permute-start.1 = (f32[64,128]{1,0:T(8,128)S(1)}, f32[64,128]{1,0:T(8,128)S(1)}, u32[]{:S(2)}, u32[]{:S(2)}) collective-permute-start(f32[64,128]{1,0:T(8,128)S(1)} %get-tuple-element.22.refs_1_), channel_id=1, source_target_pairs={{1,0},{2,1},{3,2},{4,3},{5,4},{6,5},{7,6},{8,7},{9,8},{10,9},{11,1... | collective-permute-start | bytes 98312 | tf_op jit(solution)/shard_map/ppermute | solution.py:679

commit v5 on v4

--- a/solution.py
+++ b/solution.py
@@ -86,8 +86,9 @@
 
 
 def lane_product(value, lanes_dft):
-    high = lanes_dft[: 2 * LANES, :]
-    stacked = jnp.concatenate([high, high, lanes_dft[2 * LANES :, :]], axis=0)
+    middle = lanes_dft.shape[0] // 2
+    high = lanes_dft[:middle, :]
+    stacked = jnp.concatenate([high, high, lanes_dft[middle:, :]], axis=0)
     return product(data_left(value), stacked)
 
 
@@ -162,6 +163,12 @@
     return parts
 
 
+def inner_table():
+    steps = (row_of((64, LANES)) * (lane_of((64, LANES)) // 16)) % 512
+    angle = steps.astype(jnp.float32) * (2.0 * math.pi / 512)
+    return jnp.cos(angle), -jnp.sin(angle)
+
+
 def row_dft(matrix, source, held):
     for i in range(0, 8, 2):
         pair = jnp.concatenate([source(i), source(i + 1)], axis=1)
@@ -194,10 +201,10 @@
 
 
 def columns_kernel(
-    place, got, chirp_re, chirp_im, outer_re, outer_im, inner_re, inner_im, last_re, last_im, split, lanes_dft,
-    pick, terrain, out, token, work, held, mid,
+    place, got, chirp_re, chirp_im, outer_re, outer_im, last_re, last_im, split, lanes_dft,
+    pick, terrain, seen, turned, out, token, work, held, mid,
 ):
-    e = place[0]
+    e, f = place[0], place[1]
     token[...] = jnp.zeros_like(token)
     for group in range(8):
         low = 8 * group
@@ -214,7 +221,7 @@
             work[re_rows(i, low), :] = r
             work[im_rows(i, low), :] = m
     row_dft(split, block_of(work), held)
-    ir, ii = inner_re[...], inner_im[...]
+    ir, ii = inner_table()
     for i in range(8):
         at = slice(i * 64, i * 64 + 64)
         r, m = cmul(held[i * 128 : i * 128 + 64, :], held[i * 128 + 64 : i * 128 + 128, :], ir, ii)
@@ -229,8 +236,27 @@
     lows = pltpu.roll(
         jnp.broadcast_to(terrain[...].astype(jnp.float32), (8, LANES)), lax.rem(LANES + 16 - 16 * e, LANES), 1
     )
-    aux = jnp.where(lane8 < 16, picks, jnp.where(lane8 < 32, lows, 0.0))
-    out[pl.ds(2, ROWS, stride=3), :] = jnp.broadcast_to(aux[None], (PA, 8, LANES)).reshape(ROWS, LANES)
+    common = jnp.where(lane8 < 16, picks, jnp.where(lane8 < 32, lows, 0.0))
+    head = jnp.zeros((8, LANES), jnp.float32)
+    tail = jnp.zeros((8, LANES), jnp.float32)
+    for s in range(2):
+        for j in range(2):
+            slot = 2 * s + j
+            part = turned.at[s][pl.ds(e + 8 * j, 8, stride=16), :]
+            here = lane8 // 16 == 4 + slot
+            head = jnp.where(here, shift(part, 64 + 16 * slot), head)
+            tail = jnp.where(here, shift(part, 80 + 16 * slot), tail)
+    lanes = lane_of((64, LANES))
+    rows = row_of((64, LANES))
+    right = lax.rem(f + 1, PA)
+    left = lax.rem(f + PA - 1, PA)
+    for i in range(8):
+        spread_tail = jnp.broadcast_to(tail[i : i + 1, :], (64, LANES))
+        spread_head = jnp.broadcast_to(head[i : i + 1, :], (64, LANES))
+        edge = jnp.where(rows == right, spread_tail, jnp.where(rows == left, spread_head, 0.0))
+        strip = jnp.concatenate([shift(seen[...], 32 - 16 * i), jnp.zeros((48, LANES), jnp.float32)], axis=0)
+        both = jnp.where(lanes < 32, jnp.broadcast_to(common[0:1, :], (64, LANES)), jnp.where(lanes < 48, strip, 0.0))
+        out[pl.ds(i * 192 + 2, 64, stride=3), :] = jnp.where(lanes < 64, both, edge)
 
 
 def select_profile(picks, table):
@@ -244,7 +270,7 @@
 
 def rows_kernel(
     place, got, split, tile, outer_re, outer_im, lanes_dft, back_re, back_im, inner_re, inner_im,
-    screen_re, screen_im, out, token, work, held, mid, picks, lows, low_strip,
+    screen_re, screen_im, out, token, edge, work, held, mid, picks, lows, low_strip,
 ):
     e, f = place[0], place[1]
     token[...] = jnp.zeros_like(token)
@@ -255,6 +281,13 @@
         )
 
     row_dft(split, received, held)
+    rows = row_of((64, LANES))
+    left = lax.rem(f + PA - 1, PA)
+    right = lax.rem(f + 1, PA)
+    for i in range(8):
+        aux = got[pl.ds(i * 192 + 2, 64, stride=3), :]
+        edge[i : i + 1, :] = jnp.sum(jnp.where(rows == left, aux, 0.0), axis=0, keepdims=True)
+        edge[8 + i : 9 + i, :] = jnp.sum(jnp.where(rows == right, aux, 0.0), axis=0, keepdims=True)
     for i in range(8):
         parts = [got[pl.ds(i * 192 + 2 + 3 * o, 16, stride=12), :] for o in range(4)]
         upright = jnp.concatenate(parts + parts, axis=0).T
@@ -307,10 +340,8 @@
             work[re_rows(i, low), :] = r
             work[im_rows(i, low), :] = m
     row_dft(split, block_of(work), held)
-    for i in range(8):
-        out[pl.ds(i * 192, 64, stride=3), :] = held[i * 128 : i * 128 + 64, :]
-        out[pl.ds(i * 192 + 1, 64, stride=3), :] = held[i * 128 + 64 : i * 128 + 128, :]
     lane16 = lane_of((16, LANES))
+    lanes = lane_of((64, LANES))
     for i in range(8):
         block = low_strip[i * 64 : i * 64 + 64, :]
         upright = jnp.concatenate([block, block], axis=0).T
@@ -318,27 +349,71 @@
             re = shift(upright[:16], -16 * part)
             im = shift(upright[16:32], 16 - 16 * part)
             to = 4 * (i % 2) + part
-            out[pl.ds(to * 192 + 2 + 3 * (i // 2), 16, stride=12), :] = jnp.where(
+            picks[pl.ds(to * 64 + i // 2, 16, stride=4), :] = jnp.where(
                 lane16 < 16, re, jnp.where(lane16 < 32, im, 0.0)
             )
+    for i in range(8):
+        at = slice(i * 64, i * 64 + 64)
+        known = jnp.where(lanes < 48, got[pl.ds(i * 192 + 2, 64, stride=3), :], 0.0)
+        picks[at, :] = jnp.where(lanes < 32, picks[at, :], known)
+    for i in range(8):
+        source = 6 + i // 2 if i < 4 else (i - 4) // 2
+        amount = 1 if i < 4 else PA - 1
+        odd = i % 2
+        out[pl.ds(i * 256, 64, stride=4), :] = held[i * 128 : i * 128 + 64, :]
+        out[pl.ds(i * 256 + 1, 64, stride=4), :] = held[i * 128 + 64 : i * 128 + 128, :]
+        re = shift(held[source * 128 : source * 128 + 64, :], -8 * odd)
+        im = shift(held[source * 128 + 64 : source * 128 + 128, :], 8 - 8 * odd)
+        out[pl.ds(i * 256 + 3, 64, stride=4), :] = pltpu.roll(jnp.where(lanes % 16 < 8, re, im), amount, 0)
+        beyond = pltpu.roll(picks[source * 64 : source * 64 + 64, :], amount, 0)
+        moved = jnp.where(
+            lanes < 56,
+            shift(beyond, 48 - 8 * odd),
+            jnp.where(lanes < 64, shift(beyond, 40 - 8 * odd), shift(beyond, 32 - 8 * odd)),
+        )
+        own = picks[i * 64 : i * 64 + 64, :]
+        out[pl.ds(i * 256 + 2, 64, stride=4), :] = jnp.where(lanes < 48, own, jnp.where(lanes < 72, moved, 0.0))
 
 
 def final_kernel(
-    got, chirp_re, chirp_im, outer_re, outer_im, inner_re, inner_im, coef_re, coef_im, split, lanes_dft,
-    seen, range_pair, out, work, held, mid,
+    got, chirp_re, chirp_im, outer_re, outer_im, coef_re, coef_im, split, lanes_dft, seen, range_pair, out, token, work, held, mid,
 ):
+    token[...] = jnp.zeros_like(token)
+    ir, ii = inner_table()
+    for i in range(8):
+        at = slice(i * 64, i * 64 + 64)
+        value = got[pl.ds(i * 256 + 3, 64, stride=4), :]
+        r, m = cmul(value, shift(value, -8), chirp_re[at, :], chirp_im[at, :])
+        mid[at, :LANES] = r
+        mid[at, LANES:] = m
+    beyond = lane_product(mid[...], lanes_dft)
+    few = jnp.concatenate([split[0:16, :], split[64:80, :]], axis=0)
+    halo_re = jnp.zeros((16, LANES), jnp.float32)
+    halo_im = jnp.zeros((16, LANES), jnp.float32)
+    for i in range(0, 8, 2):
+        pair = []
+        for k in (i, i + 1):
+            at = slice(k * 64, k * 64 + 64)
+            pair.append(jnp.concatenate(cmul(beyond[at, :LANES], beyond[at, LANES:], ir, ii), axis=0))
+        result = product(few, data_right(jnp.concatenate(pair, axis=1)))
+        for k in range(2):
+            at = slice((i + k) * 64, (i + k) * 64 + 16)
+            part = result[:, k * LANES : (k + 1) * LANES]
+            r, m = cmul(part[:16], part[16:], outer_re[at, :], outer_im[at, :])
+            halo_re = halo_re + r
+            halo_im = halo_im + m
+    halo = abs(GAIN) * abs(GAIN) * (halo_re * halo_re + halo_im * halo_im)
     for i in range(8):
         at = slice(i * 64, i * 64 + 64)
         r, m = cmul(
-            got[pl.ds(i * 192, 64, stride=3), :],
-            got[pl.ds(i * 192 + 1, 64, stride=3), :],
+            got[pl.ds(i * 256, 64, stride=4), :],
+            got[pl.ds(i * 256 + 1, 64, stride=4), :],
             chirp_re[at, :],
             chirp_im[at, :],
         )
         mid[at, :LANES] = r
         mid[at, LANES:] = m
     result = lane_product(mid[...], lanes_dft)
-    ir, ii = inner_re[...], inner_im[...]
     for i in range(8):
         at = slice(i * 64, i * 64 + 64)
         r, m = cmul(result[at, :LANES], result[at, LANES:], ir, ii)
@@ -366,8 +441,13 @@
     lane16 = lane_of((16, LANES))
     first_re = jnp.zeros((16, LANES), jnp.float32)
     first_im = jnp.zeros((16, LANES), jnp.float32)
-    for i in range(8):
-        aux = got[pl.ds(i * 192 + 2, 16, stride=3), :]
+    tall_halo = []
+    for i in range(8):
+        aux = got[pl.ds(i * 256 + 2, 16, stride=4), :]
+        square = aux * aux
+        first = (shift(square, 32 - 48) + shift(square, 32 - 56)) * shift(aux, 32 - 64)
+        second = shift(halo, 40 - 16 * i) * shift(aux, 40 - 64)
+        tall_halo.append(jnp.where(lane16 < 40, first, jnp.where(lane16 < 48, second, 0.0)))
         here = lane16 // 16 == i
         first_re = jnp.where(here, shift(aux, 16 * i), first_re)
         first_im = jnp.where(here, shift(aux, 16 * i - 16), first_im)
@@ -375,7 +455,7 @@
     power = [seen[...] * (re * re + im * im) for re, im in parts]
     tall = []
     for g in range(8):
-        second = jnp.where(lane16 < 32, shift(power[1], 16 - 16 * g), 0.0)
+        second = jnp.where(lane16 < 32, shift(power[1], 16 - 16 * g), tall_halo[g])
         tall.append(jnp.where(lane16 < 16, shift(power[0], -16 * g), second))
     ranged = product(range_pair[...], data_right(jnp.concatenate(tall, axis=0)))
     for s in range(2):
@@ -387,18 +467,12 @@
             for i in range(8):
                 at = i * PART + 128 + 2 * (3 * s + n)
                 out[at : at + 2, :] = value[2 * i : 2 * i + 2, :]
-    for i in range(8):
-        out[i * PART + 140 : i * PART + 144, :] = jnp.zeros((4, LANES), jnp.float32)
-
-
-def strips_kernel(got, measured, edges, strips, rows):
-    parts = [got[e * PART + 128 : e * PART + 144, :] for e in range(8)]
-    for g, value in enumerate(trade(parts)):
-        rows[pl.ds(g, 16, stride=8), :] = value
-    for s in range(2):
-        edges[16 * s : 16 * s + 16, :] = rows[48 * s : 48 * s + 16, :]
-        edges[32 + 16 * s : 48 + 16 * s, :] = measured[s]
-        strips[32 * s : 32 * s + 32, :] = rows[48 * s + 16 : 48 * s + 48, :]
+    spread = jnp.zeros((16, LANES), jnp.float32)
+    for g in range(8):
+        spread = jnp.where(lane16 // 16 == g, shift(ranged[16 * g : 16 * g + 16, :], 16 * g - 32), spread)
+    for i in range(8):
+        out[i * PART + 140 : i * PART + 142, :] = spread[2 * i : 2 * i + 2, :]
+        out[i * PART + 142 : i * PART + 144, :] = jnp.zeros((2, LANES), jnp.float32)
 
 
 def unpack_kernel(got, field_out):
@@ -408,15 +482,43 @@
             field_out.at[0][pl.ds(64 * part + g, 8, stride=8), :] = value
 
 
-def sources_kernel(place, left, own, right, strips, mask, beams, sources):
-    near = jnp.concatenate([left[:32, :], own[:32, :], right[:32, :]], axis=1)
-    far = jnp.concatenate([left[32:, :], own[32:, :], right[32:, :]], axis=1)
-    back = product(data_left(jnp.concatenate([near, far], axis=1)), beams[...])
+def sources_kernel(place, got, mask, back_measured, beams, sources, rows):
+    parts = [got[e * PART + 128 : e * PART + 144, :] for e in range(8)]
+    for g, value in enumerate(trade(parts)):
+        rows[pl.ds(g, 16, stride=8), :] = value
     seen = mask[pl.ds(pl.multiple_of(16 * place[0], 16), 16), :].astype(jnp.float32)
     for s in range(2):
+        ranged = jnp.concatenate([rows[48 * s : 48 * s + 16, :], rows[96:112, :]], axis=1)
+        back = product(data_left(ranged), beams[6 * LANES * s : 6 * LANES * (s + 1), :]) - back_measured[s]
         for c in range(2):
-            at = 32 * s + 16 * c
-            sources[s, c] = 2.0 * seen * strips[at : at + 16, :] * back[16 * s : 16 * s + 16, :]
+            at = 48 * s + 16 + 16 * c
+            sources[s, c] = 2.0 * seen * rows[at : at + 16, :] * back
+
+
+def masks_kernel(place, terrain, mask, seen):
+    e = place[0]
+    lane16 = lane_of((16, LANES))
+    group = lane16 // 16
+    low = jnp.broadcast_to(terrain[...].astype(jnp.float32), (16, LANES))
+    total = jnp.zeros((16, LANES), jnp.float32)
+    for g in range(8):
+        amount = lax.rem(LANES + 16 * g - 16 * e, LANES)
+        above = (8 * row_of((16, LANES)) + g).astype(jnp.float32) >= low
+        part = jnp.where(above, mask[pl.ds(g, 16, stride=8), :].astype(jnp.float32), 0.0)
+        total = jnp.where(group == g, pltpu.roll(part, amount, 1), total)
+    seen[...] = total
+
+
+def measured_kernel(place, edge, turned, beam_mix, back_measured):
+    e = place[0]
+    for s in range(2):
+        for j in range(2):
+            slot = 2 * s + j
+            start = pl.multiple_of(16 * e + 8 * j, 8)
+            own = dot(turned.at[s][pl.ds(start, 8), :], beam_mix[LANES : 2 * LANES, :])
+            own = own + dot(shift(edge[0:8, :], 64 - 16 * slot), beam_mix[0:LANES, :])
+            own = own + dot(shift(edge[8:16, :], 64 - 16 * slot), beam_mix[2 * LANES : 3 * LANES, :])
+            back_measured[s, 8 * j : 8 * j + 8, :] = own
 
 
 def screen(height, angle):
@@ -441,14 +543,11 @@
 
 
 def prepare_kernel(
-    place, token, profile, pick, terrain, mask, chirp_re, chirp_im, coef_re, coef_im, seen, turned,
+    place, token, profile, pick, terrain, coef_re, coef_im, turned,
 ):
     e = place[0]
-    lane16 = lane_of((16, LANES))
-    group = lane16 // 16
     picks = jnp.zeros((8, LANES), jnp.float32)
     lows = jnp.zeros((8, LANES), jnp.float32)
-    masks = jnp.zeros((16, LANES), jnp.float32)
     group8 = lane_of((8, LANES)) // 16
     wide_pick = jnp.broadcast_to(pick[...].astype(jnp.float32), (8, LANES))
     wide_low = jnp.broadcast_to(terrain[...].astype(jnp.float32), (8, LANES))
@@ -456,9 +555,6 @@
         amount = lax.rem(LANES + 16 * g - 16 * e, LANES)
         picks = jnp.where(group8 == g, pltpu.roll(wide_pick, amount, 1), picks)
         lows = jnp.where(group8 == g, pltpu.roll(wide_low, amount, 1), lows)
-        part = mask[pl.ds(g, 16, stride=8), :].astype(jnp.float32)
-        masks = jnp.where(group == g, pltpu.roll(part, amount, 1), masks)
-    seen[...] = masks
     square_row = row_of((LANES, LANES))
     square_lane = lane_of((LANES, LANES))
     wanted = jnp.broadcast_to(picks[0:1, :], (LANES, LANES))
@@ -469,17 +565,20 @@
         turned[LANES * n : LANES * (n + 1), :] = jnp.concatenate([block] * 8, axis=0).T
     lanes = lane_of((64, LANES))
     rows = row_of((64, LANES))
-    for i in range(8):
+
+    @pl.loop(0, 8)
+    def block(i):
         mixed = jnp.zeros((64, LANES), jnp.float32)
         for g in range(8):
             mixed = jnp.where(lanes // 16 == g, turned[pl.ds(512 * i + g, 64, stride=8), :], mixed)
         height = 512 * i + 8 * rows + lanes // 16
-        sr, si = screen(height, dot(mixed, onehot))
+        g = lanes // 16
+        steps = (64 * rows * rows + g * g + 1024 * i * g + 16 * rows * g) % (2 * NH)
+        sr, si = screen(height, dot(mixed, onehot) + steps.astype(jnp.float32) * (math.pi / NH))
         above = height.astype(jnp.float32) >= jnp.broadcast_to(lows[0:1, :], (64, LANES))
-        at = slice(i * 64, i * 64 + 64)
-        r, m = cmul(jnp.where(above, sr, 0.0), jnp.where(above, si, 0.0), chirp_re[at, :], chirp_im[at, :])
-        coef_re[at, :] = r
-        coef_im[at, :] = m
+        at = pl.ds(pl.multiple_of(i * 64, 64), 64)
+        coef_re[at, :] = jnp.where(above, sr, 0.0)
+        coef_im[at, :] = jnp.where(above, si, 0.0)
 
 
 def turns(steps, modulus):
@@ -495,12 +594,9 @@
 
 def height_tables(e, f, zero):
     i, j, g, t = digits()
-    row = lax.broadcasted_iota(jnp.int32, (PA, LANES), 0)
-    group = lax.broadcasted_iota(jnp.int32, (PA, LANES), 1) // 16
     return (
         turns(64 * j * j + g * g + 1024 * i * g + 16 * j * g + zero, 2 * NH),
         turns(zero - i * (8 * j + g), NH),
-        turns(zero - row * group, 512),
         turns(
             2 * (i * i + 64 * j * j + 16 * i * j + 1024 * i * g)
             + INV * ((256 * e * e + t * t + 4096 * e * f + 256 * f * t + 32 * e * t) % (2 * NA))
@@ -527,25 +623,32 @@
     return jnp.sum(jnp.where(hit, taps, 0.0), axis=-1)
 
 
-def clutter_tables(pulse, beam, measured, eh):
+def clutter_tables(pulse, beam, measured):
     half = (pulse.shape[0] - 1) // 2
     row = lax.broadcasted_iota(jnp.int32, (BOT, BOT), 0)
     col = lax.broadcasted_iota(jnp.int32, (BOT, BOT), 1)
     adjoint = band(pulse, row - col + half)
     moved = adjoint.reshape(16, 8, BOT).swapaxes(0, 1).reshape(BOT, BOT)
     range_pair = jnp.einsum("ir,hr->ih", moved, moved, precision=HIGHEST)
-    own = lax.dynamic_slice_in_dim(adjoint, 16 * eh, 16, 0)
-    turned = jnp.einsum("hr,sra->sha", own, measured, precision=HIGHEST)
+    turned = jnp.einsum("hr,sra->sha", adjoint, measured, precision=HIGHEST)
     taps = beam.shape[0]
     reach = (taps - 1) // 2
-    at = lax.broadcasted_iota(jnp.int32, (3 * LANES, LANES), 0) - LANES
+    row = lax.broadcasted_iota(jnp.int32, (3 * LANES, LANES), 0)
     col = lax.broadcasted_iota(jnp.int32, (3 * LANES, LANES), 1)
+    block, inside = row // LANES, row % LANES
+    at = jnp.where(block == 0, inside - 16, jnp.where(block == 1, inside, inside + LANES))
+    beam_mix = band(beam, jnp.where((block == 1) | (inside < 16), col - at + reach, -1))
     first = lax.broadcasted_iota(jnp.int32, (taps, 2 * taps - 1), 0)
     ahead = lax.broadcasted_iota(jnp.int32, (taps, 2 * taps - 1), 1) - (taps - 1)
     auto = jnp.sum(beam[:, None] * band(beam, first + ahead), axis=0)
-    pair = band(auto, at - col + taps - 1)
-    back = band(beam, col - at + reach)
-    return matrix_left(range_pair), turned, matrix_right(jnp.concatenate([pair, -back], axis=0))
+    row = lax.broadcasted_iota(jnp.int32, (2 * LANES, LANES), 0)
+    col = lax.broadcasted_iota(jnp.int32, (2 * LANES, LANES), 1)
+    inside = row % LANES
+    owner, step = inside // 16, (inside // 8) % 2
+    halo = jnp.where(owner < 4, 8 * owner - 32, 8 * owner + 96) + inside % 8
+    pair = band(auto, jnp.where(row < LANES, row, halo) - col + taps - 1)
+    beams = [matrix_right(jnp.where((row < LANES) | (step == s), pair, 0.0)) for s in range(2)]
+    return matrix_left(range_pair), turned, beam_mix, jnp.concatenate(beams, axis=0)
 
 
 VMEM = pl.BlockSpec(memory_space=pltpu.VMEM)
@@ -603,9 +706,9 @@
     return moved.reshape(2 * ROWS, LANES)
 
 
-def stage_columns(place, got, heights, pick, terrain, **kw):
-    chirp, outer, inner, last = heights
-    args = (got, *chirp, *outer, *inner, *last, row_matrix(1), height_lanes(), pick[None], terrain[None])
+def stage_columns(place, got, heights, pick, terrain, seen, turned, **kw):
+    chirp, outer, last = heights
+    args = (got, *chirp, *outer, *last, row_matrix(1), height_lanes(), pick[None], terrain[None], seen, turned)
     return call(columns_kernel, (f32(3 * ROWS, LANES), f32(8, LANES)), WORK, args, place, **kw)
 
 
@@ -613,17 +716,13 @@
     outer, inner, back = azimuths
     far = (row_matrix(INV), tiles(), *outer, azimuth_lanes(), *back)
     args = (got, *far, *inner, *screen)
-    return call(rows_kernel, (f32(3 * ROWS, LANES), f32(8, LANES)), WORK + [(ROWS, LANES)] * 3, args, place, **kw)
+    return call(rows_kernel, (f32(4 * ROWS, LANES), f32(8, LANES), f32(16, LANES)), WORK + [(ROWS, LANES)] * 3, args, place, **kw)
 
 
 def stage_final(got, heights, coef, seen, range_pair, **kw):
-    _, outer, inner, chirp = heights
-    args = (got, *chirp, *outer, *inner, *coef, row_matrix(1), height_lanes(), seen, range_pair)
-    return call(final_kernel, f32(8 * PART, LANES), WORK, args, **kw)
-
-
-def stage_strips(got, turned, **kw):
-    return call(strips_kernel, (f32(64, LANES), f32(64, LANES)), [(BOT, LANES)], (got, turned), **kw)
+    _, outer, chirp = heights
+    args = (got, *chirp, *outer, *coef, row_matrix(1), height_lanes(), seen, range_pair)
+    return call(final_kernel, (f32(8 * PART, LANES), f32(8, LANES)), WORK, args, **kw)
 
 
 def stage_unpack(got, **kw):
@@ -635,22 +734,31 @@
     )
 
 
-def stage_sources(place, left, own, right, strips, mask, beams, **kw):
-    return call(sources_kernel, f32(2, 2, 16, LANES), [], (left, own, right, strips, mask, beams), place, **kw)
+def stage_sources(place, got, mask, back_measured, beams, **kw):
+    args = (got, mask, back_measured, beams)
+    return call(sources_kernel, f32(2, 2, 16, LANES), [(BOT, LANES)], args, place, **kw)
+
+
+def stage_masks(place, terrain, mask, **kw):
+    return call(masks_kernel, f32(16, LANES), [], (terrain[None], mask), place, cost=200_000, **kw)
+
+
+def stage_measured(place, edge, turned, beam_mix, **kw):
+    return call(measured_kernel, f32(2, 16, LANES), [], (edge, turned, beam_mix), place, cost=200_000, **kw)
 
 
 def stage_profiles(place, token, profile, **kw):
     return call(profiles_kernel, (f32(16, LANES), f32(16, LANES)), [], (token, profile), place, cost=200_000, **kw)
 
 
-def stage_prepare(place, token, profile, pick, terrain, mask, heights, **kw):
-    outs = (f32(ROWS, LANES), f32(ROWS, LANES), f32(16, LANES))
-    args = (token, profile, pick[None], terrain[None], mask, *heights[0])
+def stage_prepare(place, token, profile, pick, terrain, **kw):
+    outs = (f32(ROWS, LANES), f32(ROWS, LANES))
+    args = (token, profile, pick[None], terrain[None])
     return call(prepare_kernel, outs, [(NH, LANES)], args, place, **kw)
 
 
 def swap_all(rows):
-    shaped = rows.reshape(ROWS, 1, 3 * LANES)
+    shaped = rows.reshape(ROWS, 1, rows.shape[0] // ROWS * LANES)
     moved = lax.all_to_all(shaped, ("ha", "az"), split_axis=0, concat_axis=0, tiled=True)
     return moved.reshape(rows.shape)
 
@@ -662,23 +770,22 @@
 
 def local(field, terrain, profile_pick, profile_table, clutter_mask, pulse, beam, measured):
     place = "here"
-    range_pair, turned, beams = clutter_tables(pulse, beam, measured, lax.axis_index("ha"))
+    range_pair, turned, beam_mix, beams = clutter_tables(pulse, beam, measured)
     e, f = lax.axis_index("ha"), lax.axis_index("az")
     got = swap_heights(stage_pack(field))
-    sent, token = stage_columns(place, got, height_tables(e, f, 0), profile_pick, terrain)
+    seen = stage_masks(place, terrain, clutter_mask)
+    sent, token = stage_columns(place, got, height_tables(e, f, 0), profile_pick, terrain, seen, turned)
     azimuths = azimuth_tables(token[0, 0].astype(jnp.int32))
     screens = stage_profiles(place, token, profile_table)
     got = swap_all(sent)
-    sent, token = stage_rows(place, got, azimuths, screens)
+    sent, token, edge = stage_rows(place, got, azimuths, screens)
     heights = height_tables(e, f, token[0, 0].astype(jnp.int32))
-    prepared = stage_prepare(place, token, profile_table, profile_pick, terrain, clutter_mask, heights)
+    coef = stage_prepare(place, token, profile_table, profile_pick, terrain)
+    back_measured = stage_measured(place, edge, turned, beam_mix)
     got = swap_all(sent)
-    got = swap_heights(stage_final(got, heights, prepared[0:2], prepared[2], range_pair))
-    edges, strips = stage_strips(got, turned)
-    left = lax.ppermute(edges, "az", [(i, (i + 1) % PA) for i in range(PA)])
-    right = lax.ppermute(edges, "az", [((i + 1) % PA, i) for i in range(PA)])
-    field_out = stage_unpack(got)
-    return field_out, stage_sources(place, left, edges, right, strips, clutter_mask, beams)
+    sent, _ = stage_final(got, heights, coef, seen, range_pair)
+    got = swap_heights(sent)
+    return stage_unpack(got), stage_sources(place, got, clutter_mask, back_measured, beams)
 
 
 def solution(mesh):

time: 156 us -> 149 us (0.955)
  starting transfers between devices: 54.2 us -> 41.4 us
  Pallas kernels: 15.8 us -> 19.4 us
    ppermute x2 -> x0, starting transfers between devices: 13.4 us -> none  [the longest x1 10.1 us: local(): right = lax.ppermute(edges, 'az', [((i + 1) % PA, i) for i in range(PA)])]
    pallas_call x7 -> x8, Pallas kernels: 9.98 us -> 13.5 us  [call(): pl.pallas_call(kernel, out_shape=outs, in_specs=specs, out_specs=jax.tree...]
    sin x6 -> x4, other arithmetic: 9.78 us -> 8.42 us  [turns(): return (jnp.cos(angle), jnp.sin(angle))]
  transfers between devices with their start and end apart: 6 -> 4, of which waited for: 4 -> 4; matrix products, arithmetic and copies ran while one was open for 9% -> 11% of each run, Pallas kernels for 3% -> 3%
where the time goes in v5:
time: 149 us; the launch traced here: 148 us
  waiting for transfers between devices  66.5 us (45%)
  starting transfers between devices  41.4 us (28%)
  Pallas kernels  19.4 us (13%)
  other arithmetic  14.1 us (9%)
  local copies, waits for them, and re-layouts  3.63 us (2%)
  between operations  2.88 us (2%)
    all_to_all x2, waiting for transfers between devices, swap_all(): lax.all_to_all(shaped, ('ha', 'az'), split_axis=0, concat_axis=0, tiled=T...  43.4 us
    all_to_all x2, starting transfers between devices, swap_all(): lax.all_to_all(shaped, ('ha', 'az'), split_axis=0, concat_axis=0, tiled=T...  26.1 us
    all_to_all x2, waiting for transfers between devices, swap_heights(): lax.all_to_all(shaped, 'ha', split_axis=0, concat_axis=0, tiled=True)  23.1 us
    all_to_all x2, starting transfers between devices, swap_heights(): lax.all_to_all(shaped, 'ha', split_axis=0, concat_axis=0, tiled=True)  15.3 us
    pallas_call x8, Pallas kernels, call(): pl.pallas_call(kernel, out_shape=outs, in_specs=specs, out_specs=jax.tree...  13.5 us
    sin x4, other arithmetic, turns(): return (jnp.cos(angle), jnp.sin(angle))  8.42 us
    pallas_call x2, Pallas kernels, gridded(): pl.pallas_call(kernel, out_shape=outs, grid=(2, 2), in_specs=[pl.BlockSpe...  5.83 us
  transfers between devices with their start and end apart: 4, of which 4 were waited for; matrix products, arithmetic and copies ran while one was open for 11% of the time, Pallas kernels for 3%

profile of v5, /device:TPU:1, one launch (start us, length us, event | category | flops | bytes accessed | tf_op | source)
XLA Modules:
  0.0 148.4 jit_solution(15464601075128570241)
XLA Ops:
  0.6 0.0 copy-start
  0.6 0.0 copy-start.11
  0.7 3.7 %shard_map.158 = f32[8,128,128]{2,1,0:T(8,128)} custom-call(f32[2,512,128]{2,1,0:T(8,128)} %field.1), custom_call_target="tpu_custom_call" | custom-call | flops 200000000 | bytes 2000000 | tf_op jit(solution)/shard_map/pallas_call | solution.py:688
  4.4 10.2 %all-to-all-start = ((f32[8,128,128]{2,1,0:T(8,128)}), f32[8,128,128]{2,1,0:T(8,128)S(1)}, u32[]{:S(2)}, u32[]{:S(2)}) async-start(f32[8,128,128]{2,1,0:T(8,128)} %shard_map.158), calls=%async_computation | async-start | bytes 1048576 | tf_op jit(solution)/shard_map/all_to_all | solution.py:768
  14.6 0.0 copy-start.53
  14.6 0.0 copy-start.37
  14.7 0.0 copy-start.23
  14.7 0.0 copy-start.25
  14.7 0.0 copy-done.11
  14.8 0.0 copy-done.6
  14.8 0.1 shard_map.159.refs_11_.seen
  14.9 0.0 copy-start.1
  14.9 0.0 copy-start.2
  15.0 0.0 copy-start.13
  15.0 0.5 select_reduce_fusion.2
  15.4 0.3 convolution_bitcast_fusion.refs_12_.refs_1_
  15.7 3.5 %fusion.74 = (f32[512,128]{1,0:T(8,128)S(1)}, f32[512,128]{1,0:T(8,128)S(1)}, f32[512,128]{1,0:T(8,128)S(1)}, f32[512,128]{1,0:T(8,128)S(1)}, f32[512,128]{1,0:T(8,128)S(1)}, /*index=5*/f32[512,128]{1,0:T(8,128)S(1)}) fusion(s32[]{:T(128)S(6)} %mul.251, s32[]{:T(128)S(6)} %mul.248, s32[]{:T(128)S(6)} %mul.247, s32[128]{0:T(128)S(1)} %get-tuple-element.51, ...), kind=kLoop, calls=%fused_computation.161 | loop fusion | flops 5505024 | bytes 1584400 | tf_op jit(solution)/shard_map/sin | solution.py:586
  19.3 9.7 %all-to-all-done = f32[8,128,128]{2,1,0:T(8,128)S(1)} async-done(((f32[8,128,128]{2,1,0:T(8,128)}), f32[8,128,128]{2,1,0:T(8,128)S(1)}, u32[]{:S(2)}, u32[]{:S(2)}) %all-to-all-start) | async-done | bytes 524320 | tf_op jit(solution)/shard_map/all_to_all | solution.py:768
  29.0 1.8 %shard_map.160 = (f32[1536,128]{1,0:T(8,128)}, f32[8,128]{1,0:T(8,128)S(1)}) custom-call(f32[1024,128]{1,0:T(8,128)S(1)} %bitcast.26, f32[512,128]{1,0:T(8,128)S(1)} %get-tuple-element.39.refs_1_, f32[512,128]{1,0:T(8,128)S(1)} %get-tuple-element.36.refs_2_, f32[512,128]{1,0:T(8,128)S(1)} %get-tuple-element.38.refs_3_, ...), custom_call_target="tpu_custom_call" | custom-call | flops 200000000 | bytes 2000000 | tf_op jit(solution)/shard_map/pallas_call | solution.py:672
  30.8 16.3 %all-to-all-start.1 = ((f32[512,1,384]{2,1,0:T(1,128)}), f32[512,1,384]{2,1,0:T(1,128)S(1)}, u32[]{:S(2)}, u32[]{:S(2)}) async-start(f32[512,1,384]{2,1,0:T(1,128)} %bitcast.5), calls=%async_computation.1 | async-start | bytes 1572864 | tf_op jit(solution)/shard_map/all_to_all | solution.py:762
  47.1 0.0 copy-start.3
  47.1 0.0 copy-start.9
  47.1 0.0 copy-start.10
  47.2 0.6 iota_shift-right-logical_fusion
  47.8 0.6 fusion.89
  48.4 0.2 select_reduce_fusion.3
  48.5 0.1 multiply_reduce_fusion
  48.6 0.5 slice.6
  49.8 0.2 shard_map.161
  50.0 0.1 fusion.92
  50.2 2.5 %fusion.64 = (f32[512,128]{1,0:T(8,128)S(1)}, f32[512,128]{1,0:T(8,128)S(1)}, f32[512,128]{1,0:T(8,128)S(1)}, f32[512,128]{1,0:T(8,128)S(1)}) fusion(s32[]{:T(128)} %bitcast.7, s32[128]{0:T(128)S(1)} %get-tuple-element.51, s32[128]{0:T(128)S(1)} %get-tuple-element.52, pred[128]{0:T(512)(128)(4,1)S(1)} %get-tuple-element.48, s32[512]{0:T(512)S(1)} %get-tuple-element.42, ...), kind=kLoop, calls=%fused_computation.151 | loop fusion | flops 3735552 | bytes 1058948 | tf_op jit(solution)/shard_map/sin | solution.py:586
  52.7 21.6 %all-to-all-done.1 = f32[512,1,384]{2,1,0:T(1,128)S(1)} async-done(((f32[512,1,384]{2,1,0:T(1,128)}), f32[512,1,384]{2,1,0:T(1,128)S(1)}, u32[]{:S(2)}, u32[]{:S(2)}) %all-to-all-start.1) | async-done | bytes 786464 | tf_op jit(solution)/shard_map/all_to_all | solution.py:762
  74.3 3.3 %shard_map.162 = (f32[2048,128]{1,0:T(8,128)}, f32[8,128]{1,0:T(8,128)S(1)}, f32[16,128]{1,0:T(8,128)S(1)}) custom-call(f32[1536,128]{1,0:T(8,128)S(1)} %bitcast.25, bf16[128,384]{1,0:T(8,128)(2,1)S(1)} %copy-done.10, bf16[128,512]{1,0:T(8,128)(2,1)S(1)} %copy-done.9, f32[512,128]{1,0:T(8,128)S(1)} %get-tuple-element.35.refs_3_, ...), custom_call_target="tpu_custom_call" | custom-call | flops 200000000 | bytes 2000000 | tf_op jit(solution)/shard_map/pallas_call | solution.py:672
  77.5 9.8 %all-to-all-start.2 = ((f32[512,1,512]{2,1,0:T(1,128)}), f32[512,1,512]{2,1,0:T(1,128)S(1)}, u32[]{:S(2)}, u32[]{:S(2)}) async-start(f32[512,1,512]{2,1,0:T(1,128)} %bitcast.8), calls=%async_computation.2 | async-start | bytes 2097152 | tf_op jit(solution)/shard_map/all_to_all | solution.py:762
  87.4 0.0 copy-start.8
  87.4 0.0 copy-start.12
  87.4 0.0 copy-start.14
  87.5 0.3 reduce-precision_convert_fusion.2
  87.9 0.2 fusion.57
  88.1 0.9 select_reduce_fusion
  89.0 0.2 constant_dynamic-update-slice_fusion.3
  89.3 0.3 constant_dynamic-update-slice_fusion.2
  89.5 0.3 fusion.81
  89.8 0.3 constant_dynamic-update-slice_fusion.1
  90.1 0.5 slice.7
  91.3 0.0 copy-start.16
  91.3 0.7 copy-done.16
  92.0 3.5 %shard_map.163 = (f32[512,128]{1,0:T(8,128)S(1)}, f32[512,128]{1,0:T(8,128)S(1)}) custom-call(f32[8,128]{1,0:T(8,128)S(1)} %copy-done.16, f32[16,4096]{1,0:T(8,128)S(1)} %copy-done.8, s32[1,128]{1,0:T(1,128)S(1)} %bitcast.31, s32[1,128]{1,0:T(1,128)S(1)} %bitcast.29), custom_call_target="tpu_custom_call" | custom-call | flops 200000000 | bytes 2000000 | tf_op jit(solution)/shard_map/pallas_call | solution.py:672
  95.5 0.0 copy-start.4
  95.5 0.7 copy-done.4
  96.3 2.3 %fusion.72 = (f32[512,128]{1,0:T(8,128)S(1)}, f32[512,128]{1,0:T(8,128)S(1)}, f32[512,128]{1,0:T(8,128)S(1)}, f32[512,128]{1,0:T(8,128)S(1)}) fusion(s32[128]{0:T(128)S(1)} %copy-done.52, s32[128]{0:T(128)S(1)} %copy-done.54, pred[128]{0:T(512)(128)(4,1)S(1)} %copy-done.56, s32[512]{0:T(512)S(1)} %copy-done.26, s32[512]{0:T(512)S(1)} %copy-done.28, ...), kind=kLoop, calls=%fused_computation.159 | loop fusion | flops 4325376 | bytes 1060116 | tf_op jit(solution)/shard_map/sin | solution.py:586
  98.6 21.9 %all-to-all-done.2 = f32[512,1,512]{2,1,0:T(1,128)S(1)} async-done(((f32[512,1,512]{2,1,0:T(1,128)}), f32[512,1,512]{2,1,0:T(1,128)S(1)}, u32[]{:S(2)}, u32[]{:S(2)}) %all-to-all-start.2) | async-done | bytes 1048608 | tf_op jit(solution)/shard_map/all_to_all | solution.py:762
  120.5 0.9 copy-done.5
  121.4 2.9 %shard_map.164 = (f32[1152,128]{1,0:T(8,128)}, f32[8,128]{1,0:T(8,128)}) custom-call(f32[2048,128]{1,0:T(8,128)S(1)} %bitcast.24, f32[512,128]{1,0:T(8,128)S(1)} %get-tuple-element.30.chirp_re, f32[512,128]{1,0:T(8,128)S(1)} %get-tuple-element.31.chirp_im, f32[512,128]{1,0:T(8,128)S(1)} %get-tuple-element.29.outer_re, ...), custom_call_target="tpu_custom_call" | custom-call | flops 200000000 | bytes 2000000 | tf_op jit(solution)/shard_map/pallas_call | solution.py:672
  124.4 0.0 copy-start.50
  124.4 5.0 %all-to-all-start.3 = ((f32[8,144,128]{2,1,0:T(8,128)}), f32[8,144,128]{2,1,0:T(8,128)S(1)}, u32[]{:S(2)}, u32[]{:S(2)}) async-start(f32[8,144,128]{2,1,0:T(8,128)} %bitcast.14), calls=%async_computation.3 | async-start | bytes 1179648 | tf_op jit(solution)/shard_map/all_to_all | solution.py:768
  129.5 0.3 constant_dynamic-update-slice_fusion
  129.7 0.3 fusion.80.refs_3_
  130.1 0.4 fusion.49
  130.4 0.7 select_reduce_fusion.1.refs_2_
  131.1 0.8 shard_map.166.refs_2_
  131.9 13.4 %all-to-all-done.3.got = f32[8,144,128]{2,1,0:T(8,128)S(1)} async-done(((f32[8,144,128]{2,1,0:T(8,128)}), f32[8,144,128]{2,1,0:T(8,128)S(1)}, u32[]{:S(2)}, u32[]{:S(2)}) %all-to-all-start.3) | async-done | bytes 589856 | tf_op jit(solution)/shard_map/all_to_all | solution.py:768
  145.2 1.0 shard_map.167
  146.2 2.1 %shard_map.165 = f32[2,512,128]{2,1,0:T(8,128)} custom-call(f32[8,144,128]{2,1,0:T(8,128)S(1)} %all-to-all-done.3.got), custom_call_target="tpu_custom_call" | custom-call | flops 200000000 | bytes 2000000 | tf_op jit(solution)/shard_map/pallas_call | solution.py:688
  (108 shorter events, 0.3 us)
Async XLA Ops:
  0.6 14.8 %copy-start = (f32[2,128,128]{2,1,0:T(8,128)S(1)}, f32[2,128,128]{2,1,0:T(8,128)}, u32[]{:S(2)}) copy-start(f32[2,128,128]{2,1,0:T(8,128)} %param.22) | copy-start | bytes 393220
  0.6 14.1 %copy-start.11 = (s32[128]{0:T(128)S(1)}, s32[128]{0:T(128)}, u32[]{:S(2)}) copy-start(s32[128]{0:T(128)} %param.16) | copy-start | bytes 1540
  0.7 14.1 %copy-start.6 = (s32[128,128]{1,0:T(8,128)S(1)}, s32[128,128]{1,0:T(8,128)}, u32[]{:S(2)}) copy-start(s32[128,128]{1,0:T(8,128)} %refs_1_.7) | copy-start | bytes 196612
  0.7 14.3 %copy-start.57 = (f32[63]{0:T(128)S(1)}, f32[63]{0:T(128)}, u32[]{:S(2)}) copy-start(f32[63]{0:T(128)} %param.20) | copy-start | bytes 760
  4.4 24.6 %all-to-all-start = ((f32[8,128,128]{2,1,0:T(8,128)}), f32[8,128,128]{2,1,0:T(8,128)S(1)}, u32[]{:S(2)}, u32[]{:S(2)}) async-start(f32[8,128,128]{2,1,0:T(8,128)} %shard_map.158), calls=%async_computation | async-start | bytes 1048576 | tf_op jit(solution)/shard_map/all_to_all | solution.py:768
  14.6 4.6 %copy-start.51 = (s32[128]{0:T(128)}, s32[128]{0:T(128)S(1)}, u32[]{:S(2)}) copy-start(s32[128]{0:T(128)S(1)} %get-tuple-element.50) | copy-start | bytes 1540
  14.6 35.5 %copy-start.35 = (s32[128]{0:T(128)}, s32[128]{0:T(128)S(1)}, u32[]{:S(2)}) copy-start(s32[128]{0:T(128)S(1)} %get-tuple-element.51) | copy-start | bytes 1540
  14.6 4.6 %copy-start.53 = (s32[128]{0:T(128)}, s32[128]{0:T(128)S(1)}, u32[]{:S(2)}) copy-start(s32[128]{0:T(128)S(1)} %get-tuple-element.53) | copy-start | bytes 1540
  14.6 35.5 %copy-start.37 = (s32[128]{0:T(128)}, s32[128]{0:T(128)S(1)}, u32[]{:S(2)}) copy-start(s32[128]{0:T(128)S(1)} %get-tuple-element.52) | copy-start | bytes 1540
  14.7 4.6 %copy-start.55 = (pred[128]{0:T(512)(128)(4,1)}, pred[128]{0:T(512)(128)(4,1)S(1)}, u32[]{:S(2)}) copy-start(pred[128]{0:T(512)(128)(4,1)S(1)} %get-tuple-element.49) | copy-start | bytes 388
  14.7 35.5 %copy-start.39 = (pred[128]{0:T(512)(128)(4,1)}, pred[128]{0:T(512)(128)(4,1)S(1)}, u32[]{:S(2)}) copy-start(pred[128]{0:T(512)(128)(4,1)S(1)} %get-tuple-element.48) | copy-start | bytes 388
  14.7 35.4 %copy-start.23 = (s32[512]{0:T(512)}, s32[512]{0:T(512)S(1)}, u32[]{:S(2)}) copy-start(s32[512]{0:T(512)S(1)} %get-tuple-element.42) | copy-start | bytes 6148
  14.7 35.4 %copy-start.25 = (s32[512]{0:T(512)}, s32[512]{0:T(512)S(1)}, u32[]{:S(2)}) copy-start(s32[512]{0:T(512)S(1)} %get-tuple-element.43) | copy-start | bytes 6148
  14.7 35.4 %copy-start.27 = (s32[512]{0:T(512)}, s32[512]{0:T(512)S(1)}, u32[]{:S(2)}) copy-start(s32[512]{0:T(512)S(1)} %get-tuple-element.44) | copy-start | bytes 6148
  14.7 35.4 %copy-start.29 = (s32[512]{0:T(512)}, s32[512]{0:T(512)S(1)}, u32[]{:S(2)}) copy-start(s32[512]{0:T(512)S(1)} %get-tuple-element.45) | copy-start | bytes 6148
  14.9 35.3 %copy-start.45 = (pred[512]{0:T(512)(128)(4,1)}, pred[512]{0:T(512)(128)(4,1)S(1)}, u32[]{:S(2)}) copy-start(pred[512]{0:T(512)(128)(4,1)S(1)} %get-tuple-element.46) | copy-start | bytes 1540
  14.9 35.3 %copy-start.47 = (pred[512]{0:T(512)(128)(4,1)}, pred[512]{0:T(512)(128)(4,1)S(1)}, u32[]{:S(2)}) copy-start(pred[512]{0:T(512)(128)(4,1)S(1)} %get-tuple-element.47) | copy-start | bytes 1540
  14.9 14.1 %copy-start.1 = (bf16[512,256]{1,0:T(8,128)(2,1)S(1)}, bf16[512,256]{1,0:T(8,128)(2,1)}, u32[]{:S(2)}) copy-start(bf16[512,256]{1,0:T(8,128)(2,1)} %constant.317.refs_8_.lanes_dft) | copy-start | bytes 786436
  14.9 14.1 %copy-start.2 = (bf16[128,384]{1,0:T(8,128)(2,1)S(1)}, bf16[128,384]{1,0:T(8,128)(2,1)}, u32[]{:S(2)}) copy-start(bf16[128,384]{1,0:T(8,128)(2,1)} %constant.312.refs_7_.split) | copy-start | bytes 294916
  15.0 14.0 %copy-start.13 = (s32[128]{0:T(128)S(1)}, s32[128]{0:T(128)}, u32[]{:S(2)}) copy-start(s32[128]{0:T(128)} %param.17) | copy-start | bytes 1540
  30.8 17.6 %copy-start.49 = (f32[31]{0:T(128)S(1)}, f32[31]{0:T(128)}, u32[]{:S(2)}) copy-start(f32[31]{0:T(128)} %param.21) | copy-start | bytes 376
  30.8 19.0 %copy-start.7 = (f32[16,4096]{1,0:T(8,128)S(1)}, f32[16,4096]{1,0:T(8,128)}, u32[]{:S(2)}) copy-start(f32[16,4096]{1,0:T(8,128)} %refs_1_.6) | copy-start | bytes 786436
  30.8 43.5 %all-to-all-start.1 = ((f32[512,1,384]{2,1,0:T(1,128)}), f32[512,1,384]{2,1,0:T(1,128)S(1)}, u32[]{:S(2)}, u32[]{:S(2)}) async-start(f32[512,1,384]{2,1,0:T(1,128)} %bitcast.5), calls=%async_computation.1 | async-start | bytes 1572864 | tf_op jit(solution)/shard_map/all_to_all | solution.py:762
  47.1 27.2 %copy-start.3 = (bf16[512,256]{1,0:T(8,128)(2,1)S(1)}, bf16[512,256]{1,0:T(8,128)(2,1)}, u32[]{:S(2)}) copy-start(bf16[512,256]{1,0:T(8,128)(2,1)} %constant.328.refs_5_) | copy-start | bytes 786436
  47.1 27.2 %copy-start.9 = (bf16[128,512]{1,0:T(8,128)(2,1)S(1)}, bf16[128,512]{1,0:T(8,128)(2,1)}, u32[]{:S(2)}) copy-start(bf16[128,512]{1,0:T(8,128)(2,1)} %constant.323.refs_2_) | copy-start | bytes 393220
  47.1 27.1 %copy-start.10 = (bf16[128,384]{1,0:T(8,128)(2,1)S(1)}, bf16[128,384]{1,0:T(8,128)(2,1)}, u32[]{:S(2)}) copy-start(bf16[128,384]{1,0:T(8,128)(2,1)} %constant.322.refs_1_) | copy-start | bytes 294916
  47.1 42.7 %copy-start.19 = (s32[256]{0:T(256)}, s32[256]{0:T(256)S(1)}, u32[]{:S(2)}) copy-start(s32[256]{0:T(256)S(1)} %get-tuple-element.62) | copy-start | bytes 3076
  47.2 42.7 %copy-start.21 = (s32[256]{0:T(256)}, s32[256]{0:T(256)S(1)}, u32[]{:S(2)}) copy-start(s32[256]{0:T(256)S(1)} %get-tuple-element.63) | copy-start | bytes 3076
  77.5 12.5 %copy-start.15 = (f32[8,128]{1,0:T(8,128)}, f32[8,128]{1,0:T(8,128)S(1)}, u32[]{:S(2)}) copy-start(f32[8,128]{1,0:T(8,128)S(1)} %get-tuple-element.17.refs_0_) | copy-start | bytes 12292
  77.5 42.9 %all-to-all-start.2 = ((f32[512,1,512]{2,1,0:T(1,128)}), f32[512,1,512]{2,1,0:T(1,128)S(1)}, u32[]{:S(2)}, u32[]{:S(2)}) async-start(f32[512,1,512]{2,1,0:T(1,128)} %bitcast.8), calls=%async_computation.2 | async-start | bytes 2097152 | tf_op jit(solution)/shard_map/all_to_all | solution.py:762
  87.4 3.9 %copy-start.8 = (f32[16,4096]{1,0:T(8,128)S(1)}, f32[16,4096]{1,0:T(8,128)}, u32[]{:S(2)}) copy-start(f32[16,4096]{1,0:T(8,128)} %refs_1_.6) | copy-start | bytes 786436
  87.4 3.9 %copy-start.12 = (s32[128]{0:T(128)S(1)}, s32[128]{0:T(128)}, u32[]{:S(2)}) copy-start(s32[128]{0:T(128)} %param.16) | copy-start | bytes 1540
  87.4 3.9 %copy-start.14 = (s32[128]{0:T(128)S(1)}, s32[128]{0:T(128)}, u32[]{:S(2)}) copy-start(s32[128]{0:T(128)} %param.17) | copy-start | bytes 1540
  87.4 3.2 %copy-start.31 = (pred[256]{0:T(512)(128)(4,1)}, pred[256]{0:T(512)(128)(4,1)S(1)}, u32[]{:S(2)}) copy-start(pred[256]{0:T(512)(128)(4,1)S(1)} %get-tuple-element.60) | copy-start | bytes 772
  87.4 3.2 %copy-start.33 = (pred[256]{0:T(512)(128)(4,1)}, pred[256]{0:T(512)(128)(4,1)S(1)}, u32[]{:S(2)}) copy-start(pred[256]{0:T(512)(128)(4,1)S(1)} %get-tuple-element.61) | copy-start | bytes 772
  87.7 8.5 %copy-start.24 = (s32[512]{0:T(512)S(1)}, s32[512]{0:T(512)}, u32[]{:S(2)}) copy-start(s32[512]{0:T(512)} %copy-done.23) | copy-start | bytes 6148
  87.8 8.5 %copy-start.26 = (s32[512]{0:T(512)S(1)}, s32[512]{0:T(512)}, u32[]{:S(2)}) copy-start(s32[512]{0:T(512)} %copy-done.25) | copy-start | bytes 6148
  87.8 8.5 %copy-start.28 = (s32[512]{0:T(512)S(1)}, s32[512]{0:T(512)}, u32[]{:S(2)}) copy-start(s32[512]{0:T(512)} %copy-done.27) | copy-start | bytes 6148
  87.8 8.5 %copy-start.30 = (s32[512]{0:T(512)S(1)}, s32[512]{0:T(512)}, u32[]{:S(2)}) copy-start(s32[512]{0:T(512)} %copy-done.29) | copy-start | bytes 6148
  87.8 8.5 %copy-start.36 = (s32[128]{0:T(128)S(1)}, s32[128]{0:T(128)}, u32[]{:S(2)}) copy-start(s32[128]{0:T(128)} %copy-done.35) | copy-start | bytes 1540
  87.8 8.5 %copy-start.38 = (s32[128]{0:T(128)S(1)}, s32[128]{0:T(128)}, u32[]{:S(2)}) copy-start(s32[128]{0:T(128)} %copy-done.37) | copy-start | bytes 1540
  87.8 8.5 %copy-start.40 = (pred[128]{0:T(512)(128)(4,1)S(1)}, pred[128]{0:T(512)(128)(4,1)}, u32[]{:S(2)}) copy-start(pred[128]{0:T(512)(128)(4,1)} %copy-done.39) | copy-start | bytes 388
  87.8 8.5 %copy-start.46 = (pred[512]{0:T(512)(128)(4,1)S(1)}, pred[512]{0:T(512)(128)(4,1)}, u32[]{:S(2)}) copy-start(pred[512]{0:T(512)(128)(4,1)} %copy-done.45) | copy-start | bytes 1540
  87.8 8.5 %copy-start.48 = (pred[512]{0:T(512)(128)(4,1)S(1)}, pred[512]{0:T(512)(128)(4,1)}, u32[]{:S(2)}) copy-start(pred[512]{0:T(512)(128)(4,1)} %copy-done.47) | copy-start | bytes 1540
  87.8 8.5 %copy-start.52 = (s32[128]{0:T(128)S(1)}, s32[128]{0:T(128)}, u32[]{:S(2)}) copy-start(s32[128]{0:T(128)} %copy-done.51) | copy-start | bytes 1540
  87.8 8.5 %copy-start.54 = (s32[128]{0:T(128)S(1)}, s32[128]{0:T(128)}, u32[]{:S(2)}) copy-start(s32[128]{0:T(128)} %copy-done.53) | copy-start | bytes 1540
  87.8 8.5 %copy-start.56 = (pred[128]{0:T(512)(128)(4,1)S(1)}, pred[128]{0:T(512)(128)(4,1)}, u32[]{:S(2)}) copy-start(pred[128]{0:T(512)(128)(4,1)} %copy-done.55) | copy-start | bytes 388
  89.0 1.6 %copy-start.17 = (f32[256,128]{1,0:T(8,128)}, f32[256,128]{1,0:T(8,128)S(1)}, u32[]{:S(2)}) copy-start(f32[256,128]{1,0:T(8,128)S(1)} %select_reduce_fusion) | copy-start | bytes 393220
  91.3 0.7 copy-start.16
  95.5 0.7 copy-start.4
  120.5 1.0 copy-start.5
  124.3 5.1 %copy-start.18 = (f32[256,128]{1,0:T(8,128)S(1)}, f32[256,128]{1,0:T(8,128)}, u32[]{:S(2)}) copy-start(f32[256,128]{1,0:T(8,128)} %copy-done.17) | copy-start | bytes 393220
  124.3 5.1 %copy-start.20 = (s32[256]{0:T(256)S(1)}, s32[256]{0:T(256)}, u32[]{:S(2)}) copy-start(s32[256]{0:T(256)} %copy-done.19) | copy-start | bytes 3076
  124.3 5.1 %copy-start.22 = (s32[256]{0:T(256)S(1)}, s32[256]{0:T(256)}, u32[]{:S(2)}) copy-start(s32[256]{0:T(256)} %copy-done.21) | copy-start | bytes 3076
  124.3 5.1 %copy-start.32 = (pred[256]{0:T(512)(128)(4,1)S(1)}, pred[256]{0:T(512)(128)(4,1)}, u32[]{:S(2)}) copy-start(pred[256]{0:T(512)(128)(4,1)} %copy-done.31) | copy-start | bytes 772
  124.4 5.1 %copy-start.34 = (pred[256]{0:T(512)(128)(4,1)S(1)}, pred[256]{0:T(512)(128)(4,1)}, u32[]{:S(2)}) copy-start(pred[256]{0:T(512)(128)(4,1)} %copy-done.33) | copy-start | bytes 772
  124.4 5.7 %copy-start.41 = (s32[384]{0:T(512)S(1)}, s32[384]{0:T(512)}, u32[]{:S(2)}) copy-start(s32[384]{0:T(512)} %get-tuple-element.54) | copy-start | bytes 4612
  124.4 5.7 %copy-start.42 = (s32[384]{0:T(512)S(1)}, s32[384]{0:T(512)}, u32[]{:S(2)}) copy-start(s32[384]{0:T(512)} %get-tuple-element.55) | copy-start | bytes 4612
  124.4 5.7 %copy-start.43 = (s32[384]{0:T(512)S(1)}, s32[384]{0:T(512)}, u32[]{:S(2)}) copy-start(s32[384]{0:T(512)} %get-tuple-element.56) | copy-start | bytes 4612
  124.4 5.7 %copy-start.44 = (s32[384]{0:T(512)S(1)}, s32[384]{0:T(512)}, u32[]{:S(2)}) copy-start(s32[384]{0:T(512)} %get-tuple-element.57) | copy-start | bytes 4612
  124.4 6.0 %copy-start.50 = (f32[31]{0:T(128)S(1)}, f32[31]{0:T(128)}, u32[]{:S(2)}) copy-start(f32[31]{0:T(128)} %param.21) | copy-start | bytes 376
  124.4 20.8 %all-to-all-start.3 = ((f32[8,144,128]{2,1,0:T(8,128)}), f32[8,144,128]{2,1,0:T(8,128)S(1)}, u32[]{:S(2)}, u32[]{:S(2)}) async-start(f32[8,144,128]{2,1,0:T(8,128)} %bitcast.14), calls=%async_computation.3 | async-start | bytes 1179648 | tf_op jit(solution)/shard_map/all_to_all | solution.py:768

commit v6 on v5

--- a/solution.py
+++ b/solution.py
@@ -193,11 +193,24 @@
     return slice(i * 64 + low, i * 64 + low + 8)
 
 
-def pack_kernel(field, out):
-    for part in range(field.shape[1] // 64):
-        rows = [field.at[0][pl.ds(64 * part + g, 8, stride=8), :] for g in range(8)]
-        for e, value in enumerate(trade(rows)):
-            out[e, 8 * part : 8 * part + 8, :] = value
+def pack_kernel(field, out, near, made, came, left):
+    gets, puts = [], []
+    for n in range(8):
+        c, p = divmod(n, 4)
+        rows, mixed = pl.ds(128 * p, 128), pl.ds(64 * c + 16 * p, 16)
+        gets.append(pltpu.make_async_copy(field.at[c, rows, :], near.at[c, rows, :], came.at[n]))
+        puts.append(pltpu.make_async_copy(made.at[:, mixed, :], out.at[:, mixed, :], left.at[n]))
+        gets[n].start()
+    for n in range(8):
+        c, p = divmod(n, 4)
+        gets[n].wait()
+        for part in (2 * p, 2 * p + 1):
+            rows = [near.at[c][pl.ds(64 * part + g, 8, stride=8), :] for g in range(8)]
+            for e, value in enumerate(trade(rows)):
+                made[e, 64 * c + 8 * part : 64 * c + 8 * part + 8, :] = value
+        puts[n].start()
+    for put in puts:
+        put.wait()
 
 
 def columns_kernel(
@@ -475,14 +488,18 @@
         out[i * PART + 142 : i * PART + 144, :] = jnp.zeros((2, LANES), jnp.float32)
 
 
-def unpack_kernel(got, field_out):
-    for part in range(got.shape[1] // 8):
-        values = trade([got[e, 8 * part : 8 * part + 8, :] for e in range(8)])
-        for g, value in enumerate(values):
-            field_out.at[0][pl.ds(64 * part + g, 8, stride=8), :] = value
-
-
-def sources_kernel(place, got, mask, back_measured, beams, sources, rows):
+def finish_kernel(place, got, mask, back_measured, beams, field_out, sources, rows, made, left):
+    puts = []
+    for n in range(8):
+        c, p = divmod(n, 4)
+        for part in (2 * p, 2 * p + 1):
+            at = 64 * c + 8 * part
+            values = trade([got[e * PART + at : e * PART + at + 8, :] for e in range(8)])
+            for g, value in enumerate(values):
+                made.at[c][pl.ds(64 * part + g, 8, stride=8), :] = value
+        piece = pl.ds(128 * p, 128)
+        puts.append(pltpu.make_async_copy(made.at[c, piece, :], field_out.at[c, piece, :], left.at[n]))
+        puts[n].start()
     parts = [got[e * PART + 128 : e * PART + 144, :] for e in range(8)]
     for g, value in enumerate(trade(parts)):
         rows[pl.ds(g, 16, stride=8), :] = value
@@ -493,6 +510,8 @@
         for c in range(2):
             at = 48 * s + 16 + 16 * c
             sources[s, c] = 2.0 * seen * rows[at : at + 16, :] * back
+    for put in puts:
+        put.wait()
 
 
 def masks_kernel(place, terrain, mask, seen):
@@ -653,6 +672,7 @@
 
 VMEM = pl.BlockSpec(memory_space=pltpu.VMEM)
 SMEM = pl.BlockSpec(memory_space=pltpu.SMEM)
+FAR = pl.BlockSpec(memory_space=pl.ANY)
 
 
 def f32(*shape):
@@ -663,7 +683,7 @@
     return kernel((lax.axis_index("ha"), lax.axis_index("az")), *refs)
 
 
-def call(kernel, outs, scratch, args, place=None, cost=2_000_000, grant=GRANT, interpret=False):
+def call(kernel, outs, scratch, args, place=None, cost=2_000_000, grant=GRANT, out_specs=None, interpret=False):
     specs = [VMEM] * len(args)
     if place == "here":
         kernel = functools.partial(placed, kernel)
@@ -673,8 +693,8 @@
         kernel,
         out_shape=outs,
         in_specs=specs,
-        out_specs=jax.tree.map(lambda _: VMEM, outs),
-        scratch_shapes=[pltpu.VMEM(shape, jnp.float32) for shape in scratch],
+        out_specs=jax.tree.map(lambda _: VMEM, outs) if out_specs is None else out_specs,
+        scratch_shapes=[pltpu.VMEM(s, jnp.float32) if isinstance(s, tuple) else s for s in scratch],
         cost_estimate=pl.CostEstimate(flops=cost * 100, bytes_accessed=cost, transcendentals=0),
         compiler_params=pltpu.CompilerParams(vmem_limit_bytes=grant),
         interpret=interpret,
@@ -684,25 +704,22 @@
 WORK = [(2 * ROWS, LANES), (2 * ROWS, LANES), (ROWS, 2 * LANES)]
 
 
-def gridded(kernel, outs, value, in_block, out_block, in_map, out_map, grant, interpret=False):
-    return pl.pallas_call(
-        kernel,
-        out_shape=outs,
-        grid=(2, 2),
-        in_specs=[pl.BlockSpec(in_block, in_map)],
-        out_specs=pl.BlockSpec(out_block, out_map),
+def stage_pack(field, interpret=False):
+    moved = pl.pallas_call(
+        pack_kernel,
+        out_shape=f32(PH, 2 * PA, LANES),
+        in_specs=[FAR],
+        out_specs=FAR,
+        scratch_shapes=[
+            pltpu.VMEM((2, NH // PH, LANES), jnp.float32),
+            pltpu.VMEM((PH, 2 * PA, LANES), jnp.float32),
+            pltpu.SemaphoreType.DMA((8,)),
+            pltpu.SemaphoreType.DMA((8,)),
+        ],
         cost_estimate=pl.CostEstimate(flops=200_000_000, bytes_accessed=2_000_000, transcendentals=0),
-        compiler_params=pltpu.CompilerParams(vmem_limit_bytes=grant),
+        compiler_params=pltpu.CompilerParams(vmem_limit_bytes=WIDE_GRANT),
         interpret=interpret,
-    )(value)
-
-
-def stage_pack(field, **kw):
-    slab, mixed = (1, 256, LANES), (PH, 32, LANES)
-    outs = f32(PH, 2 * PA, LANES)
-    moved = gridded(
-        pack_kernel, outs, field, slab, mixed, lambda c, p: (c, p, 0), lambda c, p: (0, 2 * c + p, 0), WIDE_GRANT, **kw
-    )
+    )(field)
     return moved.reshape(2 * ROWS, LANES)
 
 
@@ -725,18 +742,11 @@
     return call(final_kernel, (f32(8 * PART, LANES), f32(8, LANES)), WORK, args, **kw)
 
 
-def stage_unpack(got, **kw):
-    slab, mixed = (1, 256, LANES), (PH, 32, LANES)
-    outs = f32(2, NH // PH, LANES)
-    value = got.reshape(PH, PART, LANES)
-    return gridded(
-        unpack_kernel, outs, value, mixed, slab, lambda c, p: (0, 2 * c + p, 0), lambda c, p: (c, p, 0), GRANT, **kw
-    )
-
-
-def stage_sources(place, got, mask, back_measured, beams, **kw):
+def stage_finish(place, got, mask, back_measured, beams, **kw):
     args = (got, mask, back_measured, beams)
-    return call(sources_kernel, f32(2, 2, 16, LANES), [(BOT, LANES)], args, place, **kw)
+    outs = (f32(2, NH // PH, LANES), f32(2, 2, 16, LANES))
+    scratch = [(BOT, LANES), (2, NH // PH, LANES), pltpu.SemaphoreType.DMA((8,))]
+    return call(finish_kernel, outs, scratch, args, place, out_specs=(FAR, VMEM), **kw)
 
 
 def stage_masks(place, terrain, mask, **kw):
@@ -785,7 +795,7 @@
     got = swap_all(sent)
     sent, _ = stage_final(got, heights, coef, seen, range_pair)
     got = swap_heights(sent)
-    return stage_unpack(got), stage_sources(place, got, clutter_mask, back_measured, beams)
+    return stage_finish(place, got, clutter_mask, back_measured, beams)
 
 
 def solution(mesh):

time: 149 us -> 149 us (level)
    pallas_call x2 -> x1, Pallas kernels: 5.83 us -> 3.49 us  [stage_pack(): pl.pallas_call(pack_kernel, out_shape=f32(PH, 2 * PA, LANES), in_specs=[F...]
    pallas_call x8, Pallas kernels: 13.5 us -> 15.4 us  [call(): pl.pallas_call(kernel, out_shape=outs, in_specs=specs, out_specs=jax.tree...]
where the time goes in v6:
time: 149 us; the launch traced here: 148 us
  waiting for transfers between devices  66.5 us (45%)
  starting transfers between devices  41.4 us (28%)
  Pallas kernels  18.9 us (13%)
  other arithmetic  14.1 us (9%)
  local copies, waits for them, and re-layouts  3.63 us (2%)
  between operations  3.06 us (2%)
    all_to_all x2, waiting for transfers between devices, swap_all(): lax.all_to_all(shaped, ('ha', 'az'), split_axis=0, concat_axis=0, tiled=T...  43.4 us
    all_to_all x2, starting transfers between devices, swap_all(): lax.all_to_all(shaped, ('ha', 'az'), split_axis=0, concat_axis=0, tiled=T...  26.1 us
    all_to_all x2, waiting for transfers between devices, swap_heights(): lax.all_to_all(shaped, 'ha', split_axis=0, concat_axis=0, tiled=True)  23.1 us
    pallas_call x8, Pallas kernels, call(): pl.pallas_call(kernel, out_shape=outs, in_specs=specs, out_specs=jax.tree...  15.4 us
    all_to_all x2, starting transfers between devices, swap_heights(): lax.all_to_all(shaped, 'ha', split_axis=0, concat_axis=0, tiled=True)  15.3 us
    sin x4, other arithmetic, turns(): return (jnp.cos(angle), jnp.sin(angle))  8.42 us
    pallas_call x1, Pallas kernels, stage_pack(): pl.pallas_call(pack_kernel, out_shape=f32(PH, 2 * PA, LANES), in_specs=[F...  3.49 us
  transfers between devices with their start and end apart: 4, of which 4 were waited for; matrix products, arithmetic and copies ran while one was open for 11% of the time, Pallas kernels for 3%

profile of v6, /device:TPU:1, one launch (start us, length us, event | category | flops | bytes accessed | tf_op | source)
XLA Modules:
  0.0 148.1 jit_solution(12670931223139623073)
XLA Ops:
  0.6 0.0 copy-start
  0.6 0.0 copy-start.11
  0.7 3.5 %shard_map.158 = f32[8,128,128]{2,1,0:T(8,128)} custom-call(f32[2,512,128]{2,1,0:T(8,128)} %field.1), custom_call_target="tpu_custom_call" | custom-call | flops 200000000 | bytes 2000000 | tf_op jit(solution)/shard_map/pallas_call | solution.py:708
  4.2 10.2 %all-to-all-start = ((f32[8,128,128]{2,1,0:T(8,128)}), f32[8,128,128]{2,1,0:T(8,128)S(1)}, u32[]{:S(2)}, u32[]{:S(2)}) async-start(f32[8,128,128]{2,1,0:T(8,128)} %shard_map.158), calls=%async_computation | async-start | bytes 1048576 | tf_op jit(solution)/shard_map/all_to_all | solution.py:778
  14.5 0.0 copy-start.55
  14.5 0.0 copy-start.39
  14.5 0.0 copy-start.27
  14.6 0.0 copy-start.29
  14.6 0.1 shard_map.159.refs_11_.seen
  14.7 0.0 copy-done.57
  14.8 0.0 copy-start.1
  14.8 0.0 copy-start.2
  14.8 0.0 copy-start.13
  14.8 0.5 select_reduce_fusion.2
  15.3 0.3 convolution_bitcast_fusion.refs_12_.refs_1_
  15.5 3.5 %fusion.74 = (f32[512,128]{1,0:T(8,128)S(1)}, f32[512,128]{1,0:T(8,128)S(1)}, f32[512,128]{1,0:T(8,128)S(1)}, f32[512,128]{1,0:T(8,128)S(1)}, f32[512,128]{1,0:T(8,128)S(1)}, /*index=5*/f32[512,128]{1,0:T(8,128)S(1)}) fusion(s32[]{:T(128)S(6)} %mul.251, s32[]{:T(128)S(6)} %mul.248, s32[]{:T(128)S(6)} %mul.247, s32[128]{0:T(128)S(1)} %get-tuple-element.51, ...), kind=kLoop, calls=%fused_computation.161 | loop fusion | flops 5505024 | bytes 1584400 | tf_op jit(solution)/shard_map/sin | solution.py:605
  19.1 0.0 copy-done.51
  19.1 0.0 copy-done.53
  19.1 9.7 %all-to-all-done = f32[8,128,128]{2,1,0:T(8,128)S(1)} async-done(((f32[8,128,128]{2,1,0:T(8,128)}), f32[8,128,128]{2,1,0:T(8,128)S(1)}, u32[]{:S(2)}, u32[]{:S(2)}) %all-to-all-start) | async-done | bytes 524320 | tf_op jit(solution)/shard_map/all_to_all | solution.py:778
  28.8 1.8 %shard_map.160 = (f32[1536,128]{1,0:T(8,128)}, f32[8,128]{1,0:T(8,128)S(1)}) custom-call(f32[1024,128]{1,0:T(8,128)S(1)} %bitcast.26, f32[512,128]{1,0:T(8,128)S(1)} %get-tuple-element.39.refs_1_, f32[512,128]{1,0:T(8,128)S(1)} %get-tuple-element.36.refs_2_, f32[512,128]{1,0:T(8,128)S(1)} %get-tuple-element.38.refs_3_, ...), custom_call_target="tpu_custom_call" | custom-call | flops 200000000 | bytes 2000000 | tf_op jit(solution)/shard_map/pallas_call | solution.py:692
  30.6 16.3 %all-to-all-start.1 = ((f32[512,1,384]{2,1,0:T(1,128)}), f32[512,1,384]{2,1,0:T(1,128)S(1)}, u32[]{:S(2)}, u32[]{:S(2)}) async-start(f32[512,1,384]{2,1,0:T(1,128)} %bitcast.5), calls=%async_computation.1 | async-start | bytes 1572864 | tf_op jit(solution)/shard_map/all_to_all | solution.py:772
  46.9 0.0 copy-start.3
  46.9 0.0 copy-start.9
  46.9 0.0 copy-start.10
  47.0 0.6 iota_shift-right-logical_fusion
  47.6 0.6 fusion.89
  48.2 0.2 select_reduce_fusion.3
  48.4 0.1 multiply_reduce_fusion
  48.5 0.5 slice.6
  49.6 0.2 shard_map.161
  49.8 0.1 fusion.92
  50.0 2.5 %fusion.64 = (f32[512,128]{1,0:T(8,128)S(1)}, f32[512,128]{1,0:T(8,128)S(1)}, f32[512,128]{1,0:T(8,128)S(1)}, f32[512,128]{1,0:T(8,128)S(1)}) fusion(s32[]{:T(128)} %bitcast.7, s32[128]{0:T(128)S(1)} %get-tuple-element.51, s32[128]{0:T(128)S(1)} %get-tuple-element.52, pred[128]{0:T(512)(128)(4,1)S(1)} %get-tuple-element.48, s32[512]{0:T(512)S(1)} %get-tuple-element.42, ...), kind=kLoop, calls=%fused_computation.151 | loop fusion | flops 3735552 | bytes 1058948 | tf_op jit(solution)/shard_map/sin | solution.py:605
  52.5 21.6 %all-to-all-done.1 = f32[512,1,384]{2,1,0:T(1,128)S(1)} async-done(((f32[512,1,384]{2,1,0:T(1,128)}), f32[512,1,384]{2,1,0:T(1,128)S(1)}, u32[]{:S(2)}, u32[]{:S(2)}) %all-to-all-start.1) | async-done | bytes 786464 | tf_op jit(solution)/shard_map/all_to_all | solution.py:772
  74.1 3.3 %shard_map.162 = (f32[2048,128]{1,0:T(8,128)}, f32[8,128]{1,0:T(8,128)S(1)}, f32[16,128]{1,0:T(8,128)S(1)}) custom-call(f32[1536,128]{1,0:T(8,128)S(1)} %bitcast.24, bf16[128,384]{1,0:T(8,128)(2,1)S(1)} %copy-done.10, bf16[128,512]{1,0:T(8,128)(2,1)S(1)} %copy-done.9, f32[512,128]{1,0:T(8,128)S(1)} %get-tuple-element.35.refs_3_, ...), custom_call_target="tpu_custom_call" | custom-call | flops 200000000 | bytes 2000000 | tf_op jit(solution)/shard_map/pallas_call | solution.py:692
  77.4 9.8 %all-to-all-start.2 = ((f32[512,1,512]{2,1,0:T(1,128)}), f32[512,1,512]{2,1,0:T(1,128)S(1)}, u32[]{:S(2)}, u32[]{:S(2)}) async-start(f32[512,1,512]{2,1,0:T(1,128)} %bitcast.8), calls=%async_computation.2 | async-start | bytes 2097152 | tf_op jit(solution)/shard_map/all_to_all | solution.py:772
  87.2 0.0 copy-start.8
  87.2 0.0 copy-start.12
  87.2 0.0 copy-start.14
  87.3 0.3 reduce-precision_convert_fusion.2
  87.7 0.2 fusion.57
  87.9 0.9 select_reduce_fusion
  88.9 0.2 constant_dynamic-update-slice_fusion.3
  89.1 0.3 constant_dynamic-update-slice_fusion.2
  89.4 0.3 fusion.81
  89.6 0.3 constant_dynamic-update-slice_fusion.1
  89.9 0.5 slice.7
  91.1 0.0 copy-start.16
  91.1 0.7 copy-done.16
  91.8 3.5 %shard_map.163 = (f32[512,128]{1,0:T(8,128)S(1)}, f32[512,128]{1,0:T(8,128)S(1)}) custom-call(f32[8,128]{1,0:T(8,128)S(1)} %copy-done.16, f32[16,4096]{1,0:T(8,128)S(1)} %copy-done.8, s32[1,128]{1,0:T(1,128)S(1)} %bitcast.31, s32[1,128]{1,0:T(1,128)S(1)} %bitcast.29), custom_call_target="tpu_custom_call" | custom-call | flops 200000000 | bytes 2000000 | tf_op jit(solution)/shard_map/pallas_call | solution.py:692
  95.3 0.0 copy-start.4
  95.3 0.7 copy-done.4
  96.1 2.3 %fusion.72 = (f32[512,128]{1,0:T(8,128)S(1)}, f32[512,128]{1,0:T(8,128)S(1)}, f32[512,128]{1,0:T(8,128)S(1)}, f32[512,128]{1,0:T(8,128)S(1)}) fusion(s32[128]{0:T(128)S(1)} %copy-done.52, s32[128]{0:T(128)S(1)} %copy-done.54, pred[128]{0:T(512)(128)(4,1)S(1)} %copy-done.56, s32[512]{0:T(512)S(1)} %copy-done.26, s32[512]{0:T(512)S(1)} %copy-done.28, ...), kind=kLoop, calls=%fused_computation.159 | loop fusion | flops 4325376 | bytes 1060116 | tf_op jit(solution)/shard_map/sin | solution.py:605
  98.5 21.9 %all-to-all-done.2 = f32[512,1,512]{2,1,0:T(1,128)S(1)} async-done(((f32[512,1,512]{2,1,0:T(1,128)}), f32[512,1,512]{2,1,0:T(1,128)S(1)}, u32[]{:S(2)}, u32[]{:S(2)}) %all-to-all-start.2) | async-done | bytes 1048608 | tf_op jit(solution)/shard_map/all_to_all | solution.py:772
  120.3 0.9 copy-done.5
  121.3 2.9 %shard_map.164 = (f32[1152,128]{1,0:T(8,128)}, f32[8,128]{1,0:T(8,128)}) custom-call(f32[2048,128]{1,0:T(8,128)S(1)} %bitcast.23, f32[512,128]{1,0:T(8,128)S(1)} %get-tuple-element.30.chirp_re, f32[512,128]{1,0:T(8,128)S(1)} %get-tuple-element.31.chirp_im, f32[512,128]{1,0:T(8,128)S(1)} %get-tuple-element.29.outer_re, ...), custom_call_target="tpu_custom_call" | custom-call | flops 200000000 | bytes 2000000 | tf_op jit(solution)/shard_map/pallas_call | solution.py:692
  124.2 0.0 copy-start.50
  124.2 5.0 %all-to-all-start.3 = ((f32[8,144,128]{2,1,0:T(8,128)}), f32[8,144,128]{2,1,0:T(8,128)S(1)}, u32[]{:S(2)}, u32[]{:S(2)}) async-start(f32[8,144,128]{2,1,0:T(8,128)} %bitcast.14), calls=%async_computation.3 | async-start | bytes 1179648 | tf_op jit(solution)/shard_map/all_to_all | solution.py:778
  129.3 0.3 constant_dynamic-update-slice_fusion
  129.6 0.3 fusion.80.refs_3_
  129.9 0.4 fusion.49
  130.3 0.7 select_reduce_fusion.1.refs_2_
  130.9 0.8 shard_map.165.refs_2_
  131.7 13.4 %all-to-all-done.3 = f32[8,144,128]{2,1,0:T(8,128)S(1)} async-done(((f32[8,144,128]{2,1,0:T(8,128)}), f32[8,144,128]{2,1,0:T(8,128)S(1)}, u32[]{:S(2)}, u32[]{:S(2)}) %all-to-all-start.3) | async-done | bytes 589856 | tf_op jit(solution)/shard_map/all_to_all | solution.py:778
  145.1 2.9 %shard_map.166 = (f32[2,512,128]{2,1,0:T(8,128)}, f32[2,2,16,128]{3,2,1,0:T(8,128)}) custom-call(f32[1152,128]{1,0:T(8,128)S(1)} %bitcast.25, s32[128,128]{1,0:T(8,128)S(1)} %copy-done.6, f32[2,16,128]{2,1,0:T(8,128)S(1)} %shard_map.165.refs_2_, bf16[1536,128]{1,0:T(8,128)(2,1)S(1)} %fusion.80.refs_3_), custom_call_target="tpu_custom_call" | custom-call | flops 200000000 | bytes 2000000 | tf_op jit(solution)/shard_map/pallas_call | solution.py:692
  (107 shorter events, 0.3 us)
Async XLA Ops:
  0.6 14.6 %copy-start = (f32[2,128,128]{2,1,0:T(8,128)S(1)}, f32[2,128,128]{2,1,0:T(8,128)}, u32[]{:S(2)}) copy-start(f32[2,128,128]{2,1,0:T(8,128)} %param.22) | copy-start | bytes 393220
  0.6 13.9 %copy-start.11 = (s32[128]{0:T(128)S(1)}, s32[128]{0:T(128)}, u32[]{:S(2)}) copy-start(s32[128]{0:T(128)} %param.16) | copy-start | bytes 1540
  0.7 13.9 %copy-start.6 = (s32[128,128]{1,0:T(8,128)S(1)}, s32[128,128]{1,0:T(8,128)}, u32[]{:S(2)}) copy-start(s32[128,128]{1,0:T(8,128)} %refs_1_.7) | copy-start | bytes 196612
  0.7 14.1 %copy-start.57 = (f32[63]{0:T(128)S(1)}, f32[63]{0:T(128)}, u32[]{:S(2)}) copy-start(f32[63]{0:T(128)} %param.20) | copy-start | bytes 760
  4.2 24.6 %all-to-all-start = ((f32[8,128,128]{2,1,0:T(8,128)}), f32[8,128,128]{2,1,0:T(8,128)S(1)}, u32[]{:S(2)}, u32[]{:S(2)}) async-start(f32[8,128,128]{2,1,0:T(8,128)} %shard_map.158), calls=%async_computation | async-start | bytes 1048576 | tf_op jit(solution)/shard_map/all_to_all | solution.py:778
  14.4 4.6 %copy-start.51 = (s32[128]{0:T(128)}, s32[128]{0:T(128)S(1)}, u32[]{:S(2)}) copy-start(s32[128]{0:T(128)S(1)} %get-tuple-element.50) | copy-start | bytes 1540
  14.4 35.5 %copy-start.35 = (s32[128]{0:T(128)}, s32[128]{0:T(128)S(1)}, u32[]{:S(2)}) copy-start(s32[128]{0:T(128)S(1)} %get-tuple-element.51) | copy-start | bytes 1540
  14.4 4.6 %copy-start.53 = (s32[128]{0:T(128)}, s32[128]{0:T(128)S(1)}, u32[]{:S(2)}) copy-start(s32[128]{0:T(128)S(1)} %get-tuple-element.53) | copy-start | bytes 1540
  14.5 35.5 %copy-start.37 = (s32[128]{0:T(128)}, s32[128]{0:T(128)S(1)}, u32[]{:S(2)}) copy-start(s32[128]{0:T(128)S(1)} %get-tuple-element.52) | copy-start | bytes 1540
  14.5 4.6 %copy-start.55 = (pred[128]{0:T(512)(128)(4,1)}, pred[128]{0:T(512)(128)(4,1)S(1)}, u32[]{:S(2)}) copy-start(pred[128]{0:T(512)(128)(4,1)S(1)} %get-tuple-element.49) | copy-start | bytes 388
  14.5 35.5 %copy-start.39 = (pred[128]{0:T(512)(128)(4,1)}, pred[128]{0:T(512)(128)(4,1)S(1)}, u32[]{:S(2)}) copy-start(pred[128]{0:T(512)(128)(4,1)S(1)} %get-tuple-element.48) | copy-start | bytes 388
  14.5 35.4 %copy-start.23 = (s32[512]{0:T(512)}, s32[512]{0:T(512)S(1)}, u32[]{:S(2)}) copy-start(s32[512]{0:T(512)S(1)} %get-tuple-element.42) | copy-start | bytes 6148
  14.5 35.4 %copy-start.25 = (s32[512]{0:T(512)}, s32[512]{0:T(512)S(1)}, u32[]{:S(2)}) copy-start(s32[512]{0:T(512)S(1)} %get-tuple-element.43) | copy-start | bytes 6148
  14.5 35.4 %copy-start.27 = (s32[512]{0:T(512)}, s32[512]{0:T(512)S(1)}, u32[]{:S(2)}) copy-start(s32[512]{0:T(512)S(1)} %get-tuple-element.44) | copy-start | bytes 6148
  14.6 35.4 %copy-start.29 = (s32[512]{0:T(512)}, s32[512]{0:T(512)S(1)}, u32[]{:S(2)}) copy-start(s32[512]{0:T(512)S(1)} %get-tuple-element.45) | copy-start | bytes 6148
  14.7 35.3 %copy-start.45 = (pred[512]{0:T(512)(128)(4,1)}, pred[512]{0:T(512)(128)(4,1)S(1)}, u32[]{:S(2)}) copy-start(pred[512]{0:T(512)(128)(4,1)S(1)} %get-tuple-element.46) | copy-start | bytes 1540
  14.7 35.3 %copy-start.47 = (pred[512]{0:T(512)(128)(4,1)}, pred[512]{0:T(512)(128)(4,1)S(1)}, u32[]{:S(2)}) copy-start(pred[512]{0:T(512)(128)(4,1)S(1)} %get-tuple-element.47) | copy-start | bytes 1540
  14.8 14.1 %copy-start.1 = (bf16[512,256]{1,0:T(8,128)(2,1)S(1)}, bf16[512,256]{1,0:T(8,128)(2,1)}, u32[]{:S(2)}) copy-start(bf16[512,256]{1,0:T(8,128)(2,1)} %constant.317.refs_8_.lanes_dft) | copy-start | bytes 786436
  14.8 14.1 %copy-start.2 = (bf16[128,384]{1,0:T(8,128)(2,1)S(1)}, bf16[128,384]{1,0:T(8,128)(2,1)}, u32[]{:S(2)}) copy-start(bf16[128,384]{1,0:T(8,128)(2,1)} %constant.312.refs_7_.split) | copy-start | bytes 294916
  14.8 14.0 %copy-start.13 = (s32[128]{0:T(128)S(1)}, s32[128]{0:T(128)}, u32[]{:S(2)}) copy-start(s32[128]{0:T(128)} %param.17) | copy-start | bytes 1540
  30.6 17.6 %copy-start.49 = (f32[31]{0:T(128)S(1)}, f32[31]{0:T(128)}, u32[]{:S(2)}) copy-start(f32[31]{0:T(128)} %param.21) | copy-start | bytes 376
  30.6 19.0 %copy-start.7 = (f32[16,4096]{1,0:T(8,128)S(1)}, f32[16,4096]{1,0:T(8,128)}, u32[]{:S(2)}) copy-start(f32[16,4096]{1,0:T(8,128)} %refs_1_.6) | copy-start | bytes 786436
  30.6 43.5 %all-to-all-start.1 = ((f32[512,1,384]{2,1,0:T(1,128)}), f32[512,1,384]{2,1,0:T(1,128)S(1)}, u32[]{:S(2)}, u32[]{:S(2)}) async-start(f32[512,1,384]{2,1,0:T(1,128)} %bitcast.5), calls=%async_computation.1 | async-start | bytes 1572864 | tf_op jit(solution)/shard_map/all_to_all | solution.py:772
  46.9 27.2 %copy-start.3 = (bf16[512,256]{1,0:T(8,128)(2,1)S(1)}, bf16[512,256]{1,0:T(8,128)(2,1)}, u32[]{:S(2)}) copy-start(bf16[512,256]{1,0:T(8,128)(2,1)} %constant.328.refs_5_) | copy-start | bytes 786436
  46.9 27.2 %copy-start.9 = (bf16[128,512]{1,0:T(8,128)(2,1)S(1)}, bf16[128,512]{1,0:T(8,128)(2,1)}, u32[]{:S(2)}) copy-start(bf16[128,512]{1,0:T(8,128)(2,1)} %constant.323.refs_2_) | copy-start | bytes 393220
  46.9 27.1 %copy-start.10 = (bf16[128,384]{1,0:T(8,128)(2,1)S(1)}, bf16[128,384]{1,0:T(8,128)(2,1)}, u32[]{:S(2)}) copy-start(bf16[128,384]{1,0:T(8,128)(2,1)} %constant.322.refs_1_) | copy-start | bytes 294916
  47.0 42.7 %copy-start.19 = (s32[256]{0:T(256)}, s32[256]{0:T(256)S(1)}, u32[]{:S(2)}) copy-start(s32[256]{0:T(256)S(1)} %get-tuple-element.62) | copy-start | bytes 3076
  47.0 42.7 %copy-start.21 = (s32[256]{0:T(256)}, s32[256]{0:T(256)S(1)}, u32[]{:S(2)}) copy-start(s32[256]{0:T(256)S(1)} %get-tuple-element.63) | copy-start | bytes 3076
  77.4 12.5 %copy-start.15 = (f32[8,128]{1,0:T(8,128)}, f32[8,128]{1,0:T(8,128)S(1)}, u32[]{:S(2)}) copy-start(f32[8,128]{1,0:T(8,128)S(1)} %get-tuple-element.17.refs_0_) | copy-start | bytes 12292
  77.4 42.9 %all-to-all-start.2 = ((f32[512,1,512]{2,1,0:T(1,128)}), f32[512,1,512]{2,1,0:T(1,128)S(1)}, u32[]{:S(2)}, u32[]{:S(2)}) async-start(f32[512,1,512]{2,1,0:T(1,128)} %bitcast.8), calls=%async_computation.2 | async-start | bytes 2097152 | tf_op jit(solution)/shard_map/all_to_all | solution.py:772
  87.2 3.9 %copy-start.8 = (f32[16,4096]{1,0:T(8,128)S(1)}, f32[16,4096]{1,0:T(8,128)}, u32[]{:S(2)}) copy-start(f32[16,4096]{1,0:T(8,128)} %refs_1_.6) | copy-start | bytes 786436
  87.2 3.9 %copy-start.12 = (s32[128]{0:T(128)S(1)}, s32[128]{0:T(128)}, u32[]{:S(2)}) copy-start(s32[128]{0:T(128)} %param.16) | copy-start | bytes 1540
  87.2 3.9 %copy-start.14 = (s32[128]{0:T(128)S(1)}, s32[128]{0:T(128)}, u32[]{:S(2)}) copy-start(s32[128]{0:T(128)} %param.17) | copy-start | bytes 1540
  87.2 3.2 %copy-start.31 = (pred[256]{0:T(512)(128)(4,1)}, pred[256]{0:T(512)(128)(4,1)S(1)}, u32[]{:S(2)}) copy-start(pred[256]{0:T(512)(128)(4,1)S(1)} %get-tuple-element.60) | copy-start | bytes 772
  87.3 3.2 %copy-start.33 = (pred[256]{0:T(512)(128)(4,1)}, pred[256]{0:T(512)(128)(4,1)S(1)}, u32[]{:S(2)}) copy-start(pred[256]{0:T(512)(128)(4,1)S(1)} %get-tuple-element.61) | copy-start | bytes 772
  87.6 8.5 %copy-start.24 = (s32[512]{0:T(512)S(1)}, s32[512]{0:T(512)}, u32[]{:S(2)}) copy-start(s32[512]{0:T(512)} %copy-done.23) | copy-start | bytes 6148
  87.6 8.5 %copy-start.26 = (s32[512]{0:T(512)S(1)}, s32[512]{0:T(512)}, u32[]{:S(2)}) copy-start(s32[512]{0:T(512)} %copy-done.25) | copy-start | bytes 6148
  87.6 8.5 %copy-start.28 = (s32[512]{0:T(512)S(1)}, s32[512]{0:T(512)}, u32[]{:S(2)}) copy-start(s32[512]{0:T(512)} %copy-done.27) | copy-start | bytes 6148
  87.6 8.5 %copy-start.30 = (s32[512]{0:T(512)S(1)}, s32[512]{0:T(512)}, u32[]{:S(2)}) copy-start(s32[512]{0:T(512)} %copy-done.29) | copy-start | bytes 6148
  87.6 8.5 %copy-start.36 = (s32[128]{0:T(128)S(1)}, s32[128]{0:T(128)}, u32[]{:S(2)}) copy-start(s32[128]{0:T(128)} %copy-done.35) | copy-start | bytes 1540
  87.6 8.5 %copy-start.38 = (s32[128]{0:T(128)S(1)}, s32[128]{0:T(128)}, u32[]{:S(2)}) copy-start(s32[128]{0:T(128)} %copy-done.37) | copy-start | bytes 1540
  87.6 8.5 %copy-start.40 = (pred[128]{0:T(512)(128)(4,1)S(1)}, pred[128]{0:T(512)(128)(4,1)}, u32[]{:S(2)}) copy-start(pred[128]{0:T(512)(128)(4,1)} %copy-done.39) | copy-start | bytes 388
  87.6 8.5 %copy-start.46 = (pred[512]{0:T(512)(128)(4,1)S(1)}, pred[512]{0:T(512)(128)(4,1)}, u32[]{:S(2)}) copy-start(pred[512]{0:T(512)(128)(4,1)} %copy-done.45) | copy-start | bytes 1540
  87.6 8.5 %copy-start.48 = (pred[512]{0:T(512)(128)(4,1)S(1)}, pred[512]{0:T(512)(128)(4,1)}, u32[]{:S(2)}) copy-start(pred[512]{0:T(512)(128)(4,1)} %copy-done.47) | copy-start | bytes 1540
  87.7 8.5 %copy-start.52 = (s32[128]{0:T(128)S(1)}, s32[128]{0:T(128)}, u32[]{:S(2)}) copy-start(s32[128]{0:T(128)} %copy-done.51) | copy-start | bytes 1540
  87.7 8.5 %copy-start.54 = (s32[128]{0:T(128)S(1)}, s32[128]{0:T(128)}, u32[]{:S(2)}) copy-start(s32[128]{0:T(128)} %copy-done.53) | copy-start | bytes 1540
  87.7 8.5 %copy-start.56 = (pred[128]{0:T(512)(128)(4,1)S(1)}, pred[128]{0:T(512)(128)(4,1)}, u32[]{:S(2)}) copy-start(pred[128]{0:T(512)(128)(4,1)} %copy-done.55) | copy-start | bytes 388
  88.9 1.6 %copy-start.17 = (f32[256,128]{1,0:T(8,128)}, f32[256,128]{1,0:T(8,128)S(1)}, u32[]{:S(2)}) copy-start(f32[256,128]{1,0:T(8,128)S(1)} %select_reduce_fusion) | copy-start | bytes 393220
  91.1 0.7 copy-start.16
  95.3 0.7 copy-start.4
  120.3 1.0 copy-start.5
  124.2 5.1 %copy-start.18 = (f32[256,128]{1,0:T(8,128)S(1)}, f32[256,128]{1,0:T(8,128)}, u32[]{:S(2)}) copy-start(f32[256,128]{1,0:T(8,128)} %copy-done.17) | copy-start | bytes 393220
  124.2 5.1 %copy-start.20 = (s32[256]{0:T(256)S(1)}, s32[256]{0:T(256)}, u32[]{:S(2)}) copy-start(s32[256]{0:T(256)} %copy-done.19) | copy-start | bytes 3076
  124.2 5.1 %copy-start.22 = (s32[256]{0:T(256)S(1)}, s32[256]{0:T(256)}, u32[]{:S(2)}) copy-start(s32[256]{0:T(256)} %copy-done.21) | copy-start | bytes 3076
  124.2 5.1 %copy-start.32 = (pred[256]{0:T(512)(128)(4,1)S(1)}, pred[256]{0:T(512)(128)(4,1)}, u32[]{:S(2)}) copy-start(pred[256]{0:T(512)(128)(4,1)} %copy-done.31) | copy-start | bytes 772
  124.2 5.1 %copy-start.34 = (pred[256]{0:T(512)(128)(4,1)S(1)}, pred[256]{0:T(512)(128)(4,1)}, u32[]{:S(2)}) copy-start(pred[256]{0:T(512)(128)(4,1)} %copy-done.33) | copy-start | bytes 772
  124.2 5.7 %copy-start.41 = (s32[384]{0:T(512)S(1)}, s32[384]{0:T(512)}, u32[]{:S(2)}) copy-start(s32[384]{0:T(512)} %get-tuple-element.54) | copy-start | bytes 4612
  124.2 5.7 %copy-start.42 = (s32[384]{0:T(512)S(1)}, s32[384]{0:T(512)}, u32[]{:S(2)}) copy-start(s32[384]{0:T(512)} %get-tuple-element.55) | copy-start | bytes 4612
  124.2 5.7 %copy-start.43 = (s32[384]{0:T(512)S(1)}, s32[384]{0:T(512)}, u32[]{:S(2)}) copy-start(s32[384]{0:T(512)} %get-tuple-element.56) | copy-start | bytes 4612
  124.2 5.7 %copy-start.44 = (s32[384]{0:T(512)S(1)}, s32[384]{0:T(512)}, u32[]{:S(2)}) copy-start(s32[384]{0:T(512)} %get-tuple-element.57) | copy-start | bytes 4612
  124.2 6.0 %copy-start.50 = (f32[31]{0:T(128)S(1)}, f32[31]{0:T(128)}, u32[]{:S(2)}) copy-start(f32[31]{0:T(128)} %param.21) | copy-start | bytes 376
  124.2 20.8 %all-to-all-start.3 = ((f32[8,144,128]{2,1,0:T(8,128)}), f32[8,144,128]{2,1,0:T(8,128)S(1)}, u32[]{:S(2)}, u32[]{:S(2)}) async-start(f32[8,144,128]{2,1,0:T(8,128)} %bitcast.14), calls=%async_computation.3 | async-start | bytes 1179648 | tf_op jit(solution)/shard_map/all_to_all | solution.py:778
